TPU v7x, 32 devices: a whole 2x2x4 slice. The times are simulated.
32 devices in a mesh: dp: 8 (over z, y), mp: 4 (over x, core).
Axes of the slice: x: 2, y: 2, z: 4, core: 2. Of those that a mesh axis runs over, the one named last changes fastest.
Arguments:
- patches: bfloat16 [4096, 1152], P(('dp', 'mp')), may hold values from -600 to 600
- norm_gain: float32 [1152], replicated, may hold values from 0.1 to 1.9
- query_key_value: bfloat16 [1152, 3456], P(None, 'mp'), may hold values from -4 to 4
- output_weight: bfloat16 [1152, 1152], P(None, 'mp'), may hold values from -0.1875 to 0.1875
- embed_weight: bfloat16 [1152, 128], replicated, may hold values from -0.1875 to 0.1875
- query_tokens: bfloat16 [32, 32, 128], P('dp'), may hold values from -6 to 6
- patch_counts: int32 [8], replicated, may hold values from 1 to 512, as said below
- positive_page: int32 [32], P('dp'), may hold values from 0 to 7
- hidden_grad: bfloat16 [4096, 1152], P(('dp', 'mp')), may hold values from -6 to 6
Outputs:
- hidden_out: bfloat16 [4096, 1152], P(('dp', 'mp'))
- patches_grad: bfloat16 [4096, 1152], P(('dp', 'mp'))
- output_weight_grad: float32 [1152, 1152], P('dp', 'mp')
- page_scores: float32 [32, 8], P('dp')
- query_loss: float32 [32], P('dp')
Inputs may be any that keep to these rules, and one draw needn't show every extreme that they name: `patch_counts`: pages g*1 to g + 1 - 1 belong to group g; in every draw the pages of some group fill all 512 of its rows.
All inputs are finite; a program needn't handle non-finite values.
Results may differ from a plain program's by a relative error of at most 0.0098.
Values may be sent and summed in bfloat16 or wider, within the bound.
No kernel may reach another device: no remote copies, remote signals or barrier semaphores. Data moves between devices by JAX's collectives and lax.ppermute only.
A program may use at most 64 MiB of HBM per device.

v0:
```python
from functools import partial
import math

import jax
import jax.numpy as jnp
from jax import lax
from jax.sharding import PartitionSpec as P

HEAD_DIM = 72
EMB = 128
PPD = 1
QTOK = 32


def layer_norm(values, gain):
    center = values - jnp.mean(values, axis=-1, keepdims=True)
    spread = jnp.mean(center * center, axis=-1, keepdims=True)
    return center * lax.rsqrt(spread + 1e-06) * gain


def unit_rows(values):
    return values * lax.rsqrt(jnp.sum(values * values, axis=-1, keepdims=True) + 1e-06)


def page_index(counts_group, rows):
    ends = jnp.cumsum(counts_group)
    places = jnp.arange(rows, dtype=jnp.int32)
    which = jnp.sum((places[:, None] >= ends[None, :]).astype(jnp.int32), axis=1)
    live = places < ends[-1]
    return (jnp.where(live, which, -1), live.astype(jnp.float32))


def head_split(projected, heads):
    rows = projected.shape[0]
    parts = jnp.transpose(projected.reshape(rows, heads, 3, HEAD_DIM), (2, 1, 0, 3))
    return (parts[0], parts[1], parts[2])


def softmax_rows(query_rows, key_rows, allowed):
    scores = jnp.einsum(
        "hqe,hke->hqk", query_rows, key_rows, preferred_element_type=jnp.float32
    ) * HEAD_DIM ** (-0.5)
    scores = jnp.where(allowed[None], scores, -1e30)
    largest = jnp.max(scores, axis=-1, keepdims=True)
    raised = jnp.exp(scores - largest)
    return raised / jnp.sum(raised, axis=-1, keepdims=True)


def attend_rows(query_rows, key_rows, value_rows, allowed, live_rows):
    probs = softmax_rows(query_rows, key_rows, allowed)
    weights = probs.astype(jnp.bfloat16)
    result = jnp.einsum("hqk,hke->hqe", weights, value_rows, preferred_element_type=jnp.float32)
    return (result * live_rows[None, :, None]).astype(jnp.bfloat16)


def attend_back_rows(query_rows, key_rows, value_rows, allowed, live_rows, grad_rows):
    probs = softmax_rows(query_rows, key_rows, allowed)
    weights = probs.astype(jnp.bfloat16)
    grad_live = jnp.where(live_rows[None, :, None] > 0, grad_rows, jnp.zeros_like(grad_rows))
    grad_prob = jnp.einsum(
        "hqe,hke->hqk", grad_live, value_rows, preferred_element_type=jnp.float32
    )
    delta = jnp.sum(grad_prob * probs, axis=-1, keepdims=True)
    grad_score = (probs * (grad_prob - delta)).astype(jnp.bfloat16)
    grad_query = (
        jnp.einsum("hqk,hke->hqe", grad_score, key_rows, preferred_element_type=jnp.float32)
        * HEAD_DIM ** (-0.5)
    ).astype(jnp.bfloat16)
    grad_key = jnp.einsum(
        "hqk,hqe->hke", grad_score, query_rows, preferred_element_type=jnp.float32
    ) * HEAD_DIM ** (-0.5)
    grad_value = jnp.einsum("hqk,hqe->hke", weights, grad_live, preferred_element_type=jnp.float32)
    return (grad_query, grad_key, grad_value)


def tile_forward(query_all, key_all, value_all, page_of, live, tile_rows, first, last):

    def step(index, result):
        start = index * tile_rows
        query_part = lax.dynamic_slice_in_dim(query_all, start, tile_rows, 1)
        pages_part = lax.dynamic_slice_in_dim(page_of, start, tile_rows, 0)
        allowed_part = pages_part[:, None] == page_of[None, :]
        live_part = lax.dynamic_slice_in_dim(live, start, tile_rows, 0)
        found = attend_rows(query_part, key_all, value_all, allowed_part, live_part)
        return lax.dynamic_update_slice_in_dim(result, found, start, 1)

    return lax.fori_loop(first, last, step, jnp.zeros_like(value_all))


def tile_backward(query_all, key_all, value_all, page_of, live, grad_heads, tile_rows, first, last):

    def step(index, carry):
        grad_query, grad_key, grad_value = carry
        start = index * tile_rows
        query_part = lax.dynamic_slice_in_dim(query_all, start, tile_rows, 1)
        pages_part = lax.dynamic_slice_in_dim(page_of, start, tile_rows, 0)
        allowed_part = pages_part[:, None] == page_of[None, :]
        live_part = lax.dynamic_slice_in_dim(live, start, tile_rows, 0)
        grad_part = lax.dynamic_slice_in_dim(grad_heads, start, tile_rows, 1)
        query_step, key_step, value_step = attend_back_rows(
            query_part, key_all, value_all, allowed_part, live_part, grad_part
        )
        return (
            lax.dynamic_update_slice_in_dim(grad_query, query_step, start, 1),
            grad_key + key_step,
            grad_value + value_step,
        )

    start_carry = (
        jnp.zeros_like(query_all),
        jnp.zeros(key_all.shape, jnp.float32),
        jnp.zeros(value_all.shape, jnp.float32),
    )
    return lax.fori_loop(first, last, step, start_carry)


def patch_best(flat, emb_rows, row_pages):
    size = flat.shape[0]
    block = math.gcd(size, 2048)

    def one_block(index):
        part = lax.dynamic_slice_in_dim(flat, index * block, block, 0)
        similar = jnp.dot(part, emb_rows.T, preferred_element_type=jnp.float32)
        return jnp.stack(
            [jnp.max(jnp.where(row_pages[None, :] == 0, similar, -2.0), axis=1)], axis=1
        )

    return lax.map(one_block, jnp.arange(size // block, dtype=jnp.int32)).reshape(size, PPD)


def body(
    patches,
    norm_gain,
    query_key_value,
    output_weight,
    embed_weight,
    query_tokens,
    patch_counts,
    positive_page,
    hidden_grad,
):
    model_size = lax.axis_size("mp")
    model_index = lax.axis_index("mp")
    data_index = lax.axis_index("dp")
    rows_dev = patches.shape[0]
    rows = rows_dev * model_size
    width_dev = output_weight.shape[1]
    heads_dev = width_dev // HEAD_DIM
    tile_rows = rows // 4
    my_counts = lax.dynamic_slice_in_dim(patch_counts, data_index * PPD, PPD, 0)
    page_of, live = page_index(my_counts, rows)
    my_pages = lax.dynamic_slice_in_dim(page_of, model_index * rows_dev, rows_dev, 0)
    my_tiles = (jnp.sum(my_counts) + tile_rows - 1) // tile_rows
    patch_float = patches.astype(jnp.float32)
    normed_float, norm_back = jax.vjp(partial(layer_norm, gain=norm_gain), patch_float)
    normed = normed_float.astype(jnp.bfloat16)
    projected = jnp.dot(
        lax.all_gather(normed, "mp", axis=0, tiled=True),
        query_key_value,
        preferred_element_type=jnp.float32,
    ).astype(jnp.bfloat16)
    query_all, key_all, value_all = head_split(projected, heads_dev)
    attended_heads = tile_forward(
        query_all, key_all, value_all, page_of, live, tile_rows, 0, my_tiles
    )
    attended = jnp.transpose(attended_heads, (1, 0, 2)).reshape(rows, width_dev)
    block = attended
    mixed = lax.psum_scatter(
        lax.dot_general(
            block, output_weight, (((1,), (1,)), ((), ())), preferred_element_type=jnp.float32
        ).astype(jnp.bfloat16),
        "mp",
        scatter_dimension=0,
        tiled=True,
    ).astype(jnp.float32)
    hidden = (patch_float + mixed).astype(jnp.bfloat16)
    embedded = jnp.dot(hidden, embed_weight, preferred_element_type=jnp.float32)
    page_emb = unit_rows(embedded).astype(jnp.bfloat16)
    query_emb = unit_rows(query_tokens.astype(jnp.float32)).astype(jnp.bfloat16)
    piece = lax.all_gather(query_emb, "dp", axis=0, tiled=True)
    count = piece.shape[0]
    found = patch_best(piece.reshape(count * QTOK, EMB), page_emb, my_pages)
    best = found.reshape(count, QTOK, PPD)
    best = lax.pmax(best.astype(jnp.bfloat16), "mp").astype(best.dtype)
    part_scores = jnp.sum(best, axis=1)
    local_queries = query_tokens.shape[0]
    every_score = lax.all_gather(part_scores, "dp", axis=1, tiled=True)
    my_scores = lax.dynamic_slice_in_dim(every_score, data_index * local_queries, local_queries, 0)
    columns = jnp.arange(my_scores.shape[1], dtype=jnp.int32)
    chosen = columns[None, :] == positive_page[:, None]
    positive_score = jnp.sum(jnp.where(chosen, my_scores, 0.0), axis=1)
    negative_score = jnp.max(jnp.where(chosen, -1e30, my_scores), axis=1)
    loss = jax.nn.softplus(negative_score - positive_score)
    grad_full = lax.all_gather(hidden_grad, "mp", axis=0, tiled=True)
    grad_attended = jnp.dot(grad_full, output_weight, preferred_element_type=jnp.float32).astype(
        jnp.bfloat16
    )
    grad_heads = jnp.transpose(grad_attended.reshape(rows, heads_dev, HEAD_DIM), (1, 0, 2))
    grad_query, grad_key, grad_value = tile_backward(
        query_all, key_all, value_all, page_of, live, grad_heads, tile_rows, 0, my_tiles
    )
    stacked = jnp.stack(
        [grad_query, grad_key.astype(jnp.bfloat16), grad_value.astype(jnp.bfloat16)], axis=0
    )
    grad_projected = jnp.transpose(stacked, (2, 1, 0, 3)).reshape(rows, 3 * width_dev)
    block = grad_projected
    normed_grad = lax.psum_scatter(
        lax.dot_general(
            block, query_key_value, (((1,), (1,)), ((), ())), preferred_element_type=jnp.float32
        ).astype(jnp.bfloat16),
        "mp",
        scatter_dimension=0,
        tiled=True,
    ).astype(jnp.float32)
    patch_grad = (hidden_grad.astype(jnp.float32) + norm_back(normed_grad)[0]).astype(jnp.bfloat16)
    block = grad_full
    weight_grad = lax.psum_scatter(
        lax.dot_general(
            block, attended, (((0,), (0,)), ((), ())), preferred_element_type=jnp.float32
        ),
        "dp",
        scatter_dimension=0,
        tiled=True,
    )
    return (hidden, patch_grad, weight_grad, my_scores, loss)


def solution(mesh):
    return jax.shard_map(
        body,
        mesh=mesh,
        in_specs=(
            P(("dp", "mp"), None),
            P(),
            P(None, "mp"),
            P(None, "mp"),
            P(),
            P("dp", None, None),
            P(),
            P("dp"),
            P(("dp", "mp"), None),
        ),
        out_specs=(
            P(("dp", "mp"), None),
            P(("dp", "mp"), None),
            P("dp", "mp"),
            P("dp", None),
            P("dp"),
        ),
        check_vma=False,
    )
```

profile of v0, /device:TPU:0, one launch (start us, length us, event | category | flops | bytes accessed | tf_op | source)
XLA Modules:
  0.0 224.1 jit_solution(155788466371016371)
XLA Ops:
  9.7 1.9 fusion.54
  15.0 17.0 %all-gather.4.cloned.1.call-done = bf16[512,1152]{1,0:T(8,128)(2,1)} async-done(((bf16[128,1152]{1,0:T(8,128)(2,1)}), bf16[512,1152]{1,0:T(8,128)(2,1)}) %all-gather.4.cloned.1.call-update) | async-done | bytes 1179664 | tf_op jit(solution)/shard_map/all_gather | solution.py:158
  32.0 2.6 %convolution_convert_fusion.2 = bf16[512,864]{0,1:T(8,128)(2,1)S(1)} fusion(bf16[512,1152]{1,0:T(8,128)(2,1)} %all-gather.4.cloned.1.call-done, bf16[1152,864]{0,1:T(8,128)(2,1)S(1)} %copy-done), kind=kOutput, calls=%fused_computation.54 | convolution fusion | flops 1019658240 | bytes 4055040 | tf_op jit(solution)/shard_map/dot_general | solution.py:157
  35.6 15.4 %all-gather.6.cloned.1.call-done = bf16[512,1152]{1,0:T(8,128)(2,1)} async-done(((bf16[128,1152]{1,0:T(8,128)(2,1)}), bf16[512,1152]{1,0:T(8,128)(2,1)}) %all-gather.6.cloned.1.call-update) | async-done | bytes 1179664 | tf_op jit(solution)/shard_map/all_gather | solution.py:194
  51.0 2.6 %convolution_convert_fusion.3 = bf16[512,288]{0,1:T(8,128)(2,1)} fusion(bf16[512,1152]{1,0:T(8,128)(2,1)} %all-gather.6.cloned.1.call-done, bf16[1152,288]{0,1:T(8,128)(2,1)S(1)} %copy-done.13), kind=kOutput, calls=%fused_computation.56 | convolution fusion | flops 339886080 | bytes 2138112 | tf_op jit(solution)/shard_map/dot_general | solution.py:195
  54.4 27.3 %while.29 = (s32[]{:T(128)}, bf16[4,512,72]{1,2,0:T(8,128)(2,1)}, f32[4,512,72]{1,2,0:T(8,128)S(1)}, f32[4,512,72]{1,2,0:T(8,128)S(1)}, s32[]{:T(128)}, /*index=...) while((s32[]{:T(128)}, bf16[4,512,72]{1,2,0:T(8,128)(2,1)}, ...), condition=%wide.region_11.12_spmd, body=%wide.region_7.11_spmd.sunk | while | flops 231343232 | bytes 15206767 | solution.py:114
  55.2 2.4 %fusion.133 = (f32[4,128]{1,0:T(4,128)S(1)}, f32[4,128,512]{2,1,0:T(8,128)}) fusion(bf16[4,512,72]{1,2,0:T(8,128)(2,1)S(1)} %get-tuple-element.358, pred[128,512]{1,0:T(8,128)(4,1)S(1)} %broadcast_compare_fusion.5, bf16[4,512,72]{1,2,0:T(8,128)(2,1)} %get-tuple-element.357, s32[]{:T(128)S(6)} %select_n.113), kind=kOutput, calls=%fused_computation.107.clone.1 | convolution fusion | flops 38797824 | bytes 1484804 | tf_op jit(solution)/shard_map/while/body/sub | solution.py:45
  59.3 1.9 multiply_reduce_fusion.3
  64.3 2.4 %fusion.133 = (f32[4,128]{1,0:T(4,128)S(1)}, f32[4,128,512]{2,1,0:T(8,128)}) fusion(bf16[4,512,72]{1,2,0:T(8,128)(2,1)S(1)} %get-tuple-element.358, pred[128,512]{1,0:T(8,128)(4,1)S(1)} %broadcast_compare_fusion.5, bf16[4,512,72]{1,2,0:T(8,128)(2,1)} %get-tuple-element.357, s32[]{:T(128)S(6)} %select_n.113), kind=kOutput, calls=%fused_computation.107.clone.1 | convolution fusion | flops 38797824 | bytes 1484804 | tf_op jit(solution)/shard_map/while/body/sub | solution.py:45
  68.4 1.9 multiply_reduce_fusion.3
  73.4 2.4 %fusion.133 = (f32[4,128]{1,0:T(4,128)S(1)}, f32[4,128,512]{2,1,0:T(8,128)}) fusion(bf16[4,512,72]{1,2,0:T(8,128)(2,1)S(1)} %get-tuple-element.358, pred[128,512]{1,0:T(8,128)(4,1)S(1)} %broadcast_compare_fusion.5, bf16[4,512,72]{1,2,0:T(8,128)(2,1)} %get-tuple-element.357, s32[]{:T(128)S(6)} %select_n.113), kind=kOutput, calls=%fused_computation.107.clone.1 | convolution fusion | flops 38797824 | bytes 1484804 | tf_op jit(solution)/shard_map/while/body/sub | solution.py:45
  77.5 1.9 multiply_reduce_fusion.3
  82.8 2.6 %convolution_convert_fusion = bf16[512,1152]{1,0:T(8,128)(2,1)} fusion(bf16[512,864]{0,1:T(8,128)(2,1)S(1)} %bitcast.81, bf16[1152,864]{0,1:T(8,128)(2,1)S(1)} %copy-done), kind=kOutput, calls=%fused_computation.51 | convolution fusion | flops 1019805696 | bytes 4055040 | tf_op jit(solution)/shard_map/dot_general | solution.py:208
  86.2 17.1 %while.28 = (s32[]{:T(128)}, bf16[4,512,72]{1,2,0:T(8,128)(2,1)}, s32[]{:T(128)}, s32[512]{0:T(512)S(1)}, bf16[4,512,72]{1,2,0:T(8,128)(2,1)}, /*index=5*/bf16[4...) while((s32[]{:T(128)}, bf16[4,512,72]{1,2,0:T(8,128)(2,1)}, ...), condition=%wide.region_5.6_spmd, body=%wide.region_2.5_spmd.sunk | while | flops 115746304 | bytes 4457655 | solution.py:87
  89.1 2.7 %fusion.122 = bf16[4,512,72]{1,2,0:T(8,128)(2,1)} fusion(bf16[4,512,72]{1,2,0:T(8,128)(2,1)} %get-tuple-element.379, s32[]{:T(128)S(6)} %select_n.108, bf16[4,512,72]{1,2,0:T(8,128)(2,1)} %get-tuple-element.396, f32[4,128]{1,0:T(4,128)S(1)} %fusion.120, f32[4,128,512]{2,1,0:T(8,128)S(1)} %fusion.121, f32[128]{0:T(128)S(1)} %dynamic_slice.81), kind=kOutput, calls=%fused_computation.7.clone.1 | convolution fusion | flops 38609920 | bytes 2468356 | tf_op jit(solution)/shard_map/while/body/hqk,hke->hqe/dot_general | solution.py:52
  94.8 2.7 %fusion.122 = bf16[4,512,72]{1,2,0:T(8,128)(2,1)} fusion(bf16[4,512,72]{1,2,0:T(8,128)(2,1)} %get-tuple-element.379, s32[]{:T(128)S(6)} %select_n.108, bf16[4,512,72]{1,2,0:T(8,128)(2,1)} %get-tuple-element.396, f32[4,128]{1,0:T(4,128)S(1)} %fusion.120, f32[4,128,512]{2,1,0:T(8,128)S(1)} %fusion.121, f32[128]{0:T(128)S(1)} %dynamic_slice.81), kind=kOutput, calls=%fused_computation.7.clone.1 | convolution fusion | flops 38609920 | bytes 2468356 | tf_op jit(solution)/shard_map/while/body/hqk,hke->hqe/dot_general | solution.py:52
  100.5 2.7 %fusion.122 = bf16[4,512,72]{1,2,0:T(8,128)(2,1)} fusion(bf16[4,512,72]{1,2,0:T(8,128)(2,1)} %get-tuple-element.379, s32[]{:T(128)S(6)} %select_n.108, bf16[4,512,72]{1,2,0:T(8,128)(2,1)} %get-tuple-element.396, f32[4,128]{1,0:T(4,128)S(1)} %fusion.120, f32[4,128,512]{2,1,0:T(8,128)S(1)} %fusion.121, f32[128]{0:T(128)S(1)} %dynamic_slice.81), kind=kOutput, calls=%fused_computation.7.clone.1 | convolution fusion | flops 38609920 | bytes 2468356 | tf_op jit(solution)/shard_map/while/body/hqk,hke->hqe/dot_general | solution.py:52
  103.2 3.1 %convolution_convert_fusion.1 = bf16[512,1152]{1,0:T(8,128)(2,1)} fusion(bf16[512,288]{0,1:T(8,128)(2,1)} %bitcast.79, bf16[1152,288]{0,1:T(8,128)(2,1)} %param.16), kind=kOutput, calls=%fused_computation.52 | convolution fusion | flops 340328448 | bytes 2138112 | tf_op jit(solution)/shard_map/dot_general | solution.py:169
  106.6 1.9 convolution_bitcast_fusion
  110.4 45.0 %all_gather.14 = bf16[32,32,128]{2,1,0:T(8,128)(2,1)} all-gather(bf16[4,32,128]{2,1,0:T(8,128)(2,1)S(1)} %fusion.59), channel_id=1, replica_groups=mesh['dp'=8,'mp'=4] {'dp'}, dimensions={0}, use_global_device_ids=true | all-gather | bytes 294912 | tf_op jit(solution)/shard_map/all_gather | solution.py:180
  158.1 2.1 add_convert_fusion
  160.8 6.1 %pmax.7 = bf16[32,32,1]{1,0,2:T(8,128)(2,1)S(1)} all-reduce(bf16[32,32,1]{1,0,2:T(8,128)(2,1)S(1)} %convert_element_type.108), channel_id=1, replica_groups=mesh['dp'=8,'mp'=4] {'mp'}, use_global_device_ids=true, to_apply=%region_19.20 | all-reduce | flops 1024 | bytes 4096 | tf_op jit(solution)/shard_map/pmax | solution.py:184
  167.1 16.3 %all-gather = f32[8,1,32]{2,1,0:T(1,128)S(1)} all-gather(f32[1,1,32]{2,1,0:T(1,128)S(1)} %bitcast.85), channel_id=1, replica_groups=mesh['dp'=8,'mp'=4] {'dp'}, dimensions={0}, use_global_device_ids=true | all-gather | bytes 1152 | tf_op jit(solution)/shard_map/all_gather | solution.py:187
  184.3 33.3 %reduce-scatter.10.cloned.1.call-done = f32[144,288]{1,0:T(8,128)} async-done(((f32[1152,288]{1,0:T(8,128)}), f32[144,288]{1,0:T(8,128)}) %reduce-scatter.10.cloned.1.call-update) | async-done | bytes 165904
  (115 shorter events, 38.4 us)
Async XLA Ops:
  7.2 24.8 %copy-start = (bf16[1152,864]{0,1:T(8,128)(2,1)S(1)}, bf16[1152,864]{0,1:T(8,128)(2,1)}, u32[]{:S(2)}) copy-start(bf16[1152,864]{0,1:T(8,128)(2,1)} %param.15) | copy-start | bytes 5971972
  7.2 5.2 %copy-start.14 = (s32[8]{0:T(128)S(1)}, s32[8]{0:T(128)}, u32[]{:S(2)}) copy-start(s32[8]{0:T(128)} %param.19) | copy-start | bytes 100
  7.2 24.8 %all-gather.4.cloned.1.call-start = ((), (), s32[]{:S(2)}) async-start(), calls=%async_computation.3 | async-start | bytes 1474560 | tf_op jit(solution)/shard_map/all_gather | solution.py:158
  11.6 39.4 %all-gather.6.cloned.1.call-start = ((), (), s32[]{:S(2)}) async-start(), calls=%async_computation.5 | async-start | bytes 1474560 | tf_op jit(solution)/shard_map/all_gather | solution.py:194
  12.3 143.0 %reduce-scatter.8.cloned.1.call-start = ((), (), s32[]{:S(2)}) async-start(), calls=%async_computation.6 | async-start | bytes 1474560 | tf_op jit(solution)/shard_map/reduce_scatter | solution.py:207
  34.6 16.3 %copy-start.13 = (bf16[1152,288]{0,1:T(8,128)(2,1)S(1)}, bf16[1152,288]{0,1:T(8,128)(2,1)}, u32[]{:S(2)}) copy-start(bf16[1152,288]{0,1:T(8,128)(2,1)} %param.16) | copy-start | bytes 1990660
  59.3 1.9 copy-start.1
  68.4 1.9 copy-start.1
  77.5 1.9 copy-start.1
  81.7 1.0 copy-start.4
  85.4 72.7 %reduce-scatter.6.cloned.1.call-start = ((), (), s32[]{:S(2)}) async-start(), calls=%async_computation.4 | async-start | bytes 1474560 | tf_op jit(solution)/shard_map/reduce_scatter | solution.py:168
  103.2 3.1 %copy-start.10 = (bf16[4,32,128]{2,1,0:T(8,128)(2,1)S(1)}, bf16[4,32,128]{2,1,0:T(8,128)(2,1)}, u32[]{:S(2)}) copy-start(bf16[4,32,128]{2,1,0:T(8,128)(2,1)} %param.18) | copy-start | bytes 98308
  106.3 111.2 %reduce-scatter.10.cloned.1.call-start = ((), (), s32[]{:S(2)}) async-start(), calls=%async_computation.7 | async-start | bytes 1990656
  110.3 45.1 %copy-start.2 = (bf16[128,1152]{1,0:T(8,128)(2,1)S(1)}, bf16[128,1152]{1,0:T(8,128)(2,1)}, u32[]{:S(2)}) copy-start(bf16[128,1152]{1,0:T(8,128)(2,1)} %param.13) | copy-start | bytes 884740
  110.3 45.1 %copy-start.9 = (f32[1152]{0:T(1024)S(1)}, f32[1152]{0:T(1024)}, u32[]{:S(2)}) copy-start(f32[1152]{0:T(1024)} %param.14) | copy-start | bytes 13828
  110.3 47.8 %copy-start.5 = (bf16[128,1152]{1,0:T(8,128)(2,1)S(1)}, bf16[128,1152]{1,0:T(8,128)(2,1)}, u32[]{:S(2)}) copy-start(bf16[128,1152]{1,0:T(8,128)(2,1)} %param.21) | copy-start | bytes 884740
  155.4 2.7 %copy-start.3 = (bf16[128,1152]{1,0:T(8,128)(2,1)S(1)}, bf16[128,1152]{1,0:T(8,128)(2,1)}, u32[]{:S(2)}) copy-start(bf16[128,1152]{1,0:T(8,128)(2,1)} %reduce-scatter.8.cloned.1.call-done) | copy-start | bytes 884740
  156.6 3.5 %copy-start.7 = (bf16[1152,128]{1,0:T(8,128)(2,1)S(1)}, bf16[1152,128]{1,0:T(8,128)(2,1)}, u32[]{:S(2)}) copy-start(bf16[1152,128]{1,0:T(8,128)(2,1)} %param.17) | copy-start | bytes 884740
  158.0 25.6 %copy-start.12 = (s32[4]{0:T(128)S(1)}, s32[4]{0:T(128)}, u32[]{:S(2)}) copy-start(s32[4]{0:T(128)} %param.20) | copy-start | bytes 52
  158.1 2.4 %copy-start.8 = (bf16[32,32,128]{2,1,0:T(8,128)(2,1)S(1)}, bf16[32,32,128]{2,1,0:T(8,128)(2,1)}, u32[]{:S(2)}) copy-start(bf16[32,32,128]{2,1,0:T(8,128)(2,1)} %all_gather.14) | copy-start | bytes 786436
  160.1 57.4 %copy-start.6 = (bf16[128,1152]{1,0:T(8,128)(2,1)}, bf16[128,1152]{1,0:T(8,128)(2,1)S(1)}, u32[]{:S(2)}) copy-start(bf16[128,1152]{1,0:T(8,128)(2,1)S(1)} %get-tuple-element.190) | copy-start | bytes 884740
  183.6 34.0 %copy-start.11 = (f32[8,1,4]{0,2,1:T(4,128)}, f32[8,1,4]{0,2,1:T(4,128)S(1)}, u32[]{:S(2)}) copy-start(f32[8,1,4]{0,2,1:T(4,128)S(1)} %copy.21) | copy-start | bytes 388
Sparse Core Ops, SparseCore 0:
  11.7 20.2 all-gather.3
  33.5 17.4 all-gather.5
  85.5 32.8 reduce-scatter.7
  120.8 25.6 reduce-scatter.5
  150.3 67.1 reduce-scatter.9
where the time goes:
time: 226 us; the launch traced here: 224 us
  blocking collectives  67.4 us (30%)
  waiting for transfers between devices  66.4 us (29%)
  matrix products  53.7 us (24%)
  between operations  14.7 us (7%)
  other arithmetic  14.6 us (6%)
  local copies, waits for them, and re-layouts  6.75 us (3%)
    all_gather x1, blocking collectives, body(): piece = lax.all_gather(query_emb, 'dp', axis=0, tiled=True)  45 us
    unnamed x6, waiting for transfers between devices  34 us
    all_gather x1, waiting for transfers between devices, body(): lax.all_gather(normed, 'mp', axis=0, tiled=True)  17 us
    all_gather x1, blocking collectives, body(): every_score = lax.all_gather(part_scores, 'dp', axis=1, tiled=True)  16.3 us
    all_gather x1, waiting for transfers between devices, body(): grad_full = lax.all_gather(hidden_grad, 'mp', axis=0, tiled=True)  15.4 us
    sub x6, matrix products, softmax_rows(): raised = jnp.exp(scores - largest)  11.7 us
    dot_general x3, matrix products, attend_rows(): jnp.einsum('hqk,hke->hqe', weights, value_rows, preferred_element_type=jn...  8.08 us
    pmax x1, blocking collectives, body(): best = lax.pmax(best.astype(jnp.bfloat16), 'mp').astype(best.dtype)  6.12 us
  transfers between devices with their start and end apart: 5, of which 3 were waited for; matrix products, arithmetic and copies ran while one was open for 16% of the time, Pallas kernels for 0%

commit v1 on v0

v1 whole, which is shorter than its diff:
```python
from functools import partial
import math

import jax
import jax.numpy as jnp
from jax import lax
from jax.experimental import pallas as pl
from jax.experimental.pallas import tpu as pltpu
from jax.sharding import PartitionSpec as P

HEAD_DIM = 72
LANES = 128
EMB = 128
QTOK = 32
MP = 4
SCALE = HEAD_DIM ** (-0.5)
LOG2E = math.log2(math.e)
F32 = jnp.float32
BF16 = jnp.bfloat16

VMEM = pl.BlockSpec(memory_space=pltpu.VMEM)
SMEM = pl.BlockSpec(memory_space=pltpu.SMEM)
HBM = pl.BlockSpec(memory_space=pl.ANY)


def dot(left, right, left_dim, right_dim):
    return lax.dot_general(
        left, right, (((left_dim,), (right_dim,)), ((), ())), preferred_element_type=F32
    )


def shape(dims, kind):
    return jax.ShapeDtypeStruct(dims, kind)


def cost(flops, size, exps=0):
    return pl.CostEstimate(flops=int(flops), bytes_accessed=int(size), transcendentals=int(exps))


def full(*dims):
    return pl.BlockSpec(dims, lambda *_: (0,) * len(dims))


def place_of(index, model_index, rows_dev):
    return (model_index ^ (index // rows_dev)) * rows_dev + index % rows_dev


def pad_kernel(heads, mixing_ref, output_ref, mixing_pad, output_pad):
    mixing_pad[...] = jnp.zeros_like(mixing_pad)
    output_pad[...] = jnp.zeros_like(output_pad)
    for index in range(3 * heads):
        mixing_pad[:, index * LANES : index * LANES + HEAD_DIM] = mixing_ref[
            :, index * HEAD_DIM : (index + 1) * HEAD_DIM
        ]
    for index in range(heads):
        output_pad[:, index * LANES : index * LANES + HEAD_DIM] = output_ref[
            :, index * HEAD_DIM : (index + 1) * HEAD_DIM
        ]


def pad_weights(mixing, output, heads):
    width = mixing.shape[0]
    return pl.pallas_call(
        partial(pad_kernel, heads),
        out_shape=(
            shape((width, 3 * heads * LANES), BF16),
            shape((output.shape[0], heads * LANES), BF16),
        ),
        in_specs=[VMEM, VMEM],
        out_specs=(VMEM, VMEM),
        cost_estimate=cost(0, 8e6),
        name="pad_weights",
    )(mixing, output)


def forward_kernel(
    heads,
    rows_dev,
    where_ref,
    rows0,
    rows1,
    rows2,
    rows3,
    gain_ref,
    mixing_ref,
    output_ref,
    packed_ref,
    prob_ref,
    attended_ref,
    part0,
    part1,
    part2,
    part3,
    normed,
):
    head = pl.program_id(0)
    rows = rows_dev * MP

    @pl.when(head == 0)
    def _():
        for index, block in enumerate((rows0, rows1, rows2, rows3)):
            values = block[...].astype(F32)
            center = values - jnp.mean(values, axis=-1, keepdims=True)
            spread = jnp.mean(center * center, axis=-1, keepdims=True)
            normed[index * rows_dev : (index + 1) * rows_dev, :] = (
                center * lax.rsqrt(spread + 1e-06) * gain_ref[...]
            ).astype(BF16)

    packed = dot(normed[...], mixing_ref[...], 1, 0).astype(BF16)
    packed_ref[...] = packed
    query = packed[:, :LANES]
    key = packed[:, LANES : 2 * LANES]
    value = packed[:, 2 * LANES :]
    count = where_ref[0]
    model_index = where_ref[1]
    columns = lax.broadcasted_iota(jnp.int32, (1, rows), 1)
    seen = place_of(columns, model_index, rows_dev) < count
    step = rows_dev
    for chunk in range(rows // step):
        low = chunk * step
        score = dot(query[low : low + step], key, 1, 1)
        score = jnp.where(seen, score, -1e30)
        largest = jnp.max(score, axis=-1, keepdims=True)
        raised = jnp.exp2((score - largest) * (SCALE * LOG2E))
        total = jnp.sum(raised, axis=-1, keepdims=True)
        prob = (raised * (1.0 / total)).astype(BF16)
        prob_ref[0, low : low + step, :] = prob
        found = dot(prob, value, 1, 0)
        lines = lax.broadcasted_iota(jnp.int32, (step, 1), 0) + low
        live = place_of(lines, model_index, rows_dev) < count
        found = jnp.where(live, found, 0.0).astype(BF16)
        attended_ref[head, low : low + step, :] = found

    @pl.when(head == heads - 1)
    def _():
        joined = jnp.concatenate([attended_ref[index] for index in range(heads)], axis=1)
        for index, part in enumerate((part0, part1, part2, part3)):
            block = joined[index * rows_dev : (index + 1) * rows_dev]
            part[...] = dot(block, output_ref[...], 1, 1).astype(BF16)


def forward(where, blocks, gain, mixing_pad, output_pad, heads):
    rows_dev, width = blocks[0].shape
    rows = rows_dev * MP
    wide = 3 * LANES
    block = full(rows_dev, width)
    return pl.pallas_call(
        partial(forward_kernel, heads, rows_dev),
        grid=(heads,),
        out_shape=(
            shape((rows, heads * wide), BF16),
            shape((heads, rows, rows), BF16),
            shape((heads, rows, LANES), BF16),
        )
        + (shape((rows_dev, width), BF16),) * MP,
        in_specs=[SMEM]
        + [block] * MP
        + [
            full(1, width),
            pl.BlockSpec((width, wide), lambda head: (0, head)),
            full(width, heads * LANES),
        ],
        out_specs=(
            pl.BlockSpec((rows, wide), lambda head: (0, head)),
            pl.BlockSpec((1, rows, rows), lambda head: (head, 0, 0)),
            full(heads, rows, LANES),
        )
        + (block,) * MP,
        scratch_shapes=[pltpu.VMEM((rows, width), BF16)],
        cost_estimate=cost(3e9, 12e6, heads * rows * rows),
        name="forward_attention",
    )(where, *blocks, gain, mixing_pad, output_pad)


def weight_kernel(
    heads, rows_dev, pieces, where_ref, grad0, grad1, grad2, grad3, attended_ref, *refs
):
    outs, (stacked, result) = refs[: len(refs) - 2], refs[len(refs) - 2 :]
    for index, block in enumerate((grad0, grad1, grad2, grad3)):
        stacked[index * rows_dev : (index + 1) * rows_dev, :] = block[...]
    joined = jnp.concatenate([attended_ref[index] for index in range(heads)], axis=1)
    product = dot(stacked[...], joined, 0, 0)
    for index in range(heads):
        result[:, index * HEAD_DIM : (index + 1) * HEAD_DIM] = product[
            :, index * LANES : index * LANES + HEAD_DIM
        ]
    if pieces == 1:
        outs[0][...] = result[...]
    else:
        share = result.shape[0] // pieces
        mine = where_ref[2]
        for piece, out in enumerate(outs):
            start = pl.multiple_of((mine ^ piece) * share, 16)
            out[...] = result[pl.ds(start, share), :].astype(out.dtype)


def weight_parts(where, grads, attended, pieces):
    rows_dev, width = grads[0].shape
    heads = attended.shape[0]
    share = width // pieces
    narrow = heads * HEAD_DIM
    kinds = [F32] + [BF16] * (pieces - 1)
    return pl.pallas_call(
        partial(weight_kernel, heads, rows_dev, pieces),
        out_shape=tuple(shape((share, narrow), kind) for kind in kinds),
        in_specs=[SMEM] + [VMEM] * (MP + 1),
        out_specs=(VMEM,) * pieces,
        scratch_shapes=[
            pltpu.VMEM((rows_dev * MP, width), BF16),
            pltpu.VMEM((width, narrow), F32),
        ],
        cost_estimate=cost(7e8, 4e6),
        name="weight_parts",
    )(where, *grads, attended)


def backward_kernel(
    heads,
    rows_dev,
    where_ref,
    grad0,
    grad1,
    grad2,
    grad3,
    output_ref,
    packed_ref,
    prob_ref,
    mixing_hbm,
    part0,
    part1,
    part2,
    part3,
    stacked,
    joined,
    mixing,
    sem,
):
    head = pl.program_id(0)
    rows = rows_dev * MP
    fetch = pltpu.make_async_copy(mixing_hbm, mixing, sem)

    @pl.when(head == 0)
    def _():
        fetch.start()
        for index, block in enumerate((grad0, grad1, grad2, grad3)):
            stacked[index * rows_dev : (index + 1) * rows_dev, :] = block[...]

    count = where_ref[0]
    model_index = where_ref[1]
    lines = lax.broadcasted_iota(jnp.int32, (rows, 1), 0)
    live = place_of(lines, model_index, rows_dev) < count
    flow = dot(stacked[...], output_ref[...], 1, 0)
    flow = jnp.where(live, flow, 0.0).astype(BF16)
    query = packed_ref[:, :LANES]
    key = packed_ref[:, LANES : 2 * LANES]
    value = packed_ref[:, 2 * LANES :]
    step = rows // 2
    grad_key = jnp.zeros((rows, LANES), F32)
    grad_value = jnp.zeros((rows, LANES), F32)
    grad_query = []
    for low in range(0, rows, step):
        part = flow[low : low + step]
        weights = prob_ref[0, low : low + step, :]
        prob = weights.astype(F32)
        grad_prob = dot(part, value, 1, 1)
        delta = jnp.sum(grad_prob * prob, axis=-1, keepdims=True)
        grad_score = (prob * (grad_prob - delta)).astype(BF16)
        grad_query.append((dot(grad_score, key, 1, 0) * SCALE).astype(BF16))
        grad_key += dot(grad_score, query[low : low + step], 0, 0)
        grad_value += dot(weights, part, 0, 0)
    joined[head, :, :LANES] = jnp.concatenate(grad_query, axis=0)
    joined[head, :, LANES : 2 * LANES] = (grad_key * SCALE).astype(BF16)
    joined[head, :, 2 * LANES :] = grad_value.astype(BF16)

    @pl.when(head == heads - 1)
    def _():
        fetch.wait()
        everything = jnp.concatenate([joined[index] for index in range(heads)], axis=1)
        for index, part in enumerate((part0, part1, part2, part3)):
            block = everything[index * rows_dev : (index + 1) * rows_dev]
            part[...] = dot(block, mixing[...], 1, 1).astype(BF16)


def backward(where, grads, output_pad, packed, probs, mixing_pad, heads):
    rows_dev, width = grads[0].shape
    rows = rows_dev * MP
    wide = 3 * LANES
    block = full(rows_dev, width)
    return pl.pallas_call(
        partial(backward_kernel, heads, rows_dev),
        grid=(heads,),
        out_shape=(shape((rows_dev, width), BF16),) * MP,
        in_specs=[SMEM]
        + [block] * MP
        + [
            pl.BlockSpec((width, LANES), lambda head: (0, head)),
            pl.BlockSpec((rows, wide), lambda head: (0, head)),
            pl.BlockSpec((1, rows, rows), lambda head: (head, 0, 0)),
            HBM,
        ],
        out_specs=(block,) * MP,
        scratch_shapes=[
            pltpu.VMEM((rows, width), BF16),
            pltpu.VMEM((heads, rows, wide), BF16),
            pltpu.VMEM((width, heads * wide), BF16),
            pltpu.SemaphoreType.DMA,
        ],
        cost_estimate=cost(6e9, 12e6),
        name="backward_attention",
    )(where, *grads, output_pad, packed, probs, mixing_pad)


def score_kernel(
    rows_dev, where_ref, patch_ref, part_ref, near_ref, far_ref, embed_ref, tokens_ref,
    hidden_ref, best_ref, page_emb
):
    @pl.when(pl.program_id(0) == 0)
    def _():
        mixed = part_ref[...].astype(F32) + near_ref[...].astype(F32) + far_ref[...].astype(F32)
        hidden = (patch_ref[...].astype(F32) + mixed).astype(BF16)
        hidden_ref[...] = hidden
        embedded = dot(hidden, embed_ref[...], 1, 0)
        page_emb[...] = (
            embedded
            * lax.rsqrt(jnp.sum(embedded * embedded, axis=-1, keepdims=True) + 1e-06)
        ).astype(BF16)

    similar = dot(page_emb[...], tokens_ref[...], 1, 1)
    lines = lax.broadcasted_iota(jnp.int32, (rows_dev, 1), 0) + where_ref[1] * rows_dev
    similar = jnp.where(lines < where_ref[0], similar, -2.0)
    best_ref[...] = jnp.max(similar, axis=0, keepdims=True)


def hidden_and_best(where, patches, part, near, far, embed_weight, tokens):
    rows_dev, width = patches.shape
    size = tokens.shape[0]
    chunk = math.gcd(size, 1024)
    block = full(rows_dev, width)
    return pl.pallas_call(
        partial(score_kernel, rows_dev),
        grid=(size // chunk,),
        out_shape=(shape((rows_dev, width), BF16), shape((1, size), F32)),
        in_specs=[SMEM]
        + [block] * 4
        + [full(width, EMB), pl.BlockSpec((chunk, EMB), lambda index: (index, 0))],
        out_specs=(block, pl.BlockSpec((1, chunk), lambda index: (0, index))),
        scratch_shapes=[pltpu.VMEM((rows_dev, EMB), BF16)],
        cost_estimate=cost(1e8, 2e6),
        name="hidden_and_best",
    )(where, patches, part, near, far, embed_weight, tokens)


def norm_back_kernel(patch_ref, gain_ref, grad_ref, part_ref, near_ref, far_ref, out_ref):
    values = patch_ref[...].astype(F32)
    center = values - jnp.mean(values, axis=-1, keepdims=True)
    spread = jnp.mean(center * center, axis=-1, keepdims=True)
    inverse = lax.rsqrt(spread + 1e-06)
    flow = part_ref[...].astype(F32) + near_ref[...].astype(F32) + far_ref[...].astype(F32)
    flow = flow * gain_ref[...]
    along = jnp.mean(flow * center, axis=-1, keepdims=True)
    level = jnp.mean(flow, axis=-1, keepdims=True)
    result = inverse * (flow - level - center * (inverse * inverse * along))
    out_ref[...] = (grad_ref[...].astype(F32) + result).astype(BF16)


def norm_back(patches, gain, grads, part, near, far):
    return pl.pallas_call(
        norm_back_kernel,
        out_shape=shape(patches.shape, BF16),
        in_specs=[VMEM] * 6,
        out_specs=VMEM,
        cost_estimate=cost(3e6, 2e6),
        name="norm_back",
    )(patches, gain, grads, part, near, far)


def unit_rows(values):
    return values * lax.rsqrt(jnp.sum(values * values, axis=-1, keepdims=True) + 1e-06)


def swap(values, axis, distance):
    size = lax.axis_size(axis)
    return lax.ppermute(values, axis, [(index, index ^ distance) for index in range(size)])


def scatter_sum(parts):
    part0, part1, part2, part3 = parts
    relayed = swap(part3, "mp", 1)
    near = swap(part1, "mp", 1)
    far = swap((part2.astype(F32) + relayed.astype(F32)).astype(BF16), "mp", 2)
    return part0, near, far


def body(
    patches,
    norm_gain,
    query_key_value,
    output_weight,
    embed_weight,
    query_tokens,
    patch_counts,
    positive_page,
    hidden_grad,
):
    model_index = lax.axis_index("mp")
    data_index = lax.axis_index("dp")
    data_size = lax.axis_size("dp")
    few = data_size == 8
    heads = output_weight.shape[1] // HEAD_DIM
    gain = norm_gain.reshape(1, -1)
    count = lax.dynamic_index_in_dim(patch_counts, data_index, 0, keepdims=False)
    where = jnp.stack([count, model_index, data_index]).astype(jnp.int32)

    rows1 = swap(patches, "mp", 1)
    rows2 = swap(patches, "mp", 2)
    rows3 = swap(rows2, "mp", 1)
    grads1 = swap(hidden_grad, "mp", 1)
    late_grad, _ = lax.optimization_barrier((hidden_grad, rows2))
    grads2 = swap(late_grad, "mp", 2)
    grads3 = swap(grads2, "mp", 1)
    grads = (hidden_grad, grads1, grads2, grads3)

    local = query_tokens.shape[0]
    query_emb = unit_rows(query_tokens.astype(F32)).astype(BF16).reshape(local * QTOK, EMB)
    if few:
        pieces = [query_emb] + [swap(query_emb, "dp", index) for index in range(1, data_size)]
        tokens = jnp.concatenate(pieces, axis=0)
    else:
        tokens = lax.all_gather(query_emb, "dp", axis=0, tiled=True)

    mixing_pad, output_pad = pad_weights(query_key_value, output_weight, heads)
    packed, probs, attended, *parts = forward(
        where, (patches, rows1, rows2, rows3), gain, mixing_pad, output_pad, heads
    )
    hidden, best = hidden_and_best(where, patches, *scatter_sum(parts), embed_weight, tokens)

    if few:
        mine, *others = weight_parts(where, grads, attended, data_size)
        weight_grad = mine
        for index, other in enumerate(others):
            weight_grad = weight_grad + swap(other, "dp", index + 1).astype(F32)
    else:
        (whole,) = weight_parts(where, grads, attended, 1)
        weight_grad = lax.psum_scatter(whole, "dp", scatter_dimension=0, tiled=True)

    grad_parts = backward(where, grads, output_pad, packed, probs, mixing_pad, heads)
    patch_grad = norm_back(patches, gain, hidden_grad, *scatter_sum(grad_parts))

    best = jnp.maximum(best, swap(best, "mp", 1))
    best = jnp.maximum(best, swap(best, "mp", 2))
    part_scores = jnp.sum(best.reshape(-1, QTOK), axis=1)
    if few:
        pieces = part_scores.reshape(data_size, local)
        found = [pieces[0]]
        for index in range(1, data_size):
            found.append(swap(pieces[index], "dp", index))
        found = jnp.stack(found, axis=1)
        order = jnp.arange(data_size, dtype=jnp.int32)
        chosen = (order[:, None] ^ data_index) == order[None, :]
        my_scores = jnp.sum(jnp.where(chosen[None], found[:, :, None], 0.0), axis=1)
    else:
        every = lax.all_gather(part_scores.reshape(-1, 1), "dp", axis=1, tiled=True)
        my_scores = lax.dynamic_slice_in_dim(every, data_index * local, local, 0)
    columns = jnp.arange(my_scores.shape[1], dtype=jnp.int32)
    chosen = columns[None, :] == positive_page[:, None]
    positive_score = jnp.sum(jnp.where(chosen, my_scores, 0.0), axis=1)
    negative_score = jnp.max(jnp.where(chosen, -1e30, my_scores), axis=1)
    loss = jax.nn.softplus(negative_score - positive_score)
    return (hidden, patch_grad, weight_grad, my_scores, loss)


def solution(mesh):
    return jax.shard_map(
        body,
        mesh=mesh,
        in_specs=(
            P(("dp", "mp"), None),
            P(),
            P(None, "mp"),
            P(None, "mp"),
            P(),
            P("dp", None, None),
            P(),
            P("dp"),
            P(("dp", "mp"), None),
        ),
        out_specs=(
            P(("dp", "mp"), None),
            P(("dp", "mp"), None),
            P("dp", "mp"),
            P("dp", None),
            P("dp"),
        ),
        check_vma=False,
    )
```

time: 226 us -> 122 us (0.54)
  blocking collectives: 67.4 us -> 0 us
  waiting for transfers between devices: 66.4 us -> 12.5 us
  matrix products: 53.7 us -> 0 us
  starting transfers between devices: 0.2 us -> 46.1 us
  Pallas kernels: 0 us -> 44.7 us
  between operations: 14.7 us -> 0.92 us
  other arithmetic: 14.6 us -> 6.61 us
  local copies, waits for them, and re-layouts: 6.75 us -> 10.3 us
    all_gather x2 -> x0, blocking collectives: 61.3 us -> none  [the longest x1 45 us: body(): piece = lax.all_gather(query_emb, 'dp', axis=0, tiled=True)]
    ppermute x0 -> x35, starting transfers between devices: none -> 46.1 us  [swap(): lax.ppermute(values, axis, [(index, index ^ distance) for index in range(...]
    pallas_call x0 -> x6, Pallas kernels: none -> 44.7 us  [the longest x1 15.4 us: forward(): pl.pallas_call(partial(forward_kernel, heads, rows_dev), grid=(heads,), o...]
    dot_general x25 -> x0, matrix products: 42 us -> none  [the longest x3 8.08 us: attend_rows(): jnp.einsum('hqk,hke->hqe', weights, value_rows, preferred_element_type=jn...]
    unnamed x6 -> x0, waiting for transfers between devices: 34 us -> none
    all_gather x2 -> x0, waiting for transfers between devices: 32.4 us -> none  [the longest x1 17 us: body(): lax.all_gather(normed, 'mp', axis=0, tiled=True)]
    ppermute x0 -> x35, waiting for transfers between devices: none -> 12.5 us  [swap(): lax.ppermute(values, axis, [(index, index ^ distance) for index in range(...]
    sub x6 -> x0, matrix products: 11.7 us -> none  [softmax_rows(): raised = jnp.exp(scores - largest)]
  transfers between devices with their start and end apart: 5 -> 35, of which waited for: 3 -> 8; matrix products, arithmetic and copies ran while one was open for 16% -> 12% of each run, Pallas kernels for 0% -> 35%
where the time goes in v1:
time: 122 us; the launch traced here: 121 us
  starting transfers between devices  46.1 us (38%)
  Pallas kernels  44.7 us (37%)
  waiting for transfers between devices  12.5 us (10%)
  local copies, waits for them, and re-layouts  10.3 us (8%)
  other arithmetic  6.61 us (5%)
    ppermute x35, starting transfers between devices, swap(): lax.ppermute(values, axis, [(index, index ^ distance) for index in range(...  46.1 us
    pallas_call x1, Pallas kernels, forward(): pl.pallas_call(partial(forward_kernel, heads, rows_dev), grid=(heads,), o...  15.4 us
    pallas_call x1, Pallas kernels, backward(): pl.pallas_call(partial(backward_kernel, heads, rows_dev), grid=(heads,),...  14.8 us
    ppermute x35, waiting for transfers between devices, swap(): lax.ppermute(values, axis, [(index, index ^ distance) for index in range(...  12.5 us
    unnamed x53, local copies, waits for them, and re-layouts  8.12 us
    pallas_call x1, Pallas kernels, pad_weights(): pl.pallas_call(partial(pad_kernel, heads), out_shape=(shape((width, 3 * h...  5.98 us
    pallas_call x1, Pallas kernels, weight_parts(): pl.pallas_call(partial(weight_kernel, heads, rows_dev, pieces), out_shape...  3.41 us
    pallas_call x1, Pallas kernels, hidden_and_best(): pl.pallas_call(partial(score_kernel, rows_dev), grid=(size // chunk,), ou...  2.56 us
  transfers between devices with their start and end apart: 35, of which 8 were waited for; matrix products, arithmetic and copies ran while one was open for 12% of the time, Pallas kernels for 35%

profile of v1, /device:TPU:0, one launch (start us, length us, event | category | flops | bytes accessed | tf_op | source)
XLA Modules:
  0.0 121.2 jit_solution(17017253650907935247)
XLA Ops:
  0.6 3.0 %collective-permute-start.1 = (bf16[128,1152]{1,0:T(8,128)(2,1)}, bf16[128,1152]{1,0:T(8,128)(2,1)S(1)}, u32[]{:S(2)}, u32[]{:S(2)}) collective-permute-start(bf16[128,1152]{1,0:T(8,128)(2,1)} %patch_ref.3), channel_id=1, source_target_pairs={{0,2},{1,3},{2,0},{3,1},{4,6},{5,7},{6,4},{7,5},{8,10},{9,11},{10,... | collective-permute-start | bytes 884744 | tf_op jit(solution)/shard_map/ppermute | solution.py:383
  5.4 1.6 %collective-permute-start.6 = (bf16[128,128]{1,0:T(8,128)(2,1)S(1)}, bf16[128,128]{1,0:T(8,128)(2,1)S(1)}, u32[]{:S(2)}, u32[]{:S(2)}) collective-permute-start(bf16[128,128]{1,0:T(8,128)(2,1)S(1)} %bitcast.12), channel_id=1, source_target_pairs={{0,4},{4,0},{8,12},{12,8},{16,20},{20,16},{24,28},{28,24},{1,5},{5... | collective-permute-start | bytes 98312 | tf_op jit(solution)/shard_map/ppermute | solution.py:383
  7.0 1.6 %collective-permute-start.7 = (bf16[128,128]{1,0:T(8,128)(2,1)S(1)}, bf16[128,128]{1,0:T(8,128)(2,1)S(1)}, u32[]{:S(2)}, u32[]{:S(2)}) collective-permute-start(bf16[128,128]{1,0:T(8,128)(2,1)S(1)} %bitcast.13), channel_id=1, source_target_pairs={{0,8},{4,12},{8,0},{12,4},{16,24},{20,28},{24,16},{28,20},{1,9},{5... | collective-permute-start | bytes 98312 | tf_op jit(solution)/shard_map/ppermute | solution.py:383
  11.6 4.1 %copy.17.mixing_ref = bf16[1152,864]{1,0:T(8,128)(2,1)} copy(bf16[1152,864]{0,1:T(8,128)(2,1)} %param.11) | data formatting | bytes 3981312 | tf_op args[2]
  17.6 6.0 %pad_weights.1 = (bf16[1152,1536]{1,0:T(8,128)(2,1)}, bf16[1152,512]{1,0:T(8,128)(2,1)}) custom-call(bf16[1152,864]{1,0:T(8,128)(2,1)} %copy.17.mixing_ref, bf16[1152,288]{1,0:T(8,128)(2,1)} %copy.18.output_ref), custom_call_target="tpu_custom_call" | custom-call | bytes 8000000 | tf_op jit(solution)/shard_map/pad_weights/pallas_call | solution.py:63
  23.6 2.6 %collective-permute-start.9 = (bf16[128,128]{1,0:T(8,128)(2,1)S(1)}, bf16[128,128]{1,0:T(8,128)(2,1)S(1)}, u32[]{:S(2)}, u32[]{:S(2)}) collective-permute-start(bf16[128,128]{1,0:T(8,128)(2,1)S(1)} %bitcast.16), channel_id=1, source_target_pairs={{0,16},{4,20},{8,24},{12,28},{16,0},{20,4},{24,8},{28,12},{1,17},{... | collective-permute-start | bytes 98312 | tf_op jit(solution)/shard_map/ppermute | solution.py:383
  27.6 3.7 %collective-permute-start.11 = (bf16[128,128]{1,0:T(8,128)(2,1)S(1)}, bf16[128,128]{1,0:T(8,128)(2,1)S(1)}, u32[]{:S(2)}, u32[]{:S(2)}) collective-permute-start(bf16[128,128]{1,0:T(8,128)(2,1)S(1)} %bitcast.18), channel_id=1, source_target_pairs={{0,24},{4,28},{8,16},{12,20},{16,8},{20,12},{24,0},{28,4},{1,25},{... | collective-permute-start | bytes 98312 | tf_op jit(solution)/shard_map/ppermute | solution.py:383
  32.2 15.4 %forward_attention.1 = (bf16[512,1536]{1,0:T(8,128)(2,1)}, bf16[4,512,512]{2,1,0:T(8,128)(2,1)}, bf16[4,512,128]{2,1,0:T(8,128)(2,1)}, bf16[128,1152]{1,0:T(8,12...) custom-call(s32[3]{0:T(128)} %pad_add_fusion.where_ref, ...), custom_call_target="tpu_custom_call" | custom-call | flops 3000000000 | bytes 12000000 | tf_op jit(solution)/shard_map/forward_attention/pallas_call | solution.py:147
  52.8 3.4 %weight_parts.1 = (f32[144,288]{1,0:T(8,128)}, bf16[144,288]{1,0:T(8,128)(2,1)}, bf16[144,288]{1,0:T(8,128)(2,1)}, bf16[144,288]{1,0:T(8,128)(2,1)}, bf16[144,28...) custom-call(s32[3]{0:T(128)} %pad_add_fusion.where_ref, ...), custom_call_target="tpu_custom_call" | custom-call | flops 700000000 | bytes 4000000 | tf_op jit(solution)/shard_map/weight_parts/pallas_call | solution.py:203
  56.2 1.5 %collective-permute-start.19 = (bf16[144,288]{1,0:T(8,128)(2,1)}, bf16[144,288]{1,0:T(8,128)(2,1)S(1)}, u32[]{:S(2)}, u32[]{:S(2)}) collective-permute-start(bf16[144,288]{1,0:T(8,128)(2,1)} %get-tuple-element.45), channel_id=1, source_target_pairs={{0,4},{4,0},{8,12},{12,8},{16,20},{20,16},{24,28},{28,24},{1,5},{5... | collective-permute-start | bytes 248840 | tf_op jit(solution)/shard_map/ppermute | solution.py:383
  57.8 2.0 %collective-permute-start.21 = (bf16[144,288]{1,0:T(8,128)(2,1)}, bf16[144,288]{1,0:T(8,128)(2,1)S(1)}, u32[]{:S(2)}, u32[]{:S(2)}) collective-permute-start(bf16[144,288]{1,0:T(8,128)(2,1)} %get-tuple-element.47), channel_id=1, source_target_pairs={{0,12},{4,8},{8,4},{12,0},{16,28},{20,24},{24,20},{28,16},{1,13},{... | collective-permute-start | bytes 248840 | tf_op jit(solution)/shard_map/ppermute | solution.py:383
  59.8 14.8 %backward_attention.1 = (bf16[128,1152]{1,0:T(8,128)(2,1)}, bf16[128,1152]{1,0:T(8,128)(2,1)}, bf16[128,1152]{1,0:T(8,128)(2,1)}, bf16[128,1152]{1,0:T(8,128)(2,1)}) custom-call(s32[3]{0:T(128)} %pad_add_fusion.where_ref, bf16[128,1152]{1,0:T(8,128)(2,1)} %grad0.3, bf16[128,1152]{1,0:T(8,128)(2,1)} %copy-done.15, bf16[128,1152]{1,0:T(8,128)(2,1)} %copy-done.14, ...), custom_call_target="tpu_custom_call" | custom-call | flops 6000000000 | bytes 12000000 | tf_op jit(solution)/shard_map/backward_attention/pallas_call | solution.py:289
  74.6 2.3 %collective-permute-start.22 = (bf16[144,288]{1,0:T(8,128)(2,1)S(1)}, bf16[144,288]{1,0:T(8,128)(2,1)S(1)}, u32[]{:S(2)}, u32[]{:S(2)}) collective-permute-start(bf16[144,288]{1,0:T(8,128)(2,1)S(1)} %copy-done.21), channel_id=1, source_target_pairs={{0,16},{4,20},{8,24},{12,28},{16,0},{20,4},{24,8},{28,12},{1,17},{... | collective-permute-start | bytes 248840 | tf_op jit(solution)/shard_map/ppermute | solution.py:383
  76.9 1.7 %collective-permute-start.23 = (bf16[144,288]{1,0:T(8,128)(2,1)S(1)}, bf16[144,288]{1,0:T(8,128)(2,1)S(1)}, u32[]{:S(2)}, u32[]{:S(2)}) collective-permute-start(bf16[144,288]{1,0:T(8,128)(2,1)S(1)} %copy-done.20), channel_id=1, source_target_pairs={{0,20},{4,16},{8,28},{12,24},{16,4},{20,0},{24,12},{28,8},{1,21},{... | collective-permute-start | bytes 248840 | tf_op jit(solution)/shard_map/ppermute | solution.py:383
  78.6 3.6 %collective-permute-start.24 = (bf16[144,288]{1,0:T(8,128)(2,1)S(1)}, bf16[144,288]{1,0:T(8,128)(2,1)S(1)}, u32[]{:S(2)}, u32[]{:S(2)}) collective-permute-start(bf16[144,288]{1,0:T(8,128)(2,1)S(1)} %copy-done.19), channel_id=1, source_target_pairs={{0,24},{4,28},{8,16},{12,20},{16,8},{20,12},{24,0},{28,4},{1,25},{... | collective-permute-start | bytes 248840 | tf_op jit(solution)/shard_map/ppermute | solution.py:383
  83.2 2.6 %hidden_and_best.1 = (bf16[128,1152]{1,0:T(8,128)(2,1)}, f32[1,1024]{1,0:T(1,128)}) custom-call(s32[3]{0:T(128)} %pad_add_fusion.where_ref, bf16[128,1152]{1,0:T(8,128)(2,1)} %patch_ref.3, bf16[128,1152]{1,0:T(8,128)(2,1)} %get-tuple-element.31.part_ref, bf16[128,1152]{1,0:T(8,128)(2,1)} %copy-done.2, bf16[128,1152]{1,0:T(8,128)(2,1)} %copy-done.4, ...), custom_call_target="tpu_custom_call" | custom-call | flops 100000000 | bytes 2000000 | tf_op jit(solution)/shard_map/hidden_and_best/pallas_call | solution.py:339
  85.8 4.3 %collective-permute-done.22 = bf16[144,288]{1,0:T(8,128)(2,1)S(1)} collective-permute-done((bf16[144,288]{1,0:T(8,128)(2,1)S(1)}, bf16[144,288]{1,0:T(8,128)(2,1)S(1)}, u32[]{:S(2)}, u32[]{:S(2)}) %collective-permute-start.22) | collective-permute-done | bytes 82976 | tf_op jit(solution)/shard_map/ppermute | solution.py:383
  90.0 3.4 %collective-permute-done.23 = bf16[144,288]{1,0:T(8,128)(2,1)S(1)} collective-permute-done((bf16[144,288]{1,0:T(8,128)(2,1)S(1)}, bf16[144,288]{1,0:T(8,128)(2,1)S(1)}, u32[]{:S(2)}, u32[]{:S(2)}) %collective-permute-start.23) | collective-permute-done | bytes 82976 | tf_op jit(solution)/shard_map/ppermute | solution.py:383
  99.5 2.4 %collective-permute-start.34 = (f32[4]{0:T(128)S(1)}, f32[4]{0:T(128)S(1)}, u32[]{:S(2)}, u32[]{:S(2)}) collective-permute-start(f32[4]{0:T(128)S(1)} %get-tuple-element.55), channel_id=1, source_target_pairs={{0,28},{4,24},{8,20},{12,16},{16,12},{20,8},{24,4},{28,0},{1,29},{... | collective-permute-start | bytes 56 | tf_op jit(solution)/shard_map/ppermute | solution.py:383
  103.3 3.8 %collective-permute-start.29 = (f32[4]{0:T(128)S(1)}, f32[4]{0:T(128)S(1)}, u32[]{:S(2)}, u32[]{:S(2)}) collective-permute-start(f32[4]{0:T(128)S(1)} %get-tuple-element.60), channel_id=1, source_target_pairs={{0,8},{4,12},{8,0},{12,4},{16,24},{20,28},{24,16},{28,20},{1,9},{5... | collective-permute-start | bytes 56 | tf_op jit(solution)/shard_map/ppermute | solution.py:383
  109.5 2.0 %collective-permute-start.32 = (f32[4]{0:T(128)S(1)}, f32[4]{0:T(128)S(1)}, u32[]{:S(2)}, u32[]{:S(2)}) collective-permute-start(f32[4]{0:T(128)S(1)} %get-tuple-element.57), channel_id=1, source_target_pairs={{0,20},{4,16},{8,28},{12,24},{16,4},{20,0},{24,12},{28,8},{1,21},{... | collective-permute-start | bytes 56 | tf_op jit(solution)/shard_map/ppermute | solution.py:383
  111.5 3.3 %collective-permute-start.33 = (f32[4]{0:T(128)S(1)}, f32[4]{0:T(128)S(1)}, u32[]{:S(2)}, u32[]{:S(2)}) collective-permute-start(f32[4]{0:T(128)S(1)} %get-tuple-element.56), channel_id=1, source_target_pairs={{0,24},{4,28},{8,16},{12,20},{16,8},{20,12},{24,0},{28,4},{1,25},{... | collective-permute-start | bytes 56 | tf_op jit(solution)/shard_map/ppermute | solution.py:383
  114.9 2.0 %collective-permute-done.33 = f32[4]{0:T(128)S(1)} collective-permute-done((f32[4]{0:T(128)S(1)}, f32[4]{0:T(128)S(1)}, u32[]{:S(2)}, u32[]{:S(2)}) %collective-permute-start.33) | collective-permute-done | bytes 48 | tf_op jit(solution)/shard_map/ppermute | solution.py:383
  118.6 2.5 %norm_back.1 = bf16[128,1152]{1,0:T(8,128)(2,1)} custom-call(bf16[128,1152]{1,0:T(8,128)(2,1)} %patch_ref.3, f32[1,1152]{1,0:T(1,128)} %reshape.68.gain_ref, bf16[128,1152]{1,0:T(8,128)(2,1)} %grad0.3, bf16[128,1152]{1,0:T(8,128)(2,1)} %get-tuple-element.39.part_ref, bf16[128,1152]{1,0:T(8,128)(2,1)} %copy-done.6, bf16[128,1152]{1,0:T(8,128)(2,1)} %copy-done.7), custom_call_target="tpu_custom_call" | custom-call | flops 3000000 | bytes 2000000 | tf_op jit(solution)/shard_map/norm_back/pallas_call | solution.py:367
  (127 shorter events, 26.9 us)
Async XLA Ops:
  0.6 25.6 %collective-permute-start.1 = (bf16[128,1152]{1,0:T(8,128)(2,1)}, bf16[128,1152]{1,0:T(8,128)(2,1)S(1)}, u32[]{:S(2)}, u32[]{:S(2)}) collective-permute-start(bf16[128,1152]{1,0:T(8,128)(2,1)} %patch_ref.3), channel_id=1, source_target_pairs={{0,2},{1,3},{2,0},{3,1},{4,6},{5,7},{6,4},{7,5},{8,10},{9,11},{10,... | collective-permute-start | bytes 884744 | tf_op jit(solution)/shard_map/ppermute | solution.py:383
  3.7 27.6 %collective-permute-start = (bf16[128,1152]{1,0:T(8,128)(2,1)}, bf16[128,1152]{1,0:T(8,128)(2,1)S(1)}, u32[]{:S(2)}, u32[]{:S(2)}) collective-permute-start(bf16[128,1152]{1,0:T(8,128)(2,1)} %patch_ref.3), channel_id=1, source_target_pairs={{0,1},{1,0},{2,3},{3,2},{4,5},{5,4},{6,7},{7,6},{8,9},{9,8},{10,11... | collective-permute-start | bytes 884744 | tf_op jit(solution)/shard_map/ppermute | solution.py:383
  5.4 18.2 %collective-permute-start.6 = (bf16[128,128]{1,0:T(8,128)(2,1)S(1)}, bf16[128,128]{1,0:T(8,128)(2,1)S(1)}, u32[]{:S(2)}, u32[]{:S(2)}) collective-permute-start(bf16[128,128]{1,0:T(8,128)(2,1)S(1)} %bitcast.12), channel_id=1, source_target_pairs={{0,4},{4,0},{8,12},{12,8},{16,20},{20,16},{24,28},{28,24},{1,5},{5... | collective-permute-start | bytes 98312 | tf_op jit(solution)/shard_map/ppermute | solution.py:383
  7.0 19.3 %collective-permute-start.7 = (bf16[128,128]{1,0:T(8,128)(2,1)S(1)}, bf16[128,128]{1,0:T(8,128)(2,1)S(1)}, u32[]{:S(2)}, u32[]{:S(2)}) collective-permute-start(bf16[128,128]{1,0:T(8,128)(2,1)S(1)} %bitcast.13), channel_id=1, source_target_pairs={{0,8},{4,12},{8,0},{12,4},{16,24},{20,28},{24,16},{28,20},{1,9},{5... | collective-permute-start | bytes 98312 | tf_op jit(solution)/shard_map/ppermute | solution.py:383
  8.5 19.1 %collective-permute-start.8 = (bf16[128,128]{1,0:T(8,128)(2,1)S(1)}, bf16[128,128]{1,0:T(8,128)(2,1)S(1)}, u32[]{:S(2)}, u32[]{:S(2)}) collective-permute-start(bf16[128,128]{1,0:T(8,128)(2,1)S(1)} %bitcast.14), channel_id=1, source_target_pairs={{0,12},{4,8},{8,4},{12,0},{16,28},{20,24},{24,20},{28,16},{1,13},{... | collective-permute-start | bytes 98312 | tf_op jit(solution)/shard_map/ppermute | solution.py:383
  23.6 24.0 %collective-permute-start.9 = (bf16[128,128]{1,0:T(8,128)(2,1)S(1)}, bf16[128,128]{1,0:T(8,128)(2,1)S(1)}, u32[]{:S(2)}, u32[]{:S(2)}) collective-permute-start(bf16[128,128]{1,0:T(8,128)(2,1)S(1)} %bitcast.16), channel_id=1, source_target_pairs={{0,16},{4,20},{8,24},{12,28},{16,0},{20,4},{24,8},{28,12},{1,17},{... | collective-permute-start | bytes 98312 | tf_op jit(solution)/shard_map/ppermute | solution.py:383
  26.2 21.5 %collective-permute-start.10 = (bf16[128,128]{1,0:T(8,128)(2,1)S(1)}, bf16[128,128]{1,0:T(8,128)(2,1)S(1)}, u32[]{:S(2)}, u32[]{:S(2)}) collective-permute-start(bf16[128,128]{1,0:T(8,128)(2,1)S(1)} %bitcast.17), channel_id=1, source_target_pairs={{0,20},{4,16},{8,28},{12,24},{16,4},{20,0},{24,12},{28,8},{1,21},{... | collective-permute-start | bytes 98312 | tf_op jit(solution)/shard_map/ppermute | solution.py:383
  27.6 20.7 %collective-permute-start.11 = (bf16[128,128]{1,0:T(8,128)(2,1)S(1)}, bf16[128,128]{1,0:T(8,128)(2,1)S(1)}, u32[]{:S(2)}, u32[]{:S(2)}) collective-permute-start(bf16[128,128]{1,0:T(8,128)(2,1)S(1)} %bitcast.18), channel_id=1, source_target_pairs={{0,24},{4,28},{8,16},{12,20},{16,8},{20,12},{24,0},{28,4},{1,25},{... | collective-permute-start | bytes 98312 | tf_op jit(solution)/shard_map/ppermute | solution.py:383
  31.3 26.5 %collective-permute-start.12 = (bf16[128,128]{1,0:T(8,128)(2,1)S(1)}, bf16[128,128]{1,0:T(8,128)(2,1)S(1)}, u32[]{:S(2)}, u32[]{:S(2)}) collective-permute-start(bf16[128,128]{1,0:T(8,128)(2,1)S(1)} %bitcast.19), channel_id=1, source_target_pairs={{0,28},{4,24},{8,20},{12,16},{16,12},{20,8},{24,4},{28,0},{1,29},{... | collective-permute-start | bytes 98312 | tf_op jit(solution)/shard_map/ppermute | solution.py:383
  31.5 16.9 %collective-permute-start.14 = (bf16[128,1152]{1,0:T(8,128)(2,1)S(1)}, bf16[128,1152]{1,0:T(8,128)(2,1)S(1)}, u32[]{:S(2)}, u32[]{:S(2)}) collective-permute-start(bf16[128,1152]{1,0:T(8,128)(2,1)S(1)} %copy-done.5), channel_id=1, source_target_pairs={{0,2},{1,3},{2,0},{3,1},{4,6},{5,7},{6,4},{7,5},{8,10},{9,11},{10,... | collective-permute-start | bytes 884744 | tf_op jit(solution)/shard_map/ppermute | solution.py:383
  48.3 26.3 %collective-permute-start.3 = (bf16[128,1152]{1,0:T(8,128)(2,1)}, bf16[128,1152]{1,0:T(8,128)(2,1)S(1)}, u32[]{:S(2)}, u32[]{:S(2)}) collective-permute-start(bf16[128,1152]{1,0:T(8,128)(2,1)} %get-tuple-element.32), channel_id=1, source_target_pairs={{0,1},{1,0},{2,3},{3,2},{4,5},{5,4},{6,7},{7,6},{8,9},{9,8},{10,11... | collective-permute-start | bytes 884744 | tf_op jit(solution)/shard_map/ppermute | solution.py:383
  50.5 31.8 %collective-permute-start.5 = (bf16[128,1152]{1,0:T(8,128)(2,1)S(1)}, bf16[128,1152]{1,0:T(8,128)(2,1)S(1)}, u32[]{:S(2)}, u32[]{:S(2)}) collective-permute-start(bf16[128,1152]{1,0:T(8,128)(2,1)S(1)} %add_convert_fusion.1), channel_id=1, source_target_pairs={{0,2},{1,3},{2,0},{3,1},{4,6},{5,7},{6,4},{7,5},{8,10},{9,11},{10,... | collective-permute-start | bytes 884744 | tf_op jit(solution)/shard_map/ppermute | solution.py:383
  56.2 20.7 %collective-permute-start.19 = (bf16[144,288]{1,0:T(8,128)(2,1)}, bf16[144,288]{1,0:T(8,128)(2,1)S(1)}, u32[]{:S(2)}, u32[]{:S(2)}) collective-permute-start(bf16[144,288]{1,0:T(8,128)(2,1)} %get-tuple-element.45), channel_id=1, source_target_pairs={{0,4},{4,0},{8,12},{12,8},{16,20},{20,16},{24,28},{28,24},{1,5},{5... | collective-permute-start | bytes 248840 | tf_op jit(solution)/shard_map/ppermute | solution.py:383
  57.8 20.8 %collective-permute-start.20 = (bf16[144,288]{1,0:T(8,128)(2,1)}, bf16[144,288]{1,0:T(8,128)(2,1)S(1)}, u32[]{:S(2)}, u32[]{:S(2)}) collective-permute-start(bf16[144,288]{1,0:T(8,128)(2,1)} %get-tuple-element.46), channel_id=1, source_target_pairs={{0,8},{4,12},{8,0},{12,4},{16,24},{20,28},{24,16},{28,20},{1,9},{5... | collective-permute-start | bytes 248840 | tf_op jit(solution)/shard_map/ppermute | solution.py:383
  57.8 24.5 %collective-permute-start.21 = (bf16[144,288]{1,0:T(8,128)(2,1)}, bf16[144,288]{1,0:T(8,128)(2,1)S(1)}, u32[]{:S(2)}, u32[]{:S(2)}) collective-permute-start(bf16[144,288]{1,0:T(8,128)(2,1)} %get-tuple-element.47), channel_id=1, source_target_pairs={{0,12},{4,8},{8,4},{12,0},{16,28},{20,24},{24,20},{28,16},{1,13},{... | collective-permute-start | bytes 248840 | tf_op jit(solution)/shard_map/ppermute | solution.py:383
  74.6 15.4 %collective-permute-start.22 = (bf16[144,288]{1,0:T(8,128)(2,1)S(1)}, bf16[144,288]{1,0:T(8,128)(2,1)S(1)}, u32[]{:S(2)}, u32[]{:S(2)}) collective-permute-start(bf16[144,288]{1,0:T(8,128)(2,1)S(1)} %copy-done.21), channel_id=1, source_target_pairs={{0,16},{4,20},{8,24},{12,28},{16,0},{20,4},{24,8},{28,12},{1,17},{... | collective-permute-start | bytes 248840 | tf_op jit(solution)/shard_map/ppermute | solution.py:383
  76.9 16.5 %collective-permute-start.23 = (bf16[144,288]{1,0:T(8,128)(2,1)S(1)}, bf16[144,288]{1,0:T(8,128)(2,1)S(1)}, u32[]{:S(2)}, u32[]{:S(2)}) collective-permute-start(bf16[144,288]{1,0:T(8,128)(2,1)S(1)} %copy-done.20), channel_id=1, source_target_pairs={{0,20},{4,16},{8,28},{12,24},{16,4},{20,0},{24,12},{28,8},{1,21},{... | collective-permute-start | bytes 248840 | tf_op jit(solution)/shard_map/ppermute | solution.py:383
  78.6 14.9 %collective-permute-start.24 = (bf16[144,288]{1,0:T(8,128)(2,1)S(1)}, bf16[144,288]{1,0:T(8,128)(2,1)S(1)}, u32[]{:S(2)}, u32[]{:S(2)}) collective-permute-start(bf16[144,288]{1,0:T(8,128)(2,1)S(1)} %copy-done.19), channel_id=1, source_target_pairs={{0,24},{4,28},{8,16},{12,20},{16,8},{20,12},{24,0},{28,4},{1,25},{... | collective-permute-start | bytes 248840 | tf_op jit(solution)/shard_map/ppermute | solution.py:383
  82.2 11.3 %collective-permute-start.25 = (bf16[144,288]{1,0:T(8,128)(2,1)S(1)}, bf16[144,288]{1,0:T(8,128)(2,1)S(1)}, u32[]{:S(2)}, u32[]{:S(2)}) collective-permute-start(bf16[144,288]{1,0:T(8,128)(2,1)S(1)} %copy-done.18), channel_id=1, source_target_pairs={{0,28},{4,24},{8,20},{12,16},{16,12},{20,8},{24,4},{28,0},{1,29},{... | collective-permute-start | bytes 248840 | tf_op jit(solution)/shard_map/ppermute | solution.py:383
  82.4 13.8 %collective-permute-start.17 = (bf16[128,1152]{1,0:T(8,128)(2,1)}, bf16[128,1152]{1,0:T(8,128)(2,1)S(1)}, u32[]{:S(2)}, u32[]{:S(2)}) collective-permute-start(bf16[128,1152]{1,0:T(8,128)(2,1)} %get-tuple-element.42), channel_id=1, source_target_pairs={{0,1},{1,0},{2,3},{3,2},{4,5},{5,4},{6,7},{7,6},{8,9},{9,8},{10,11... | collective-permute-start | bytes 884744 | tf_op jit(solution)/shard_map/ppermute | solution.py:383
  90.0 27.8 %collective-permute-start.16 = (bf16[128,1152]{1,0:T(8,128)(2,1)}, bf16[128,1152]{1,0:T(8,128)(2,1)S(1)}, u32[]{:S(2)}, u32[]{:S(2)}) collective-permute-start(bf16[128,1152]{1,0:T(8,128)(2,1)} %get-tuple-element.40), channel_id=1, source_target_pairs={{0,1},{1,0},{2,3},{3,2},{4,5},{5,4},{6,7},{7,6},{8,9},{9,8},{10,11... | collective-permute-start | bytes 884744 | tf_op jit(solution)/shard_map/ppermute | solution.py:383
  96.2 21.6 %collective-permute-start.18 = (bf16[128,1152]{1,0:T(8,128)(2,1)S(1)}, bf16[128,1152]{1,0:T(8,128)(2,1)S(1)}, u32[]{:S(2)}, u32[]{:S(2)}) collective-permute-start(bf16[128,1152]{1,0:T(8,128)(2,1)S(1)} %add_convert_fusion), channel_id=1, source_target_pairs={{0,2},{1,3},{2,0},{3,1},{4,6},{5,7},{6,4},{7,5},{8,10},{9,11},{10,... | collective-permute-start | bytes 884744 | tf_op jit(solution)/shard_map/ppermute | solution.py:383
  99.5 7.6 %collective-permute-start.34 = (f32[4]{0:T(128)S(1)}, f32[4]{0:T(128)S(1)}, u32[]{:S(2)}, u32[]{:S(2)}) collective-permute-start(f32[4]{0:T(128)S(1)} %get-tuple-element.55), channel_id=1, source_target_pairs={{0,28},{4,24},{8,20},{12,16},{16,12},{20,8},{24,4},{28,0},{1,29},{... | collective-permute-start | bytes 56 | tf_op jit(solution)/shard_map/ppermute | solution.py:383
  108.0 6.8 %collective-permute-start.31 = (f32[4]{0:T(128)S(1)}, f32[4]{0:T(128)S(1)}, u32[]{:S(2)}, u32[]{:S(2)}) collective-permute-start(f32[4]{0:T(128)S(1)} %get-tuple-element.58), channel_id=1, source_target_pairs={{0,16},{4,20},{8,24},{12,28},{16,0},{20,4},{24,8},{28,12},{1,17},{... | collective-permute-start | bytes 56 | tf_op jit(solution)/shard_map/ppermute | solution.py:383
  (33 other events, 274.2 us)

commit v2 on v1

v2 whole, which is shorter than its diff:
```python
from functools import partial
import math

import jax
import jax.numpy as jnp
from jax import lax
from jax.experimental import pallas as pl
from jax.experimental.pallas import tpu as pltpu
from jax.sharding import PartitionSpec as P

HEAD_DIM = 72
LANES = 128
EMB = 128
QTOK = 32
MP = 4
SCALE = HEAD_DIM ** (-0.5)
LOG2E = math.log2(math.e)
F32 = jnp.float32
BF16 = jnp.bfloat16

VMEM = pl.BlockSpec(memory_space=pltpu.VMEM)
SMEM = pl.BlockSpec(memory_space=pltpu.SMEM)
HBM = pl.BlockSpec(memory_space=pl.ANY)


def dot(left, right, left_dim, right_dim):
    return lax.dot_general(
        left, right, (((left_dim,), (right_dim,)), ((), ())), preferred_element_type=F32
    )


def shape(dims, kind):
    return jax.ShapeDtypeStruct(dims, kind)


def cost(flops, size, exps=0):
    return pl.CostEstimate(flops=int(flops), bytes_accessed=int(size), transcendentals=int(exps))


def grant(mebibytes):
    return pltpu.CompilerParams(vmem_limit_bytes=mebibytes * 1024 * 1024)


def full(*dims):
    return pl.BlockSpec(dims, lambda *_: (0,) * len(dims))


def unit_rows(values):
    return values * lax.rsqrt(jnp.sum(values * values, axis=-1, keepdims=True) + 1e-06)


def place_of(index, model_index, rows_dev):
    return (model_index ^ (index // rows_dev)) * rows_dev + index % rows_dev


def prepare_kernel(heads, mixing_ref, output_ref, tokens_ref, mixing_pad, output_pad, unit_ref):
    def spread(source, target, index):
        target[index * LANES : index * LANES + HEAD_DIM, :] = source[
            index * HEAD_DIM : (index + 1) * HEAD_DIM, :
        ]
        target[index * LANES + HEAD_DIM : (index + 1) * LANES, :] = jnp.zeros(
            (LANES - HEAD_DIM, target.shape[1]), BF16
        )

    values = tokens_ref[...].astype(F32)
    unit_ref[...] = unit_rows(values).astype(BF16)
    for index in range(3 * heads):
        spread(mixing_ref, mixing_pad, index)
    for index in range(heads):
        spread(output_ref, output_pad, index)


def prepare(mixing, output, tokens, heads):
    width = mixing.shape[1]
    return pl.pallas_call(
        partial(prepare_kernel, heads),
        out_shape=(
            shape((3 * heads * LANES, width), BF16),
            shape((heads * LANES, width), BF16),
            shape(tokens.shape, BF16),
        ),
        in_specs=[VMEM] * 3,
        out_specs=(VMEM,) * 3,
        cost_estimate=cost(0, 8e6),
        name="prepare",
        compiler_params=grant(24),
    )(mixing, output, tokens)


def hand_out(product, keep0, keep2, send):
    size = keep0.shape[0]
    keep0[...] = product[:size].astype(BF16)
    send[:size, :] = product[size : 2 * size].astype(BF16)
    keep2[...] = product[2 * size : 3 * size].astype(BF16)
    send[size:, :] = product[3 * size :].astype(BF16)


def forward_kernel(
    heads,
    rows_dev,
    counts_ref,
    rows0,
    rows1,
    rows2,
    rows3,
    gain_ref,
    mixing_ref,
    output_ref,
    packed_ref,
    prob_ref,
    attended_ref,
    keep0,
    keep2,
    send,
    normed,
):
    head = pl.program_id(0)
    rows = rows_dev * MP

    @pl.when(head == 0)
    def _():
        for index, block in enumerate((rows0, rows1, rows2, rows3)):
            values = block[...].astype(F32)
            center = values - jnp.mean(values, axis=-1, keepdims=True)
            spread = jnp.mean(center * center, axis=-1, keepdims=True)
            normed[index * rows_dev : (index + 1) * rows_dev, :] = (
                center * lax.rsqrt(spread + 1e-06) * gain_ref[...]
            ).astype(BF16)

    packed = dot(normed[...], mixing_ref[...], 1, 1).astype(BF16)
    packed_ref[...] = packed
    query = packed[:, :LANES]
    key = packed[:, LANES : 2 * LANES]
    value = packed[:, 2 * LANES :]
    count = counts_ref[lax.axis_index("dp")]
    model_index = lax.axis_index("mp")
    columns = lax.broadcasted_iota(jnp.int32, (1, rows), 1)
    seen = place_of(columns, model_index, rows_dev) < count
    step = rows_dev
    for chunk in range(rows // step):
        low = chunk * step
        score = dot(query[low : low + step], key, 1, 1)
        score = jnp.where(seen, score, -1e30)
        largest = jnp.max(score, axis=-1, keepdims=True)
        raised = jnp.exp2((score - largest) * (SCALE * LOG2E))
        total = jnp.sum(raised, axis=-1, keepdims=True)
        prob = (raised * (1.0 / total)).astype(BF16)
        prob_ref[0, low : low + step, :] = prob
        found = dot(prob, value, 1, 0)
        lines = lax.broadcasted_iota(jnp.int32, (step, 1), 0) + low
        live = place_of(lines, model_index, rows_dev) < count
        found = jnp.where(live, found, 0.0).astype(BF16)
        attended_ref[head, low : low + step, :] = found

    @pl.when(head == heads - 1)
    def _():
        joined = jnp.concatenate([attended_ref[index] for index in range(heads)], axis=1)
        hand_out(dot(joined, output_ref[...], 1, 0), keep0, keep2, send)


def handed_shapes(rows_dev, width):
    kept = shape((rows_dev, width), BF16)
    return (kept, kept, shape((2 * rows_dev, width), BF16))


def forward(counts, blocks, gain, mixing_pad, output_pad, heads):
    rows_dev, width = blocks[0].shape
    rows = rows_dev * MP
    wide = 3 * LANES
    block = full(rows_dev, width)
    return pl.pallas_call(
        partial(forward_kernel, heads, rows_dev),
        grid=(heads,),
        out_shape=(
            shape((rows, heads * wide), BF16),
            shape((heads, rows, rows), BF16),
            shape((heads, rows, LANES), BF16),
        )
        + handed_shapes(rows_dev, width),
        in_specs=[SMEM]
        + [block] * MP
        + [
            full(1, width),
            pl.BlockSpec((wide, width), lambda head: (head, 0)),
            full(heads * LANES, width),
        ],
        out_specs=(
            pl.BlockSpec((rows, wide), lambda head: (0, head)),
            pl.BlockSpec((1, rows, rows), lambda head: (head, 0, 0)),
            full(heads, rows, LANES),
        )
        + (block, block, full(2 * rows_dev, width)),
        scratch_shapes=[pltpu.VMEM((rows, width), BF16)],
        cost_estimate=cost(3e9, 12e6, heads * rows * rows),
        name="forward_attention",
        compiler_params=grant(24),
    )(counts, *blocks, gain, mixing_pad, output_pad)


def weight_kernel(heads, rows_dev, order, grad0, grad1, grad2, grad3, attended_ref, *refs):
    outs, (stacked, result) = refs[: len(refs) - 2], refs[len(refs) - 2 :]
    for index, block in enumerate((grad0, grad1, grad2, grad3)):
        stacked[index * rows_dev : (index + 1) * rows_dev, :] = block[...]
    joined = jnp.concatenate([attended_ref[index] for index in range(heads)], axis=1)
    product = dot(stacked[...], joined, 0, 0)
    for index in range(heads):
        result[:, index * HEAD_DIM : (index + 1) * HEAD_DIM] = product[
            :, index * LANES : index * LANES + HEAD_DIM
        ]
    if order is None:
        outs[0][...] = result[...]
    else:
        mine = lax.axis_index("dp")
        share = result.shape[0] // sum(len(group) for group in order)
        for group, out in zip(order, outs):
            for spot, piece in enumerate(group):
                start = pl.multiple_of((mine ^ piece) * share, 16)
                out[spot * share : (spot + 1) * share, :] = result[
                    pl.ds(start, share), :
                ].astype(out.dtype)


def weight_parts(grads, attended, order):
    rows_dev, width = grads[0].shape
    heads = attended.shape[0]
    narrow = heads * HEAD_DIM
    if order is None:
        outs = (shape((width, narrow), F32),)
    else:
        share = width // sum(len(group) for group in order)
        outs = tuple(
            shape((len(group) * share, narrow), F32 if index == 0 else BF16)
            for index, group in enumerate(order)
        )
    return pl.pallas_call(
        partial(weight_kernel, heads, rows_dev, order),
        out_shape=outs,
        in_specs=[VMEM] * (MP + 1),
        out_specs=(VMEM,) * len(outs),
        scratch_shapes=[
            pltpu.VMEM((rows_dev * MP, width), BF16),
            pltpu.VMEM((width, narrow), F32),
        ],
        cost_estimate=cost(7e8, 4e6),
        name="weight_parts",
        compiler_params=grant(20),
    )(*grads, attended)


def backward_kernel(
    heads,
    last,
    rows_dev,
    counts_ref,
    grad0,
    grad1,
    grad2,
    grad3,
    output_ref,
    packed_ref,
    prob_ref,
    *refs,
):
    head = pl.program_id(0)
    rows = rows_dev * MP
    if last:
        earlier, mixing_hbm, keep0, keep2, send, stacked, joined, mixing, sem = refs
        fetch = pltpu.make_async_copy(mixing_hbm, mixing, sem)
    else:
        joined, stacked = refs

    @pl.when(head == 0)
    def _():
        if last:
            fetch.start()
        for index, block in enumerate((grad0, grad1, grad2, grad3)):
            stacked[index * rows_dev : (index + 1) * rows_dev, :] = block[...]

    count = counts_ref[lax.axis_index("dp")]
    model_index = lax.axis_index("mp")
    lines = lax.broadcasted_iota(jnp.int32, (rows, 1), 0)
    live = place_of(lines, model_index, rows_dev) < count
    flow = dot(stacked[...], output_ref[...], 1, 1)
    flow = jnp.where(live, flow, 0.0).astype(BF16)
    query = packed_ref[:, :LANES]
    key = packed_ref[:, LANES : 2 * LANES]
    value = packed_ref[:, 2 * LANES :]
    step = rows // 2
    grad_key = jnp.zeros((rows, LANES), F32)
    grad_value = jnp.zeros((rows, LANES), F32)
    grad_query = []
    for low in range(0, rows, step):
        part = flow[low : low + step]
        weights = prob_ref[0, low : low + step, :]
        prob = weights.astype(F32)
        grad_prob = dot(part, value, 1, 1)
        delta = jnp.sum(grad_prob * prob, axis=-1, keepdims=True)
        grad_score = (prob * (grad_prob - delta)).astype(BF16)
        grad_query.append((dot(grad_score, key, 1, 0) * SCALE).astype(BF16))
        grad_key += dot(grad_score, query[low : low + step], 0, 0)
        grad_value += dot(weights, part, 0, 0)
    joined[head, :, :LANES] = jnp.concatenate(grad_query, axis=0)
    joined[head, :, LANES : 2 * LANES] = (grad_key * SCALE).astype(BF16)
    joined[head, :, 2 * LANES :] = grad_value.astype(BF16)

    if last:

        @pl.when(head == heads - 1)
        def _():
            fetch.wait()
            pieces = [earlier[index] for index in range(earlier.shape[0])]
            pieces += [joined[index] for index in range(heads)]
            everything = jnp.concatenate(pieces, axis=1)
            hand_out(dot(everything, mixing[...], 1, 0), keep0, keep2, send)


def backward(counts, grads, output_pad, packed, probs, first, heads, rest=()):
    rows_dev, width = grads[0].shape
    rows = rows_dev * MP
    wide = 3 * LANES
    block = full(rows_dev, width)
    stacked = pltpu.VMEM((rows, width), BF16)
    if rest:
        earlier, mixing_pad = rest
        out_shape = handed_shapes(rows_dev, width)
        more_specs = [full(*earlier.shape), HBM]
        out_specs = (block, block, full(2 * rows_dev, width))
        scratch = [
            stacked,
            pltpu.VMEM((heads, rows, wide), BF16),
            pltpu.VMEM(mixing_pad.shape, BF16),
            pltpu.SemaphoreType.DMA,
        ]
    else:
        out_shape = shape((heads, rows, wide), BF16)
        more_specs = []
        out_specs = full(heads, rows, wide)
        scratch = [stacked]
    return pl.pallas_call(
        partial(backward_kernel, heads, bool(rest), rows_dev),
        grid=(heads,),
        out_shape=out_shape,
        in_specs=[SMEM]
        + [block] * MP
        + [
            pl.BlockSpec((LANES, width), lambda head: (head + first, 0)),
            pl.BlockSpec((rows, wide), lambda head: (0, head + first)),
            pl.BlockSpec((1, rows, rows), lambda head: (head + first, 0, 0)),
        ]
        + more_specs,
        out_specs=out_specs,
        scratch_shapes=scratch,
        cost_estimate=cost(3e9, 6e6),
        name="backward_attention",
        compiler_params=grant(24),
    )(counts, *grads, output_pad, packed, probs, *rest)


def score_kernel(
    rows_dev, few, counts_ref, patch_ref, part_ref, near_ref, far_ref, embed_ref, tokens_ref,
    hidden_ref, best_ref, page_emb
):
    mine = lax.axis_index("dp")

    @pl.when(pl.program_id(0) == 0)
    def _():
        mixed = part_ref[...].astype(F32) + near_ref[...].astype(F32) + far_ref[...].astype(F32)
        hidden = (patch_ref[...].astype(F32) + mixed).astype(BF16)
        hidden_ref[...] = hidden
        embedded = dot(hidden, embed_ref[...], 1, 0)
        page_emb[...] = unit_rows(embedded).astype(BF16)

    similar = dot(page_emb[...], tokens_ref[...], 1, 1)
    lines = lax.broadcasted_iota(jnp.int32, (rows_dev, 1), 0) + lax.axis_index("mp") * rows_dev
    similar = jnp.where(lines < counts_ref[mine], similar, -2.0)
    best = jnp.max(similar, axis=0, keepdims=True)
    if few:
        size = best_ref.shape[1]
        for piece in range(best.shape[1] // size):
            row = best[:, piece * size : (piece + 1) * size]
            for copy in range(MP):
                best_ref[pl.ds((mine ^ piece) * MP + copy, 1), :] = row
    else:
        best_ref[...] = best


def hidden_and_best(counts, patches, part, received, far, embed_weight, tokens, few, local):
    rows_dev, width = patches.shape
    size = tokens.shape[0]
    chunk = size if few else math.gcd(size, 1024)
    block = full(rows_dev, width)
    if few:
        best_shape, best_spec = shape((size // local * MP, local), F32), full(size // local * MP, local)
    else:
        best_shape, best_spec = shape((1, size), F32), pl.BlockSpec((1, chunk), lambda index: (0, index))
    return pl.pallas_call(
        partial(score_kernel, rows_dev, few),
        grid=(size // chunk,),
        out_shape=(shape((rows_dev, width), BF16), best_shape),
        in_specs=[SMEM]
        + [block] * 4
        + [full(width, EMB), pl.BlockSpec((chunk, EMB), lambda index: (index, 0))],
        out_specs=(block, best_spec),
        scratch_shapes=[pltpu.VMEM((rows_dev, EMB), BF16)],
        cost_estimate=cost(1e8, 2e6),
        name="hidden_and_best",
        compiler_params=grant(12),
    )(counts, patches, part, received, far, embed_weight, tokens)


def page_score_kernel(found_ref, score_ref):
    pages = found_ref.shape[0] // MP
    best = jnp.max(found_ref[...].reshape(pages, MP, found_ref.shape[1]), axis=1)
    turned = best.T
    for query in range(score_ref.shape[0]):
        score_ref[query : query + 1, :] = jnp.sum(
            turned[query * QTOK : (query + 1) * QTOK], axis=0, keepdims=True
        )


def page_scores(found):
    return pl.pallas_call(
        page_score_kernel,
        out_shape=shape((found.shape[1] // QTOK, found.shape[0] // MP), F32),
        in_specs=[VMEM],
        out_specs=VMEM,
        name="page_scores",
        compiler_params=grant(4),
    )(found)


def norm_back_kernel(patch_ref, gain_ref, grad_ref, part_ref, near_ref, far_ref, out_ref):
    values = patch_ref[...].astype(F32)
    center = values - jnp.mean(values, axis=-1, keepdims=True)
    spread = jnp.mean(center * center, axis=-1, keepdims=True)
    inverse = lax.rsqrt(spread + 1e-06)
    flow = part_ref[...].astype(F32) + near_ref[...].astype(F32) + far_ref[...].astype(F32)
    flow = flow * gain_ref[...]
    along = jnp.mean(flow * center, axis=-1, keepdims=True)
    level = jnp.mean(flow, axis=-1, keepdims=True)
    result = inverse * (flow - level - center * (inverse * inverse * along))
    out_ref[...] = (grad_ref[...].astype(F32) + result).astype(BF16)


def norm_back(patches, gain, grads, part, near, far):
    block = full(*patches.shape)
    return pl.pallas_call(
        norm_back_kernel,
        grid=(1,),
        out_shape=shape(patches.shape, BF16),
        in_specs=[block, full(*gain.shape), block, block, block, block],
        out_specs=block,
        cost_estimate=cost(3e6, 2e6),
        name="norm_back",
        compiler_params=grant(12),
    )(patches, gain, grads, part, near, far)


def swap(values, axis, distance):
    size = lax.axis_size(axis)
    return lax.ppermute(values, axis, [(index, index ^ distance) for index in range(size)])


def scatter_sum(parts):
    part0, part2, send = parts
    received = swap(send, "mp", 1)
    relayed = received[part2.shape[0] :]
    far = swap((part2.astype(F32) + relayed.astype(F32)).astype(BF16), "mp", 2)
    return part0, received, far


def after(values, *others):
    return lax.optimization_barrier((values, *others))[0]


def body(
    patches,
    norm_gain,
    query_key_value,
    output_weight,
    embed_weight,
    query_tokens,
    patch_counts,
    positive_page,
    hidden_grad,
):
    data_index = lax.axis_index("dp")
    data_size = lax.axis_size("dp")
    few = data_size == 8
    heads = output_weight.shape[1] // HEAD_DIM
    gain = norm_gain.reshape(1, -1)

    rows2 = swap(patches, "mp", 2)
    rows1 = swap(patches, "mp", 1)
    grads2 = swap(hidden_grad, "mp", 2)
    grads1 = swap(hidden_grad, "mp", 1)

    local = query_tokens.shape[0]
    mixing_pad, output_pad, query_emb = prepare(
        query_key_value.T, output_weight.T, query_tokens.reshape(local * QTOK, EMB), heads
    )
    rows3 = swap(after(rows2, query_emb), "mp", 1)
    if few:
        tokens = query_emb
        for distance in (1, 2, 4):
            tokens = jnp.concatenate([tokens, swap(tokens, "dp", distance)], axis=0)
    else:
        tokens = lax.all_gather(query_emb, "dp", axis=0, tiled=True)

    packed, probs, attended, *parts = forward(
        patch_counts, (patches, rows1, rows2, rows3), gain, mixing_pad, output_pad, heads
    )
    grads3 = swap(after(grads2, rows3), "mp", 1)
    grads = (hidden_grad, grads1, grads2, grads3)
    part, received, far = scatter_sum(parts)
    half = heads // 2
    common = (patch_counts, grads, output_pad, packed, probs)
    if few:
        order = ((0, 4), (2, 6), (1, 5, 3, 7))
        kept, second, first = weight_parts(grads, after(attended, received), order)
        got1 = swap(first, "dp", 1).astype(F32)
        earlier = backward(*common[:4], after(probs, kept), 0, half)
        tokens = after(tokens, earlier)
    else:
        (whole,) = weight_parts(grads, attended, None)
        weight_grad = lax.psum_scatter(whole, "dp", scatter_dimension=0, tiled=True)
        earlier = backward(*common, 0, half)
    hidden, best = hidden_and_best(
        patch_counts, patches, part, received, far, embed_weight, tokens, few, local * QTOK
    )
    if few:
        middle = kept.shape[0]
        share = middle // 2
        going = (second.astype(F32) + got1[middle:]).astype(BF16)
        got2 = swap(going, "dp", 2).astype(F32)
        earlier = after(earlier, best, going)
    grad_parts = backward(*common, half, heads - half, (earlier, mixing_pad))
    part, received, far = scatter_sum(grad_parts)
    patch_grad = norm_back(patches, gain, hidden_grad, part, received, far)
    if few:
        kept = kept + got1[:middle] + got2
        weight_grad = kept[:share] + swap(kept[share:].astype(BF16), "dp", 4).astype(F32)
        my_scores = page_scores(lax.all_to_all(best, ("dp", "mp"), 0, 0, tiled=True))
    else:
        best = jnp.maximum(best, swap(best, "mp", 1))
        best = jnp.maximum(best, swap(best, "mp", 2))
        part_scores = jnp.sum(best.reshape(-1, QTOK), axis=1)
        every = lax.all_gather(part_scores.reshape(-1, 1), "dp", axis=1, tiled=True)
        my_scores = lax.dynamic_slice_in_dim(every, data_index * local, local, 0)
    columns = jnp.arange(my_scores.shape[1], dtype=jnp.int32)
    chosen = columns[None, :] == positive_page[:, None]
    positive_score = jnp.sum(jnp.where(chosen, my_scores, 0.0), axis=1)
    negative_score = jnp.max(jnp.where(chosen, -1e30, my_scores), axis=1)
    loss = jax.nn.softplus(negative_score - positive_score)
    return (hidden, patch_grad, weight_grad, my_scores, loss)


def solution(mesh):
    return jax.shard_map(
        body,
        mesh=mesh,
        in_specs=(
            P(("dp", "mp"), None),
            P(),
            P(None, "mp"),
            P(None, "mp"),
            P(),
            P("dp", None, None),
            P(),
            P("dp"),
            P(("dp", "mp"), None),
        ),
        out_specs=(
            P(("dp", "mp"), None),
            P(("dp", "mp"), None),
            P("dp", "mp"),
            P("dp", None),
            P("dp"),
        ),
        check_vma=False,
    )
```

time: 122 us -> 82.4 us (0.68)
  starting transfers between devices: 46.1 us -> 17.3 us
  Pallas kernels: 44.7 us -> 27.9 us
  blocking collectives: 0 us -> 10.4 us
  waiting for transfers between devices: 12.5 us -> 19.8 us
  local copies, waits for them, and re-layouts: 10.3 us -> 3.45 us
  other arithmetic: 6.61 us -> 2.51 us
    ppermute x35 -> x16, starting transfers between devices: 46.1 us -> 17.3 us  [swap(): lax.ppermute(values, axis, [(index, index ^ distance) for index in range(...]
    pallas_call x5 -> x7, Pallas kernels: 29.3 us -> 15.9 us  [the longest x2 11.1 us: backward(): pl.pallas_call(partial(backward_kernel, heads, bool(rest), rows_dev), gri...]
    all_to_all x0 -> x1, blocking collectives: none -> 10.4 us  [body(): lax.all_to_all(best, ('dp', 'mp'), 0, 0, tiled=True)]
    ppermute x35 -> x16, waiting for transfers between devices: 12.5 us -> 19.8 us  [swap(): lax.ppermute(values, axis, [(index, index ^ distance) for index in range(...]
    unnamed x53 -> x18, local copies, waits for them, and re-layouts: 8.12 us -> 3.43 us
    pallas_call x1, Pallas kernels: 15.4 us -> 11.9 us  [forward(): pl.pallas_call(partial(forward_kernel, heads, rows_dev), grid=(heads,), o...]
    dynamic_slice x1 -> x0, local copies, waits for them, and re-layouts: 1.31 us -> none  [body(): lax.dynamic_index_in_dim(patch_counts, data_index, 0, keepdims=False)]
    another operation x1 -> x0, other arithmetic: 1.29 us -> none  [body(): where = jnp.stack([count, model_index, data_index]).astype(jnp.int32)]
  transfers between devices with their start and end apart: 35 -> 16, of which waited for: 8 -> 9; matrix products, arithmetic and copies ran while one was open for 12% -> 3% of each run, Pallas kernels for 35% -> 10%
where the time goes in v2:
time: 82.4 us; the launch traced here: 82.1 us
  Pallas kernels  27.9 us (34%)
  waiting for transfers between devices  19.8 us (24%)
  starting transfers between devices  17.3 us (21%)
  blocking collectives  10.4 us (13%)
  local copies, waits for them, and re-layouts  3.45 us (4%)
  other arithmetic  2.51 us (3%)
    ppermute x16, waiting for transfers between devices, swap(): lax.ppermute(values, axis, [(index, index ^ distance) for index in range(...  19.8 us
    ppermute x16, starting transfers between devices, swap(): lax.ppermute(values, axis, [(index, index ^ distance) for index in range(...  17.3 us
    pallas_call x1, Pallas kernels, forward(): pl.pallas_call(partial(forward_kernel, heads, rows_dev), grid=(heads,), o...  11.9 us
    pallas_call x2, Pallas kernels, backward(): pl.pallas_call(partial(backward_kernel, heads, bool(rest), rows_dev), gri...  11.1 us
    all_to_all x1, blocking collectives, body(): lax.all_to_all(best, ('dp', 'mp'), 0, 0, tiled=True)  10.4 us
    unnamed x18, local copies, waits for them, and re-layouts  3.43 us
  transfers between devices with their start and end apart: 16, of which 9 were waited for; matrix products, arithmetic and copies ran while one was open for 3% of the time, Pallas kernels for 10%

profile of v2, /device:TPU:0, one launch (start us, length us, event | category | flops | bytes accessed | tf_op | source)
XLA Modules:
  0.0 82.1 jit_solution(4650607060992185393)
XLA Ops:
  0.6 3.0 %collective-permute-start.1 = (bf16[128,1152]{1,0:T(8,128)(2,1)}, bf16[128,1152]{1,0:T(8,128)(2,1)S(1)}, u32[]{:S(2)}, u32[]{:S(2)}) collective-permute-start(bf16[128,1152]{1,0:T(8,128)(2,1)} %patch_ref.3), channel_id=1, source_target_pairs={{0,2},{1,3},{2,0},{3,1},{4,6},{5,7},{6,4},{7,5},{8,10},{9,11},{10,... | collective-permute-start | bytes 884744 | tf_op jit(solution)/shard_map/ppermute | solution.py:461
  3.7 1.6 %copy-done = bf16[1152,864]{0,1:T(8,128)(2,1)S(1)} copy-done((bf16[1152,864]{0,1:T(8,128)(2,1)S(1)}, bf16[1152,864]{0,1:T(8,128)(2,1)}, u32[]{:S(2)}) %copy-start) | copy-done | bytes 1990680
  5.2 1.1 %copy-done.2 = bf16[1152,288]{0,1:T(8,128)(2,1)S(1)} copy-done((bf16[1152,288]{0,1:T(8,128)(2,1)S(1)}, bf16[1152,288]{0,1:T(8,128)(2,1)}, u32[]{:S(2)}) %copy-start.2) | copy-done | bytes 663576
  6.3 0.8 copy-done.5
  7.4 3.5 %collective-permute-done.1.rows2 = bf16[128,1152]{1,0:T(8,128)(2,1)S(1)} collective-permute-done((bf16[128,1152]{1,0:T(8,128)(2,1)}, bf16[128,1152]{1,0:T(8,128)(2,1)S(1)}, u32[]{:S(2)}, u32[]{:S(2)}) %collective-permute-start.1) | collective-permute-done | bytes 294944 | tf_op jit(solution)/shard_map/ppermute | solution.py:461
  10.9 1.6 %collective-permute-done.2.rows3 = bf16[128,1152]{1,0:T(8,128)(2,1)S(1)} collective-permute-done((bf16[128,1152]{1,0:T(8,128)(2,1)S(1)}, bf16[128,1152]{1,0:T(8,128)(2,1)S(1)}, u32[]{:S(2)}, u32[]{:S(2)}) %collective-permute-start.2) | collective-permute-done | bytes 294944 | tf_op jit(solution)/shard_map/ppermute | solution.py:461
  12.5 11.9 %forward_attention.1 = (bf16[512,1536]{1,0:T(8,128)(2,1)S(1)}, bf16[4,512,512]{2,1,0:T(8,128)(2,1)S(1)}, bf16[4,512,128]{2,1,0:T(8,128)(2,1)S(1)}, bf16[128,1152...) custom-call(s32[8]{0:T(128)S(1)} %copy-done.6, bf16[128,1152]{1,0:T(8,128)(2,1)S(1)} %copy-done.1, ...), custom_call_target="tpu_custom_call" | custom-call | flops 3000000000 | bytes 12000000 | tf_op jit(solution)/shard_map/forward_attention/pallas_call | solution.py:171
  24.6 1.8 %collective-permute-start.5 = (bf16[128,128]{1,0:T(8,128)(2,1)S(1)}, bf16[128,128]{1,0:T(8,128)(2,1)S(1)}, u32[]{:S(2)}, u32[]{:S(2)}) collective-permute-start(bf16[128,128]{1,0:T(8,128)(2,1)S(1)} %get-tuple-element.28), channel_id=1, source_target_pairs={{0,4},{4,0},{8,12},{12,8},{16,20},{20,16},{24,28},{28,24},{1,5},{5... | collective-permute-start | bytes 98312 | tf_op jit(solution)/shard_map/ppermute | solution.py:461
  26.4 1.5 %collective-permute-start.9 = (bf16[128,1152]{1,0:T(8,128)(2,1)S(1)}, bf16[128,1152]{1,0:T(8,128)(2,1)S(1)}, u32[]{:S(2)}, u32[]{:S(2)}) collective-permute-start(bf16[128,1152]{1,0:T(8,128)(2,1)S(1)} %copy-done.3), channel_id=1, source_target_pairs={{0,2},{1,3},{2,0},{3,1},{4,6},{5,7},{6,4},{7,5},{8,10},{9,11},{10,... | collective-permute-start | bytes 884744 | tf_op jit(solution)/shard_map/ppermute | solution.py:461
  28.5 1.8 %collective-permute-start.6 = (bf16[256,128]{1,0:T(8,128)(2,1)S(1)}, bf16[256,128]{1,0:T(8,128)(2,1)S(1)}, u32[]{:S(2)}, u32[]{:S(2)}) collective-permute-start(bf16[256,128]{1,0:T(8,128)(2,1)S(1)} %pad_maximum_fusion.2), channel_id=1, source_target_pairs={{0,8},{4,12},{8,0},{12,4},{16,24},{20,28},{24,16},{28,20},{1,9},{5... | collective-permute-start | bytes 196616 | tf_op jit(solution)/shard_map/ppermute | solution.py:461
  30.4 2.4 %collective-permute-done.6 = bf16[256,128]{1,0:T(8,128)(2,1)S(1)} collective-permute-done((bf16[256,128]{1,0:T(8,128)(2,1)S(1)}, bf16[256,128]{1,0:T(8,128)(2,1)S(1)}, u32[]{:S(2)}, u32[]{:S(2)}) %collective-permute-start.6) | collective-permute-done | bytes 65568 | tf_op jit(solution)/shard_map/ppermute | solution.py:461
  32.8 2.9 %collective-permute-start.7 = (bf16[512,128]{1,0:T(8,128)(2,1)S(1)}, bf16[512,128]{1,0:T(8,128)(2,1)S(1)}, u32[]{:S(2)}, u32[]{:S(2)}) collective-permute-start(bf16[512,128]{1,0:T(8,128)(2,1)S(1)} %pad_maximum_fusion.1), channel_id=1, source_target_pairs={{0,16},{4,20},{8,24},{12,28},{16,0},{20,4},{24,8},{28,12},{1,17},{... | collective-permute-start | bytes 393224 | tf_op jit(solution)/shard_map/ppermute | solution.py:461
  35.8 1.6 %collective-permute-start.4 = (bf16[128,1152]{1,0:T(8,128)(2,1)S(1)}, bf16[128,1152]{1,0:T(8,128)(2,1)S(1)}, u32[]{:S(2)}, u32[]{:S(2)}) collective-permute-start(bf16[128,1152]{1,0:T(8,128)(2,1)S(1)} %add_convert_fusion.1), channel_id=1, source_target_pairs={{0,2},{1,3},{2,0},{3,1},{4,6},{5,7},{6,4},{7,5},{8,10},{9,11},{10,... | collective-permute-start | bytes 884744 | tf_op jit(solution)/shard_map/ppermute | solution.py:461
  37.4 1.2 %weight_parts.1 = (f32[288,288]{1,0:T(8,128)S(1)}, bf16[288,288]{1,0:T(8,128)(2,1)S(1)}, bf16[576,288]{1,0:T(8,128)(2,1)S(1)}) custom-call(bf16[128,1152]{1,0:T(8,128)(2,1)S(1)} %copy-done.3, bf16[128,1152]{1,0:T(8,128)(2,1)S(1)} %collective-permute-done.8.grad1, bf16[128,1152]{1,0:T(8,128)(2,1)S(1)} %collective-permute-done.9.grad2, ...), custom_call_target="tpu_custom_call" | custom-call | flops 700000000 | bytes 4000000 | tf_op jit(solution)/shard_map/weight_parts/pallas_call | solution.py:235
  38.5 1.6 %collective-permute-start.11 = (bf16[576,288]{1,0:T(8,128)(2,1)S(1)}, bf16[576,288]{1,0:T(8,128)(2,1)S(1)}, u32[]{:S(2)}, u32[]{:S(2)}) collective-permute-start(bf16[576,288]{1,0:T(8,128)(2,1)S(1)} %get-tuple-element.46), channel_id=1, source_target_pairs={{0,4},{4,0},{8,12},{12,8},{16,20},{20,16},{24,28},{28,24},{1,5},{5... | collective-permute-start | bytes 995336 | tf_op jit(solution)/shard_map/ppermute | solution.py:461
  40.6 4.2 %backward_attention.2.refs_0_ = bf16[2,512,384]{2,1,0:T(8,128)(2,1)S(1)} custom-call(s32[8]{0:T(128)S(1)} %copy-done.6, bf16[128,1152]{1,0:T(8,128)(2,1)S(1)} %copy-done.3, bf16[128,1152]{1,0:T(8,128)(2,1)S(1)} %collective-permute-done.8.grad1, bf16[128,1152]{1,0:T(8,128)(2,1)S(1)} %collective-permute-done.9.grad2, ...), custom_call_target="tpu_custom_call" | custom-call | flops 3000000000 | bytes 6000000 | tf_op jit(solution)/shard_map/backward_attention/pallas_call | solution.py:339
  45.3 1.4 %hidden_and_best.1 = (bf16[128,1152]{1,0:T(8,128)(2,1)}, f32[32,128]{1,0:T(8,128)S(1)}) custom-call(s32[8]{0:T(128)S(1)} %copy-done.6, bf16[128,1152]{1,0:T(8,128)(2,1)S(1)} %copy-done.1, bf16[128,1152]{1,0:T(8,128)(2,1)S(1)} %get-tuple-element.32.part_ref, bf16[256,1152]{1,0:T(8,128)(2,1)S(1)} %collective-permute-done.3.near_ref, ...), custom_call_target="tpu_custom_call" | custom-call | flops 100000000 | bytes 2000000 | tf_op jit(solution)/shard_map/hidden_and_best/pallas_call | solution.py:396
  46.7 4.2 %collective-permute-done.11 = bf16[576,288]{1,0:T(8,128)(2,1)S(1)} collective-permute-done((bf16[576,288]{1,0:T(8,128)(2,1)S(1)}, bf16[576,288]{1,0:T(8,128)(2,1)S(1)}, u32[]{:S(2)}, u32[]{:S(2)}) %collective-permute-start.11) | collective-permute-done | bytes 331808 | tf_op jit(solution)/shard_map/ppermute | solution.py:461
  51.0 6.9 %backward_attention.3 = (bf16[128,1152]{1,0:T(8,128)(2,1)S(1)}, bf16[128,1152]{1,0:T(8,128)(2,1)S(1)}, bf16[256,1152]{1,0:T(8,128)(2,1)S(1)}) custom-call(s32[8]{0:T(128)S(1)} %copy-done.6, bf16[128,1152]{1,0:T(8,128)(2,1)S(1)} %copy-done.3, bf16[128,1152]{1,0:T(8,128)(2,1)S(1)} %collective-permute-done.8.grad1, ...), custom_call_target="tpu_custom_call" | custom-call | flops 3000000000 | bytes 6000000 | tf_op jit(solution)/shard_map/backward_attention/pallas_call | solution.py:339
  58.0 1.6 %collective-permute-start.14 = (bf16[288,288]{1,0:T(8,128)(2,1)S(1)}, bf16[288,288]{1,0:T(8,128)(2,1)S(1)}, u32[]{:S(2)}, u32[]{:S(2)}) collective-permute-start(bf16[288,288]{1,0:T(8,128)(2,1)S(1)} %fusion.1), channel_id=1, source_target_pairs={{0,8},{4,12},{8,0},{12,4},{16,24},{20,28},{24,16},{28,20},{1,9},{5... | collective-permute-start | bytes 497672 | tf_op jit(solution)/shard_map/ppermute | solution.py:461
  59.6 10.4 %all_to_all.11 = f32[32,1,128]{2,1,0:T(1,128)S(1)} all-to-all(f32[32,1,128]{2,1,0:T(1,128)S(1)} %bitcast.11), channel_id=1, replica_groups=mesh['dp'=8,'mp'=4] {'dp','mp'}, dimensions={0} | all-to-all | bytes 32768 | tf_op jit(solution)/shard_map/all_to_all | solution.py:543
  70.7 0.9 %select_reduce_fusion = (f32[4]{0:T(128)S(1)}, f32[4]{0:T(128)S(1)}) fusion(f32[4,8]{1,0:T(4,128)} %page_scores.1, s32[4]{0:T(128)S(1)} %copy-done.8), kind=kLoop, calls=%fused_computation.12 | loop fusion | flops 152 | bytes 176 | tf_op jit(solution)/shard_map/reduce_sum | solution.py:552
  73.6 6.2 %collective-permute-done.15 = bf16[144,288]{1,0:T(8,128)(2,1)S(1)} collective-permute-done((bf16[144,288]{1,0:T(8,128)(2,1)S(1)}, bf16[144,288]{1,0:T(8,128)(2,1)S(1)}, u32[]{:S(2)}, u32[]{:S(2)}) %collective-permute-start.15) | collective-permute-done | bytes 82976 | tf_op jit(solution)/shard_map/ppermute | solution.py:461
  80.9 1.2 %norm_back.1 = bf16[128,1152]{1,0:T(8,128)(2,1)} custom-call(bf16[128,1152]{1,0:T(8,128)(2,1)S(1)} %copy-done.1, f32[1,1152]{1,0:T(1,128)S(1)} %reshape.20.gain_ref, bf16[128,1152]{1,0:T(8,128)(2,1)S(1)} %copy-done.3, bf16[128,1152]{1,0:T(8,128)(2,1)S(1)} %get-tuple-element.48.part_ref, bf16[256,1152]{1,0:T(8,128)(2,1)S(1)} %collective-permute-done.12.near_ref, ...), custom_call_target="tpu_custom_call" | custom-call | flops 3000000 | bytes 2000000 | tf_op jit(solution)/shard_map/norm_back/pallas_call | solution.py:447
  (48 shorter events, 6.2 us)
Async XLA Ops:
  0.6 11.8 %copy-start.6 = (s32[8]{0:T(128)S(1)}, s32[8]{0:T(128)}, u32[]{:S(2)}) copy-start(s32[8]{0:T(128)} %counts_ref.7) | copy-start | bytes 100
  0.6 10.2 %collective-permute-start.1 = (bf16[128,1152]{1,0:T(8,128)(2,1)}, bf16[128,1152]{1,0:T(8,128)(2,1)S(1)}, u32[]{:S(2)}, u32[]{:S(2)}) collective-permute-start(bf16[128,1152]{1,0:T(8,128)(2,1)} %patch_ref.3), channel_id=1, source_target_pairs={{0,2},{1,3},{2,0},{3,1},{4,6},{5,7},{6,4},{7,5},{8,10},{9,11},{10,... | collective-permute-start | bytes 884744 | tf_op jit(solution)/shard_map/ppermute | solution.py:461
  3.7 7.2 %collective-permute-start = (bf16[128,1152]{1,0:T(8,128)(2,1)}, bf16[128,1152]{1,0:T(8,128)(2,1)S(1)}, u32[]{:S(2)}, u32[]{:S(2)}) collective-permute-start(bf16[128,1152]{1,0:T(8,128)(2,1)} %patch_ref.3), channel_id=1, source_target_pairs={{0,1},{1,0},{2,3},{3,2},{4,5},{5,4},{6,7},{7,6},{8,9},{9,8},{10,11... | collective-permute-start | bytes 884744 | tf_op jit(solution)/shard_map/ppermute | solution.py:461
  3.7 1.6 %copy-start = (bf16[1152,864]{0,1:T(8,128)(2,1)S(1)}, bf16[1152,864]{0,1:T(8,128)(2,1)}, u32[]{:S(2)}) copy-start(bf16[1152,864]{0,1:T(8,128)(2,1)} %param.11) | copy-start | bytes 5971972
  5.2 1.1 %copy-start.2 = (bf16[1152,288]{0,1:T(8,128)(2,1)S(1)}, bf16[1152,288]{0,1:T(8,128)(2,1)}, u32[]{:S(2)}) copy-start(bf16[1152,288]{0,1:T(8,128)(2,1)} %param.12) | copy-start | bytes 1990660
  7.1 3.8 %copy-start.7 = (f32[1152]{0:T(1024)S(1)}, f32[1152]{0:T(1024)}, u32[]{:S(2)}) copy-start(f32[1152]{0:T(1024)} %param.10) | copy-start | bytes 13828
  7.1 5.4 %copy-start.1 = (bf16[128,1152]{1,0:T(8,128)(2,1)S(1)}, bf16[128,1152]{1,0:T(8,128)(2,1)}, u32[]{:S(2)}) copy-start(bf16[128,1152]{1,0:T(8,128)(2,1)} %patch_ref.3) | copy-start | bytes 884740
  10.9 1.6 %collective-permute-start.2 = (bf16[128,1152]{1,0:T(8,128)(2,1)S(1)}, bf16[128,1152]{1,0:T(8,128)(2,1)S(1)}, u32[]{:S(2)}, u32[]{:S(2)}) collective-permute-start(bf16[128,1152]{1,0:T(8,128)(2,1)S(1)} %collective-permute-done.1.rows2), channel_id=1, source_target_pairs={{0,1},{1,0},{2,3},{3,2},{4,5},{5,4},{6,7},{7,6},{8,9},{9,8},{10,11... | collective-permute-start | bytes 884744 | tf_op jit(solution)/shard_map/ppermute | solution.py:461
  12.5 13.9 %copy-start.3 = (bf16[128,1152]{1,0:T(8,128)(2,1)S(1)}, bf16[128,1152]{1,0:T(8,128)(2,1)}, u32[]{:S(2)}) copy-start(bf16[128,1152]{1,0:T(8,128)(2,1)} %grad_ref.1) | copy-start | bytes 884740
  24.4 11.3 %collective-permute-start.3 = (bf16[256,1152]{1,0:T(8,128)(2,1)S(1)}, bf16[256,1152]{1,0:T(8,128)(2,1)S(1)}, u32[]{:S(2)}, u32[]{:S(2)}) collective-permute-start(bf16[256,1152]{1,0:T(8,128)(2,1)S(1)} %get-tuple-element.33), channel_id=1, source_target_pairs={{0,1},{1,0},{2,3},{3,2},{4,5},{5,4},{6,7},{7,6},{8,9},{9,8},{10,11... | collective-permute-start | bytes 1769480 | tf_op jit(solution)/shard_map/ppermute | solution.py:461
  24.6 3.9 %collective-permute-start.5 = (bf16[128,128]{1,0:T(8,128)(2,1)S(1)}, bf16[128,128]{1,0:T(8,128)(2,1)S(1)}, u32[]{:S(2)}, u32[]{:S(2)}) collective-permute-start(bf16[128,128]{1,0:T(8,128)(2,1)S(1)} %get-tuple-element.28), channel_id=1, source_target_pairs={{0,4},{4,0},{8,12},{12,8},{16,20},{20,16},{24,28},{28,24},{1,5},{5... | collective-permute-start | bytes 98312 | tf_op jit(solution)/shard_map/ppermute | solution.py:461
  26.4 9.3 %collective-permute-start.9 = (bf16[128,1152]{1,0:T(8,128)(2,1)S(1)}, bf16[128,1152]{1,0:T(8,128)(2,1)S(1)}, u32[]{:S(2)}, u32[]{:S(2)}) collective-permute-start(bf16[128,1152]{1,0:T(8,128)(2,1)S(1)} %copy-done.3), channel_id=1, source_target_pairs={{0,2},{1,3},{2,0},{3,1},{4,6},{5,7},{6,4},{7,5},{8,10},{9,11},{10,... | collective-permute-start | bytes 884744 | tf_op jit(solution)/shard_map/ppermute | solution.py:461
  28.5 4.3 %collective-permute-start.6 = (bf16[256,128]{1,0:T(8,128)(2,1)S(1)}, bf16[256,128]{1,0:T(8,128)(2,1)S(1)}, u32[]{:S(2)}, u32[]{:S(2)}) collective-permute-start(bf16[256,128]{1,0:T(8,128)(2,1)S(1)} %pad_maximum_fusion.2), channel_id=1, source_target_pairs={{0,8},{4,12},{8,0},{12,4},{16,24},{20,28},{24,16},{28,20},{1,9},{5... | collective-permute-start | bytes 196616 | tf_op jit(solution)/shard_map/ppermute | solution.py:461
  30.4 7.0 %collective-permute-start.8 = (bf16[128,1152]{1,0:T(8,128)(2,1)S(1)}, bf16[128,1152]{1,0:T(8,128)(2,1)S(1)}, u32[]{:S(2)}, u32[]{:S(2)}) collective-permute-start(bf16[128,1152]{1,0:T(8,128)(2,1)S(1)} %copy-done.3), channel_id=1, source_target_pairs={{0,1},{1,0},{2,3},{3,2},{4,5},{5,4},{6,7},{7,6},{8,9},{9,8},{10,11... | collective-permute-start | bytes 884744 | tf_op jit(solution)/shard_map/ppermute | solution.py:461
  32.8 7.8 %collective-permute-start.7 = (bf16[512,128]{1,0:T(8,128)(2,1)S(1)}, bf16[512,128]{1,0:T(8,128)(2,1)S(1)}, u32[]{:S(2)}, u32[]{:S(2)}) collective-permute-start(bf16[512,128]{1,0:T(8,128)(2,1)S(1)} %pad_maximum_fusion.1), channel_id=1, source_target_pairs={{0,16},{4,20},{8,24},{12,28},{16,0},{20,4},{24,8},{28,12},{1,17},{... | collective-permute-start | bytes 393224 | tf_op jit(solution)/shard_map/ppermute | solution.py:461
  35.7 1.6 %collective-permute-start.10 = (bf16[128,1152]{1,0:T(8,128)(2,1)S(1)}, bf16[128,1152]{1,0:T(8,128)(2,1)S(1)}, u32[]{:S(2)}, u32[]{:S(2)}) collective-permute-start(bf16[128,1152]{1,0:T(8,128)(2,1)S(1)} %collective-permute-done.9.grad2), channel_id=1, source_target_pairs={{0,1},{1,0},{2,3},{3,2},{4,5},{5,4},{6,7},{7,6},{8,9},{9,8},{10,11... | collective-permute-start | bytes 884744 | tf_op jit(solution)/shard_map/ppermute | solution.py:461
  35.8 9.5 %collective-permute-start.4 = (bf16[128,1152]{1,0:T(8,128)(2,1)S(1)}, bf16[128,1152]{1,0:T(8,128)(2,1)S(1)}, u32[]{:S(2)}, u32[]{:S(2)}) collective-permute-start(bf16[128,1152]{1,0:T(8,128)(2,1)S(1)} %add_convert_fusion.1), channel_id=1, source_target_pairs={{0,2},{1,3},{2,0},{3,1},{4,6},{5,7},{6,4},{7,5},{8,10},{9,11},{10,... | collective-permute-start | bytes 884744 | tf_op jit(solution)/shard_map/ppermute | solution.py:461
  38.5 12.3 %collective-permute-start.11 = (bf16[576,288]{1,0:T(8,128)(2,1)S(1)}, bf16[576,288]{1,0:T(8,128)(2,1)S(1)}, u32[]{:S(2)}, u32[]{:S(2)}) collective-permute-start(bf16[576,288]{1,0:T(8,128)(2,1)S(1)} %get-tuple-element.46), channel_id=1, source_target_pairs={{0,4},{4,0},{8,12},{12,8},{16,20},{20,16},{24,28},{28,24},{1,5},{5... | collective-permute-start | bytes 995336 | tf_op jit(solution)/shard_map/ppermute | solution.py:461
  40.6 4.7 %copy-start.4 = (bf16[1152,128]{1,0:T(8,128)(2,1)S(1)}, bf16[1152,128]{1,0:T(8,128)(2,1)}, u32[]{:S(2)}) copy-start(bf16[1152,128]{1,0:T(8,128)(2,1)} %embed_ref.1) | copy-start | bytes 884740
  51.0 19.7 %copy-start.8 = (s32[4]{0:T(128)S(1)}, s32[4]{0:T(128)}, u32[]{:S(2)}) copy-start(s32[4]{0:T(128)} %param.16) | copy-start | bytes 52
  57.9 14.5 %collective-permute-start.12 = (bf16[256,1152]{1,0:T(8,128)(2,1)S(1)}, bf16[256,1152]{1,0:T(8,128)(2,1)S(1)}, u32[]{:S(2)}, u32[]{:S(2)}) collective-permute-start(bf16[256,1152]{1,0:T(8,128)(2,1)S(1)} %get-tuple-element.49), channel_id=1, source_target_pairs={{0,1},{1,0},{2,3},{3,2},{4,5},{5,4},{6,7},{7,6},{8,9},{9,8},{10,11... | collective-permute-start | bytes 1769480 | tf_op jit(solution)/shard_map/ppermute | solution.py:461
  58.0 13.6 %collective-permute-start.14 = (bf16[288,288]{1,0:T(8,128)(2,1)S(1)}, bf16[288,288]{1,0:T(8,128)(2,1)S(1)}, u32[]{:S(2)}, u32[]{:S(2)}) collective-permute-start(bf16[288,288]{1,0:T(8,128)(2,1)S(1)} %fusion.1), channel_id=1, source_target_pairs={{0,8},{4,12},{8,0},{12,4},{16,24},{20,28},{24,16},{28,20},{1,9},{5... | collective-permute-start | bytes 497672 | tf_op jit(solution)/shard_map/ppermute | solution.py:461
  71.7 8.0 %collective-permute-start.15 = (bf16[144,288]{1,0:T(8,128)(2,1)S(1)}, bf16[144,288]{1,0:T(8,128)(2,1)S(1)}, u32[]{:S(2)}, u32[]{:S(2)}) collective-permute-start(bf16[144,288]{1,0:T(8,128)(2,1)S(1)} %slice.41), channel_id=1, source_target_pairs={{0,16},{4,20},{8,24},{12,28},{16,0},{20,4},{24,8},{28,12},{1,17},{... | collective-permute-start | bytes 248840 | tf_op jit(solution)/shard_map/ppermute | solution.py:461
  72.5 8.4 %collective-permute-start.13 = (bf16[128,1152]{1,0:T(8,128)(2,1)S(1)}, bf16[128,1152]{1,0:T(8,128)(2,1)S(1)}, u32[]{:S(2)}, u32[]{:S(2)}) collective-permute-start(bf16[128,1152]{1,0:T(8,128)(2,1)S(1)} %add_convert_fusion), channel_id=1, source_target_pairs={{0,2},{1,3},{2,0},{3,1},{4,6},{5,7},{6,4},{7,5},{8,10},{9,11},{10,... | collective-permute-start | bytes 884744 | tf_op jit(solution)/shard_map/ppermute | solution.py:461
  (1 other events, 0.8 us)

commit v3 on v2

v3 whole, which is shorter than its diff:
```python
from functools import partial
import math

import jax
import jax.numpy as jnp
from jax import lax
from jax.experimental import pallas as pl
from jax.experimental.pallas import tpu as pltpu
from jax.sharding import PartitionSpec as P


HEAD_DIM = 72
LANES = 128
EMB = 128
QTOK = 32
MP = 4
HEAD_GROUP = 4
DISTANCES = (4, 1, 2)
ARRIVAL = (0, 4, 1, 5, 2, 6, 3, 7)
SCALE = HEAD_DIM ** (-0.5)
LOG2E = math.log2(math.e)
F32 = jnp.float32
BF16 = jnp.bfloat16

VMEM = pl.BlockSpec(memory_space=pltpu.VMEM)
SMEM = pl.BlockSpec(memory_space=pltpu.SMEM)
HBM = pl.BlockSpec(memory_space=pl.ANY)


def dot(left, right, left_dim, right_dim):
    return lax.dot_general(
        left, right, (((left_dim,), (right_dim,)), ((), ())), preferred_element_type=F32
    )


def shape(dims, kind):
    return jax.ShapeDtypeStruct(dims, kind)


def cost(flops, size, exps=0):
    return pl.CostEstimate(flops=int(flops), bytes_accessed=int(size), transcendentals=int(exps))


def grant(mebibytes):
    return pltpu.CompilerParams(vmem_limit_bytes=mebibytes * 1024 * 1024)


def full(*dims):
    return pl.BlockSpec(dims, lambda *_: (0,) * len(dims))


def unit_rows(values):
    return values * lax.rsqrt(jnp.sum(values * values, axis=-1, keepdims=True) + 1e-06)


def place_of(index, model_index, rows_dev):
    return (model_index ^ (index // rows_dev)) * rows_dev + index % rows_dev


def prepare_kernel(heads, mixing_ref, output_ref, tokens_ref, mixing_pad, output_pad, unit_ref):
    def spread(source, target, index):
        target[index * LANES : index * LANES + HEAD_DIM, :] = source[
            index * HEAD_DIM : (index + 1) * HEAD_DIM, :
        ]
        target[index * LANES + HEAD_DIM : (index + 1) * LANES, :] = jnp.zeros(
            (LANES - HEAD_DIM, target.shape[1]), BF16
        )

    values = tokens_ref[...].astype(F32)
    unit_ref[...] = unit_rows(values).astype(BF16)
    for index in range(3 * heads):
        spread(mixing_ref, mixing_pad, index)
    for index in range(heads):
        spread(output_ref, output_pad, index)


def prepare(mixing, output, tokens, heads):
    width = mixing.shape[1]
    return pl.pallas_call(
        partial(prepare_kernel, heads),
        out_shape=(
            shape((3 * heads * LANES, width), BF16),
            shape((heads * LANES, width), BF16),
            shape(tokens.shape, BF16),
        ),
        in_specs=[VMEM] * 3,
        out_specs=(VMEM,) * 3,
        cost_estimate=cost(0, 8e6),
        name="prepare",
        compiler_params=grant(24),
    )(mixing, output, tokens)


def hand_out(product, keep0, keep2, send):
    size = keep0.shape[0]
    keep0[...] = product[:size].astype(BF16)
    send[:size, :] = product[size : 2 * size].astype(BF16)
    keep2[...] = product[2 * size : 3 * size].astype(BF16)
    send[size:, :] = product[3 * size :].astype(BF16)


def forward_kernel(
    heads,
    rows_dev,
    counts_ref,
    rows0,
    rows1,
    rows2,
    rows3,
    gain_ref,
    mixing_ref,
    output_ref,
    packed_ref,
    prob_ref,
    attended_ref,
    keep0,
    keep2,
    send,
    normed,
):
    turn = pl.program_id(0)
    rows = rows_dev * MP
    group = prob_ref.shape[0]

    @pl.when(turn == 0)
    def _():
        for index, block in enumerate((rows0, rows1, rows2, rows3)):
            values = block[...].astype(F32)
            center = values - jnp.mean(values, axis=-1, keepdims=True)
            spread = jnp.mean(center * center, axis=-1, keepdims=True)
            normed[index * rows_dev : (index + 1) * rows_dev, :] = (
                center * lax.rsqrt(spread + 1e-06) * gain_ref[...]
            ).astype(BF16)

    packed = dot(normed[...], mixing_ref[...], 1, 1).astype(BF16)
    packed_ref[...] = packed
    count = counts_ref[lax.axis_index("dp")]
    model_index = lax.axis_index("mp")
    columns = lax.broadcasted_iota(jnp.int32, (1, rows), 1)
    seen = place_of(columns, model_index, rows_dev) < count
    lines = lax.broadcasted_iota(jnp.int32, (rows, 1), 0)
    live = place_of(lines, model_index, rows_dev) < count
    for index in range(group):
        own = packed[:, index * 3 * LANES : (index + 1) * 3 * LANES]
        query, key, value = own[:, :LANES], own[:, LANES : 2 * LANES], own[:, 2 * LANES :]
        score = dot(query, key, 1, 1)
        score = jnp.where(seen, score, -1e30)
        largest = jnp.max(score, axis=-1, keepdims=True)
        raised = jnp.exp2((score - largest) * (SCALE * LOG2E))
        total = jnp.sum(raised, axis=-1, keepdims=True)
        prob = (raised * (1.0 / total)).astype(BF16)
        prob_ref[index] = prob
        found = dot(prob, value, 1, 0)
        attended_ref[turn * group + index] = jnp.where(live, found, 0.0).astype(BF16)

    @pl.when(turn == pl.num_programs(0) - 1)
    def _():
        joined = jnp.concatenate([attended_ref[index] for index in range(heads)], axis=1)
        hand_out(dot(joined, output_ref[...], 1, 0), keep0, keep2, send)


def handed_shapes(rows_dev, width):
    kept = shape((rows_dev, width), BF16)
    return (kept, kept, shape((2 * rows_dev, width), BF16))


def forward(counts, blocks, gain, mixing_pad, output_pad, heads):
    rows_dev, width = blocks[0].shape
    rows = rows_dev * MP
    wide = 3 * LANES
    group = HEAD_GROUP if heads % HEAD_GROUP == 0 else 1
    block = full(rows_dev, width)
    return pl.pallas_call(
        partial(forward_kernel, heads, rows_dev),
        grid=(heads // group,),
        out_shape=(
            shape((rows, heads * wide), BF16),
            shape((heads, rows, rows), BF16),
            shape((heads, rows, LANES), BF16),
        )
        + handed_shapes(rows_dev, width),
        in_specs=[SMEM]
        + [block] * MP
        + [
            full(1, width),
            pl.BlockSpec((group * wide, width), lambda turn: (turn, 0)),
            full(heads * LANES, width),
        ],
        out_specs=(
            pl.BlockSpec((rows, group * wide), lambda turn: (0, turn)),
            pl.BlockSpec((group, rows, rows), lambda turn: (turn, 0, 0)),
            full(heads, rows, LANES),
        )
        + (block, block, full(2 * rows_dev, width)),
        scratch_shapes=[pltpu.VMEM((rows, width), BF16)],
        cost_estimate=cost(3e9, 12e6, heads * rows * rows),
        name="forward_attention",
        compiler_params=grant(28),
    )(counts, *blocks, gain, mixing_pad, output_pad)


def weight_kernel(
    heads, rows_dev, order, counts_ref, grad0, grad1, grad2, grad3, attended_ref, output_ref, *refs
):
    (flow_ref, *outs), (stacked, result) = refs[: len(refs) - 2], refs[len(refs) - 2 :]
    for index, block in enumerate((grad0, grad1, grad2, grad3)):
        stacked[index * rows_dev : (index + 1) * rows_dev, :] = block[...]
    joined = jnp.concatenate([attended_ref[index] for index in range(heads)], axis=1)
    count = counts_ref[lax.axis_index("dp")]
    lines = lax.broadcasted_iota(jnp.int32, (rows_dev * MP, 1), 0)
    live = place_of(lines, lax.axis_index("mp"), rows_dev) < count
    flow = dot(stacked[...], output_ref[...], 1, 1)
    flow_ref[...] = jnp.where(live, flow, 0.0).astype(BF16)
    product = dot(stacked[...], joined, 0, 0)
    for index in range(heads):
        result[:, index * HEAD_DIM : (index + 1) * HEAD_DIM] = product[
            :, index * LANES : index * LANES + HEAD_DIM
        ]
    if order is None:
        outs[0][...] = result[...]
    else:
        mine = lax.axis_index("dp")
        share = result.shape[0] // sum(len(group) for group in order)
        for group, out in zip(order, outs):
            for spot, piece in enumerate(group):
                start = pl.multiple_of((mine ^ piece) * share, 16)
                out[spot * share : (spot + 1) * share, :] = result[
                    pl.ds(start, share), :
                ].astype(out.dtype)


def weight_parts(counts, grads, attended, output_pad, order):
    rows_dev, width = grads[0].shape
    heads = attended.shape[0]
    narrow = heads * HEAD_DIM
    if order is None:
        outs = (shape((width, narrow), F32),)
    else:
        share = width // sum(len(group) for group in order)
        outs = tuple(
            shape((len(group) * share, narrow), F32 if index == 0 else BF16)
            for index, group in enumerate(order)
        )
    outs = (shape((rows_dev * MP, heads * LANES), BF16),) + outs
    return pl.pallas_call(
        partial(weight_kernel, heads, rows_dev, order),
        out_shape=outs,
        in_specs=[SMEM] + [VMEM] * (MP + 2),
        out_specs=(VMEM,) * len(outs),
        scratch_shapes=[
            pltpu.VMEM((rows_dev * MP, width), BF16),
            pltpu.VMEM((width, narrow), F32),
        ],
        cost_estimate=cost(7e8, 4e6),
        name="weight_parts",
        compiler_params=grant(20),
    )(counts, *grads, attended, output_pad)


def backward_kernel(last, flow_ref, packed_ref, prob_ref, *refs):
    if last:
        earlier, mixing_hbm, keep0, keep2, send, mixing, sem = refs
        fetch = pltpu.make_async_copy(mixing_hbm, mixing, sem)
        fetch.start()
    pieces = []
    for index in range(prob_ref.shape[0]):
        flow = flow_ref[:, index * LANES : (index + 1) * LANES]
        own = packed_ref[:, index * 3 * LANES : (index + 1) * 3 * LANES]
        query, key, value = own[:, :LANES], own[:, LANES : 2 * LANES], own[:, 2 * LANES :]
        weights = prob_ref[index]
        prob = weights.astype(F32)
        grad_prob = dot(flow, value, 1, 1)
        delta = jnp.sum(grad_prob * prob, axis=-1, keepdims=True)
        grad_score = (prob * (grad_prob - delta)).astype(BF16)
        pieces.append((dot(grad_score, key, 1, 0) * SCALE).astype(BF16))
        pieces.append((dot(grad_score, query, 0, 0) * SCALE).astype(BF16))
        pieces.append(dot(weights, flow, 0, 0).astype(BF16))
    if last:
        fetch.wait()
        everything = jnp.concatenate([earlier[...]] + pieces, axis=1)
        hand_out(dot(everything, mixing[...], 1, 0), keep0, keep2, send)
    else:
        for index, piece in enumerate(pieces):
            refs[0][:, index * LANES : (index + 1) * LANES] = piece


def backward(flow, packed, probs, first, heads, rest=()):
    rows = flow.shape[0]
    rows_dev = rows // MP
    wide = 3 * LANES
    if rest:
        earlier, mixing_pad = rest
        width = mixing_pad.shape[1]
        out_shape = handed_shapes(rows_dev, width)
        more_specs = [full(*earlier.shape), HBM]
        out_specs = (full(rows_dev, width), full(rows_dev, width), full(2 * rows_dev, width))
        scratch = [pltpu.VMEM(mixing_pad.shape, BF16), pltpu.SemaphoreType.DMA]
    else:
        out_shape = shape((rows, heads * wide), BF16)
        more_specs = []
        out_specs = full(rows, heads * wide)
        scratch = []
    turn = first // heads
    return pl.pallas_call(
        partial(backward_kernel, bool(rest)),
        grid=(1,),
        out_shape=out_shape,
        in_specs=[
            pl.BlockSpec((rows, heads * LANES), lambda _: (0, turn)),
            pl.BlockSpec((rows, heads * wide), lambda _: (0, turn)),
            pl.BlockSpec((heads, rows, rows), lambda _: (turn, 0, 0)),
        ]
        + more_specs,
        out_specs=out_specs,
        scratch_shapes=scratch,
        cost_estimate=cost(3e9, 6e6),
        name="backward_last" if rest else "backward_first",
        compiler_params=grant(28),
    )(flow, packed, probs, *rest)


def score_kernel(
    rows_dev, few, counts_ref, patch_ref, part_ref, near_ref, far_ref, embed_ref, tokens_ref,
    hidden_ref, best_ref, page_emb
):
    mine = lax.axis_index("dp")

    @pl.when(pl.program_id(0) == 0)
    def _():
        mixed = part_ref[...].astype(F32) + near_ref[...].astype(F32) + far_ref[...].astype(F32)
        hidden = (patch_ref[...].astype(F32) + mixed).astype(BF16)
        hidden_ref[...] = hidden
        embedded = dot(hidden, embed_ref[...], 1, 0)
        page_emb[...] = unit_rows(embedded).astype(BF16)

    similar = dot(page_emb[...], tokens_ref[...], 1, 1)
    lines = lax.broadcasted_iota(jnp.int32, (rows_dev, 1), 0) + lax.axis_index("mp") * rows_dev
    similar = jnp.where(lines < counts_ref[mine], similar, -2.0)
    best = jnp.max(similar, axis=0, keepdims=True)
    if few:
        size = best_ref.shape[1]
        for piece in range(best.shape[1] // size):
            row = best[:, piece * size : (piece + 1) * size]
            for copy in range(MP):
                best_ref[pl.ds((mine ^ ARRIVAL[piece]) * MP + copy, 1), :] = row
    else:
        best_ref[...] = best


def hidden_and_best(counts, patches, part, received, far, embed_weight, tokens, few, local):
    rows_dev, width = patches.shape
    size = tokens.shape[0]
    chunk = size if few else math.gcd(size, 1024)
    block = full(rows_dev, width)
    if few:
        best_shape, best_spec = shape((size // local * MP, local), F32), full(size // local * MP, local)
    else:
        best_shape, best_spec = shape((1, size), F32), pl.BlockSpec((1, chunk), lambda index: (0, index))
    return pl.pallas_call(
        partial(score_kernel, rows_dev, few),
        grid=(size // chunk,),
        out_shape=(shape((rows_dev, width), BF16), best_shape),
        in_specs=[SMEM]
        + [block] * 4
        + [full(width, EMB), pl.BlockSpec((chunk, EMB), lambda index: (index, 0))],
        out_specs=(block, best_spec),
        scratch_shapes=[pltpu.VMEM((rows_dev, EMB), BF16)],
        cost_estimate=cost(1e8, 2e6),
        name="hidden_and_best",
        compiler_params=grant(12),
    )(counts, patches, part, received, far, embed_weight, tokens)


def norm_back_kernel(patch_ref, gain_ref, grad_ref, part_ref, near_ref, far_ref, *refs):
    values = patch_ref[...].astype(F32)
    center = values - jnp.mean(values, axis=-1, keepdims=True)
    spread = jnp.mean(center * center, axis=-1, keepdims=True)
    inverse = lax.rsqrt(spread + 1e-06)
    flow = part_ref[...].astype(F32) + near_ref[...].astype(F32) + far_ref[...].astype(F32)
    flow = flow * gain_ref[...]
    along = jnp.mean(flow * center, axis=-1, keepdims=True)
    level = jnp.mean(flow, axis=-1, keepdims=True)
    result = inverse * (flow - level - center * (inverse * inverse * along))
    out = (grad_ref[...].astype(F32) + result).astype(BF16)
    if len(refs) == 1:
        refs[0][...] = out
        return
    mine_ref, other_ref, found_ref, positive_ref, out_ref, weight_ref, score_ref, loss_ref = refs
    out_ref[...] = out
    weight_ref[...] = mine_ref[...] + other_ref[...].astype(F32)
    pages = found_ref.shape[0] // MP
    best = jnp.max(found_ref[...].reshape(pages, MP, found_ref.shape[1]), axis=1)
    turned = best.T
    columns = lax.broadcasted_iota(jnp.int32, (1, pages), 1)
    for query in range(score_ref.shape[0]):
        row = jnp.sum(turned[query * QTOK : (query + 1) * QTOK], axis=0, keepdims=True)
        score_ref[query : query + 1, :] = row
        chosen = columns == positive_ref[query]
        positive = jnp.sum(jnp.where(chosen, row, 0.0), axis=1, keepdims=True)
        negative = jnp.max(jnp.where(chosen, -1e30, row), axis=1, keepdims=True)
        gap = negative - positive
        loss = jnp.maximum(gap, 0.0) + jnp.log1p(jnp.exp(-jnp.abs(gap)))
        loss_ref[query] = loss[0, 0]


def norm_back(patches, gain, grads, part, near, far, more=()):
    block = full(*patches.shape)
    out_shape, out_specs, specs = [shape(patches.shape, BF16)], [block], []
    if more:
        mine, _, found, positive = more
        scores = (positive.shape[0], found.shape[0] // MP)
        specs = [full(*mine.shape), full(*mine.shape), full(*found.shape), SMEM]
        out_shape += [shape(mine.shape, F32), shape(scores, F32), shape(positive.shape, F32)]
        out_specs += [full(*mine.shape), full(*scores), SMEM]
    return pl.pallas_call(
        norm_back_kernel,
        grid=(1,),
        out_shape=tuple(out_shape),
        in_specs=[block, full(*gain.shape), block, block, block, block] + specs,
        out_specs=tuple(out_specs),
        cost_estimate=cost(3e6, 2e6),
        name="norm_back",
        compiler_params=grant(12),
    )(patches, gain, grads, part, near, far, *more)


def join_kernel(kept_ref, got1_ref, got2_ref, mine_ref, send_ref):
    half, share = kept_ref.shape[0], mine_ref.shape[0]
    total = kept_ref[...] + got1_ref[:half, :].astype(F32) + got2_ref[...].astype(F32)
    mine_ref[...] = total[:share]
    send_ref[...] = total[share:].astype(BF16)


def join_parts(kept, got1, got2):
    share = (kept.shape[0] // 2, kept.shape[1])
    return pl.pallas_call(
        join_kernel,
        out_shape=(shape(share, F32), shape(share, BF16)),
        in_specs=[VMEM] * 3,
        out_specs=(VMEM,) * 2,
        cost_estimate=cost(3e5, 1e6),
        name="join_parts",
        compiler_params=grant(6),
    )(kept, got1, got2)


def swap(values, axis, distance):
    size = lax.axis_size(axis)
    return lax.ppermute(values, axis, [(index, index ^ distance) for index in range(size)])


def scatter_sum(parts):
    part0, part2, send = parts
    received = swap(send, "mp", 1)
    relayed = received[part2.shape[0] :]
    going = (part2.astype(F32) + relayed.astype(F32)).astype(BF16)
    return part0, received, swap(going, "mp", 2), going


def after(values, *others):
    return lax.optimization_barrier((values, *others))[0]


def body(
    patches,
    norm_gain,
    query_key_value,
    output_weight,
    embed_weight,
    query_tokens,
    patch_counts,
    positive_page,
    hidden_grad,
):
    data_index = lax.axis_index("dp")
    data_size = lax.axis_size("dp")
    few = data_size == 8
    heads = output_weight.shape[1] // HEAD_DIM
    gain = norm_gain.reshape(1, -1)

    rows2 = swap(patches, "mp", 2)
    rows1 = swap(patches, "mp", 1)
    grads2 = swap(hidden_grad, "mp", 2)
    grads1 = swap(hidden_grad, "mp", 1)

    local = query_tokens.shape[0]
    mixing_pad, output_pad, query_emb = prepare(
        query_key_value.T, output_weight.T, query_tokens.reshape(local * QTOK, EMB), heads
    )
    if few:
        tokens = query_emb
        for distance in DISTANCES[:2]:
            other = swap(tokens, "dp", distance)
            tokens = jnp.concatenate([tokens, other], axis=0)
    else:
        tokens = lax.all_gather(query_emb, "dp", axis=0, tiled=True)
    rows2 = after(rows2, query_emb)
    rows3 = swap(rows2, "mp", 1)

    packed, probs, attended, *parts = forward(
        patch_counts, (patches, rows1, rows2, rows3), gain, mixing_pad, output_pad, heads
    )
    grads3 = swap(after(grads2, rows3), "mp", 1)
    grads = (hidden_grad, grads1, grads2, grads3)
    part, received, far, _ = scatter_sum(parts)
    half = heads - heads // 4
    if few:
        order = ((0, 4), (2, 6), (1, 5, 3, 7))
        flow, kept, second, first = weight_parts(patch_counts, grads, attended, output_pad, order)
        got1 = swap(first, "dp", 1)
        other = swap(tokens, "dp", 2)
        tokens = jnp.concatenate([tokens, after(other, kept)], axis=0)
        earlier = backward(flow, packed, probs, 0, half)
        tokens = after(tokens, earlier)
    else:
        flow, whole = weight_parts(patch_counts, grads, attended, output_pad, None)
        weight_grad = lax.psum_scatter(whole, "dp", scatter_dimension=0, tiled=True)
        earlier = backward(flow, packed, probs, 0, half)
    hidden, best = hidden_and_best(
        patch_counts, patches, part, received, far, embed_weight, tokens, few, local * QTOK
    )
    if few:
        earlier, best = lax.optimization_barrier((earlier, best))
    grad_parts = backward(flow, packed, probs, half, heads - half, (earlier, mixing_pad))
    part, received, far, sent = scatter_sum(grad_parts)
    more = ()
    if few:
        going = (second.astype(F32) + got1[kept.shape[0] :].astype(F32)).astype(BF16)
        got2 = swap(going, "dp", 2)
        mine, send = join_parts(kept, got1, got2)
        other = swap(send, "dp", 4)
        found = lax.all_to_all(after(best, sent), ("dp", "mp"), 0, 0, tiled=True)
        more = (mine, other, found, positive_page)
    patch_grad, *rest = norm_back(patches, gain, hidden_grad, part, received, far, more)
    if few:
        return (hidden, patch_grad, *rest)
    best = jnp.maximum(best, swap(best, "mp", 1))
    best = jnp.maximum(best, swap(best, "mp", 2))
    part_scores = jnp.sum(best.reshape(-1, QTOK), axis=1)
    every = lax.all_gather(part_scores.reshape(-1, 1), "dp", axis=1, tiled=True)
    my_scores = lax.dynamic_slice_in_dim(every, data_index * local, local, 0)
    columns = jnp.arange(my_scores.shape[1], dtype=jnp.int32)
    chosen = columns[None, :] == positive_page[:, None]
    positive_score = jnp.sum(jnp.where(chosen, my_scores, 0.0), axis=1)
    negative_score = jnp.max(jnp.where(chosen, -1e30, my_scores), axis=1)
    loss = jax.nn.softplus(negative_score - positive_score)
    return (hidden, patch_grad, weight_grad, my_scores, loss)


def solution(mesh):
    return jax.shard_map(
        body,
        mesh=mesh,
        in_specs=(
            P(("dp", "mp"), None),
            P(),
            P(None, "mp"),
            P(None, "mp"),
            P(),
            P("dp", None, None),
            P(),
            P("dp"),
            P(("dp", "mp"), None),
        ),
        out_specs=(
            P(("dp", "mp"), None),
            P(("dp", "mp"), None),
            P("dp", "mp"),
            P("dp", None),
            P("dp"),
        ),
        check_vma=False,
    )
```

time: 82.4 us -> 82 us (level)
  waiting for transfers between devices: 19.8 us -> 33.4 us
  blocking collectives: 10.4 us -> 0 us
  Pallas kernels: 27.9 us -> 19.3 us
  starting transfers between devices: 17.3 us -> 24.4 us
  other arithmetic: 2.51 us -> 0.25 us
    all_to_all x1 -> x0, blocking collectives: 10.4 us -> none  [body(): lax.all_to_all(best, ('dp', 'mp'), 0, 0, tiled=True)]
    pallas_call x5, Pallas kernels: 24.9 us -> 14.9 us  [the longest x2 7.08 us: backward(): pl.pallas_call(partial(backward_kernel, bool(rest)), grid=(1,), out_shape...]
    ppermute x16, waiting for transfers between devices: 19.8 us -> 26.7 us  [swap(): lax.ppermute(values, axis, [(index, index ^ distance) for index in range(...]
    all_to_all x0 -> x1, waiting for transfers between devices: none -> 6.65 us  [body(): found = lax.all_to_all(after(best, sent), ('dp', 'mp'), 0, 0, tiled=True)]
    all_to_all x0 -> x1, starting transfers between devices: none -> 3.99 us  [body(): found = lax.all_to_all(after(best, sent), ('dp', 'mp'), 0, 0, tiled=True)]
    ppermute x16, starting transfers between devices: 17.3 us -> 20.4 us  [swap(): lax.ppermute(values, axis, [(index, index ^ distance) for index in range(...]
    pallas_call x1, Pallas kernels: 1.16 us -> 2.36 us  [weight_parts(): pl.pallas_call(partial(weight_kernel, heads, rows_dev, order), out_shape=...]
    reduce_sum x1 -> x0, other arithmetic: 0.89 us -> none  [body(): positive_score = jnp.sum(jnp.where(chosen, my_scores, 0.0), axis=1)]
  transfers between devices with their start and end apart: 16 -> 17, of which waited for: 9 -> 10; matrix products, arithmetic and copies ran while one was open for 3% -> 0% of each run, Pallas kernels for 10% -> 14%
where the time goes in v3:
time: 82 us; the launch traced here: 81.7 us
  waiting for transfers between devices  33.4 us (41%)
  starting transfers between devices  24.4 us (30%)
  Pallas kernels  19.3 us (24%)
  local copies, waits for them, and re-layouts  3.43 us (4%)
  between operations  0.93 us (1%)
    ppermute x16, waiting for transfers between devices, swap(): lax.ppermute(values, axis, [(index, index ^ distance) for index in range(...  26.7 us
    ppermute x16, starting transfers between devices, swap(): lax.ppermute(values, axis, [(index, index ^ distance) for index in range(...  20.4 us
    pallas_call x2, Pallas kernels, backward(): pl.pallas_call(partial(backward_kernel, bool(rest)), grid=(1,), out_shape...  7.08 us
    all_to_all x1, waiting for transfers between devices, body(): found = lax.all_to_all(after(best, sent), ('dp', 'mp'), 0, 0, tiled=True)  6.65 us
    pallas_call x1, Pallas kernels, forward(): pl.pallas_call(partial(forward_kernel, heads, rows_dev), grid=(heads // g...  5.91 us
    all_to_all x1, starting transfers between devices, body(): found = lax.all_to_all(after(best, sent), ('dp', 'mp'), 0, 0, tiled=True)  3.99 us
    unnamed x18, local copies, waits for them, and re-layouts  3.43 us
    pallas_call x1, Pallas kernels, weight_parts(): pl.pallas_call(partial(weight_kernel, heads, rows_dev, order), out_shape=...  2.36 us
  transfers between devices with their start and end apart: 17, of which 10 were waited for; matrix products, arithmetic and copies ran while one was open for 0% of the time, Pallas kernels for 14%

profile of v3, /device:TPU:0, one launch (start us, length us, event | category | flops | bytes accessed | tf_op | source)
XLA Modules:
  0.0 81.7 jit_solution(7365422762523193102)
XLA Ops:
  0.6 3.0 %collective-permute-start.1 = (bf16[128,1152]{1,0:T(8,128)(2,1)}, bf16[128,1152]{1,0:T(8,128)(2,1)S(1)}, u32[]{:S(2)}, u32[]{:S(2)}) collective-permute-start(bf16[128,1152]{1,0:T(8,128)(2,1)} %patch_ref.3), channel_id=1, source_target_pairs={{0,2},{1,3},{2,0},{3,1},{4,6},{5,7},{6,4},{7,5},{8,10},{9,11},{10,... | collective-permute-start | bytes 884744 | tf_op jit(solution)/shard_map/ppermute | solution.py:449
  3.7 1.6 %copy-done = bf16[1152,864]{0,1:T(8,128)(2,1)S(1)} copy-done((bf16[1152,864]{0,1:T(8,128)(2,1)S(1)}, bf16[1152,864]{0,1:T(8,128)(2,1)}, u32[]{:S(2)}) %copy-start) | copy-done | bytes 1990680
  7.4 3.5 %collective-permute-done.1.rows2 = bf16[128,1152]{1,0:T(8,128)(2,1)S(1)} collective-permute-done((bf16[128,1152]{1,0:T(8,128)(2,1)}, bf16[128,1152]{1,0:T(8,128)(2,1)S(1)}, u32[]{:S(2)}, u32[]{:S(2)}) %collective-permute-start.1) | collective-permute-done | bytes 294944 | tf_op jit(solution)/shard_map/ppermute | solution.py:449
  10.9 1.7 %collective-permute-start.9 = (bf16[128,1152]{1,0:T(8,128)(2,1)S(1)}, bf16[128,1152]{1,0:T(8,128)(2,1)S(1)}, u32[]{:S(2)}, u32[]{:S(2)}) collective-permute-start(bf16[128,1152]{1,0:T(8,128)(2,1)S(1)} %copy-done.1), channel_id=1, source_target_pairs={{0,2},{1,3},{2,0},{3,1},{4,6},{5,7},{6,4},{7,5},{8,10},{9,11},{10,... | collective-permute-start | bytes 884744 | tf_op jit(solution)/shard_map/ppermute | solution.py:449
  12.7 5.9 %forward_attention.1 = (bf16[512,1536]{1,0:T(8,128)(2,1)S(1)}, bf16[4,512,512]{2,1,0:T(8,128)(2,1)S(1)}, bf16[4,512,128]{2,1,0:T(8,128)(2,1)S(1)}, bf16[128,1152...) custom-call(s32[8]{0:T(128)S(1)} %copy-done.6, bf16[128,1152]{1,0:T(8,128)(2,1)S(1)} %copy-done.2, ...), custom_call_target="tpu_custom_call" | custom-call | flops 3000000000 | bytes 12000000 | tf_op jit(solution)/shard_map/forward_attention/pallas_call | solution.py:173
  18.9 2.6 %collective-permute-start.5 = (bf16[128,128]{1,0:T(8,128)(2,1)S(1)}, bf16[128,128]{1,0:T(8,128)(2,1)S(1)}, u32[]{:S(2)}, u32[]{:S(2)}) collective-permute-start(bf16[128,128]{1,0:T(8,128)(2,1)S(1)} %get-tuple-element.36), channel_id=1, source_target_pairs={{0,16},{4,20},{8,24},{12,28},{16,0},{20,4},{24,8},{28,12},{1,17},{... | collective-permute-start | bytes 98312 | tf_op jit(solution)/shard_map/ppermute | solution.py:449
  22.0 1.7 %collective-permute-done.5 = bf16[128,128]{1,0:T(8,128)(2,1)S(1)} collective-permute-done((bf16[128,128]{1,0:T(8,128)(2,1)S(1)}, bf16[128,128]{1,0:T(8,128)(2,1)S(1)}, u32[]{:S(2)}, u32[]{:S(2)}) %collective-permute-start.5) | collective-permute-done | bytes 32800 | tf_op jit(solution)/shard_map/ppermute | solution.py:449
  23.7 1.5 %collective-permute-start.6 = (bf16[256,128]{1,0:T(8,128)(2,1)S(1)}, bf16[256,128]{1,0:T(8,128)(2,1)S(1)}, u32[]{:S(2)}, u32[]{:S(2)}) collective-permute-start(bf16[256,128]{1,0:T(8,128)(2,1)S(1)} %pad_maximum_fusion.2), channel_id=1, source_target_pairs={{0,4},{4,0},{8,12},{12,8},{16,20},{20,16},{24,28},{28,24},{1,5},{5... | collective-permute-start | bytes 196616 | tf_op jit(solution)/shard_map/ppermute | solution.py:449
  25.2 2.7 %collective-permute-done.6 = bf16[256,128]{1,0:T(8,128)(2,1)S(1)} collective-permute-done((bf16[256,128]{1,0:T(8,128)(2,1)S(1)}, bf16[256,128]{1,0:T(8,128)(2,1)S(1)}, u32[]{:S(2)}, u32[]{:S(2)}) %collective-permute-start.6) | collective-permute-done | bytes 65568 | tf_op jit(solution)/shard_map/ppermute | solution.py:449
  28.0 1.6 %collective-permute-start.7 = (bf16[512,128]{1,0:T(8,128)(2,1)S(1)}, bf16[512,128]{1,0:T(8,128)(2,1)S(1)}, u32[]{:S(2)}, u32[]{:S(2)}) collective-permute-start(bf16[512,128]{1,0:T(8,128)(2,1)S(1)} %pad_maximum_fusion.1), channel_id=1, source_target_pairs={{0,8},{4,12},{8,0},{12,4},{16,24},{20,28},{24,16},{28,20},{1,9},{5... | collective-permute-start | bytes 393224 | tf_op jit(solution)/shard_map/ppermute | solution.py:449
  29.6 2.4 %weight_parts.1 = (bf16[512,512]{1,0:T(8,128)(2,1)S(1)}, f32[288,288]{1,0:T(8,128)S(1)}, bf16[288,288]{1,0:T(8,128)(2,1)S(1)}, bf16[576,288]{1,0:T(8,128)(2,1)S(1)}) custom-call(s32[8]{0:T(128)S(1)} %copy-done.6, bf16[128,1152]{1,0:T(8,128)(2,1)S(1)} %copy-done.1, bf16[128,1152]{1,0:T(8,128)(2,1)S(1)} %collective-permute-done.8.grad1, ...), custom_call_target="tpu_custom_call" | custom-call | flops 700000000 | bytes 4000000 | tf_op jit(solution)/shard_map/weight_parts/pallas_call | solution.py:245
  33.1 1.5 %collective-permute-start.4 = (bf16[128,1152]{1,0:T(8,128)(2,1)S(1)}, bf16[128,1152]{1,0:T(8,128)(2,1)S(1)}, u32[]{:S(2)}, u32[]{:S(2)}) collective-permute-start(bf16[128,1152]{1,0:T(8,128)(2,1)S(1)} %add_convert_fusion.1), channel_id=1, source_target_pairs={{0,2},{1,3},{2,0},{3,1},{4,6},{5,7},{6,4},{7,5},{8,10},{9,11},{10,... | collective-permute-start | bytes 884744 | tf_op jit(solution)/shard_map/ppermute | solution.py:449
  34.7 2.7 %backward_first.1.refs_0_ = bf16[512,1152]{1,0:T(8,128)(2,1)S(1)} custom-call(bf16[512,512]{1,0:T(8,128)(2,1)S(1)} %get-tuple-element.47.flow_ref, bf16[512,1536]{1,0:T(8,128)(2,1)S(1)} %get-tuple-element.48.packed_ref, bf16[4,512,512]{2,1,0:T(8,128)(2,1)S(1)} %get-tuple-element.49.prob_ref), custom_call_target="tpu_custom_call" | custom-call | flops 3000000000 | bytes 6000000 | tf_op jit(solution)/shard_map/backward_first/pallas_call | solution.py:304
  37.3 2.6 %collective-permute-done.4.far_ref = bf16[128,1152]{1,0:T(8,128)(2,1)S(1)} collective-permute-done((bf16[128,1152]{1,0:T(8,128)(2,1)S(1)}, bf16[128,1152]{1,0:T(8,128)(2,1)S(1)}, u32[]{:S(2)}, u32[]{:S(2)}) %collective-permute-start.4) | collective-permute-done | bytes 294944 | tf_op jit(solution)/shard_map/ppermute | solution.py:449
  39.9 1.7 %hidden_and_best.1 = (bf16[128,1152]{1,0:T(8,128)(2,1)}, f32[32,128]{1,0:T(8,128)}) custom-call(s32[8]{0:T(128)S(1)} %copy-done.6, bf16[128,1152]{1,0:T(8,128)(2,1)S(1)} %copy-done.2, bf16[128,1152]{1,0:T(8,128)(2,1)S(1)} %get-tuple-element.40.part_ref, bf16[256,1152]{1,0:T(8,128)(2,1)S(1)} %collective-permute-done.3.near_ref, ...), custom_call_target="tpu_custom_call" | custom-call | flops 100000000 | bytes 2000000 | tf_op jit(solution)/shard_map/hidden_and_best/pallas_call | solution.py:359
  41.6 4.4 %backward_last.1 = (bf16[128,1152]{1,0:T(8,128)(2,1)S(1)}, bf16[128,1152]{1,0:T(8,128)(2,1)S(1)}, bf16[256,1152]{1,0:T(8,128)(2,1)S(1)}) custom-call(bf16[512,512]{1,0:T(8,128)(2,1)S(1)} %get-tuple-element.47.flow_ref, bf16[512,1536]{1,0:T(8,128)(2,1)S(1)} %get-tuple-element.48.packed_ref, bf16[4,512,512]{2,1,0:T(8,128)(2,1)S(1)} %get-tuple-element.49.prob_ref, ...), custom_call_target="tpu_custom_call" | custom-call | flops 3000000000 | bytes 6000000 | tf_op jit(solution)/shard_map/backward_last/pallas_call | solution.py:304
  46.2 1.6 %collective-permute-start.13 = (bf16[576,288]{1,0:T(8,128)(2,1)S(1)}, bf16[576,288]{1,0:T(8,128)(2,1)S(1)}, u32[]{:S(2)}, u32[]{:S(2)}) collective-permute-start(bf16[576,288]{1,0:T(8,128)(2,1)S(1)} %get-tuple-element.57), channel_id=1, source_target_pairs={{0,4},{4,0},{8,12},{12,8},{16,20},{20,16},{24,28},{28,24},{1,5},{5... | collective-permute-start | bytes 995336 | tf_op jit(solution)/shard_map/ppermute | solution.py:449
  49.7 9.0 %collective-permute-done.13.got1_ref = bf16[576,288]{1,0:T(8,128)(2,1)S(1)} collective-permute-done((bf16[576,288]{1,0:T(8,128)(2,1)S(1)}, bf16[576,288]{1,0:T(8,128)(2,1)S(1)}, u32[]{:S(2)}, u32[]{:S(2)}) %collective-permute-start.13) | collective-permute-done | bytes 331808 | tf_op jit(solution)/shard_map/ppermute | solution.py:449
  58.8 1.6 %collective-permute-start.14 = (bf16[288,288]{1,0:T(8,128)(2,1)S(1)}, bf16[288,288]{1,0:T(8,128)(2,1)S(1)}, u32[]{:S(2)}, u32[]{:S(2)}) collective-permute-start(bf16[288,288]{1,0:T(8,128)(2,1)S(1)} %add_convert_fusion.2), channel_id=1, source_target_pairs={{0,8},{4,12},{8,0},{12,4},{16,24},{20,28},{24,16},{28,20},{1,9},{5... | collective-permute-start | bytes 497672 | tf_op jit(solution)/shard_map/ppermute | solution.py:449
  60.4 5.3 %collective-permute-done.14.got2_ref = bf16[288,288]{1,0:T(8,128)(2,1)S(1)} collective-permute-done((bf16[288,288]{1,0:T(8,128)(2,1)S(1)}, bf16[288,288]{1,0:T(8,128)(2,1)S(1)}, u32[]{:S(2)}, u32[]{:S(2)}) %collective-permute-start.14) | collective-permute-done | bytes 165920 | tf_op jit(solution)/shard_map/ppermute | solution.py:449
  65.9 2.8 %collective-permute-start.15 = (bf16[144,288]{1,0:T(8,128)(2,1)S(1)}, bf16[144,288]{1,0:T(8,128)(2,1)S(1)}, u32[]{:S(2)}, u32[]{:S(2)}) collective-permute-start(bf16[144,288]{1,0:T(8,128)(2,1)S(1)} %get-tuple-element.60), channel_id=1, source_target_pairs={{0,16},{4,20},{8,24},{12,28},{16,0},{20,4},{24,8},{28,12},{1,17},{... | collective-permute-start | bytes 248840 | tf_op jit(solution)/shard_map/ppermute | solution.py:449
  68.6 4.0 %all-to-all-start = ((f32[32,1,128]{2,1,0:T(1,128)}), f32[32,1,128]{2,1,0:T(1,128)S(1)}, u32[]{:S(2)}, u32[]{:S(2)}) async-start(f32[32,1,128]{2,1,0:T(1,128)} %bitcast.4), calls=%async_computation | async-start | bytes 32768 | tf_op jit(solution)/shard_map/all_to_all | solution.py:532
  73.1 6.7 %all-to-all-done = f32[32,1,128]{2,1,0:T(1,128)S(1)} async-done(((f32[32,1,128]{2,1,0:T(1,128)}), f32[32,1,128]{2,1,0:T(1,128)S(1)}, u32[]{:S(2)}, u32[]{:S(2)}) %all-to-all-start) | async-done | bytes 16416 | tf_op jit(solution)/shard_map/all_to_all | solution.py:532
  79.7 1.8 %norm_back.1 = (bf16[128,1152]{1,0:T(8,128)(2,1)}, f32[144,288]{1,0:T(8,128)}, f32[4,8]{1,0:T(4,128)}, f32[4]{0:T(128)}) custom-call(bf16[128,1152]{1,0:T(8,128)(2,1)S(1)} %copy-done.2, f32[1,1152]{1,0:T(1,128)S(1)} %reshape.19.gain_ref, bf16[128,1152]{1,0:T(8,128)(2,1)S(1)} %copy-done.1, bf16[128,1152]{1,0:T(8,128)(2,1)S(1)} %get-tuple-element.54.part_ref, ...), custom_call_target="tpu_custom_call" | custom-call | flops 3000000 | bytes 2000000 | tf_op jit(solution)/shard_map/norm_back/pallas_call | solution.py:415
  (43 shorter events, 6.8 us)
Async XLA Ops:
  0.6 12.0 %copy-start.6 = (s32[8]{0:T(128)S(1)}, s32[8]{0:T(128)}, u32[]{:S(2)}) copy-start(s32[8]{0:T(128)} %counts_ref.5) | copy-start | bytes 100
  0.6 10.2 %collective-permute-start.1 = (bf16[128,1152]{1,0:T(8,128)(2,1)}, bf16[128,1152]{1,0:T(8,128)(2,1)S(1)}, u32[]{:S(2)}, u32[]{:S(2)}) collective-permute-start(bf16[128,1152]{1,0:T(8,128)(2,1)} %patch_ref.3), channel_id=1, source_target_pairs={{0,2},{1,3},{2,0},{3,1},{4,6},{5,7},{6,4},{7,5},{8,10},{9,11},{10,... | collective-permute-start | bytes 884744 | tf_op jit(solution)/shard_map/ppermute | solution.py:449
  3.7 9.0 %collective-permute-start = (bf16[128,1152]{1,0:T(8,128)(2,1)}, bf16[128,1152]{1,0:T(8,128)(2,1)S(1)}, u32[]{:S(2)}, u32[]{:S(2)}) collective-permute-start(bf16[128,1152]{1,0:T(8,128)(2,1)} %patch_ref.3), channel_id=1, source_target_pairs={{0,1},{1,0},{2,3},{3,2},{4,5},{5,4},{6,7},{7,6},{8,9},{9,8},{10,11... | collective-permute-start | bytes 884744 | tf_op jit(solution)/shard_map/ppermute | solution.py:449
  3.7 1.6 %copy-start = (bf16[1152,864]{0,1:T(8,128)(2,1)S(1)}, bf16[1152,864]{0,1:T(8,128)(2,1)}, u32[]{:S(2)}) copy-start(bf16[1152,864]{0,1:T(8,128)(2,1)} %param.11) | copy-start | bytes 5971972
  7.1 3.8 %copy-start.1 = (bf16[128,1152]{1,0:T(8,128)(2,1)S(1)}, bf16[128,1152]{1,0:T(8,128)(2,1)}, u32[]{:S(2)}) copy-start(bf16[128,1152]{1,0:T(8,128)(2,1)} %grad_ref.1) | copy-start | bytes 884740
  7.1 5.6 %copy-start.8 = (f32[1152]{0:T(1024)S(1)}, f32[1152]{0:T(1024)}, u32[]{:S(2)}) copy-start(f32[1152]{0:T(1024)} %param.10) | copy-start | bytes 13828
  7.1 5.6 %copy-start.2 = (bf16[128,1152]{1,0:T(8,128)(2,1)S(1)}, bf16[128,1152]{1,0:T(8,128)(2,1)}, u32[]{:S(2)}) copy-start(bf16[128,1152]{1,0:T(8,128)(2,1)} %patch_ref.3) | copy-start | bytes 884740
  10.9 1.8 %collective-permute-start.2 = (bf16[128,1152]{1,0:T(8,128)(2,1)S(1)}, bf16[128,1152]{1,0:T(8,128)(2,1)S(1)}, u32[]{:S(2)}, u32[]{:S(2)}) collective-permute-start(bf16[128,1152]{1,0:T(8,128)(2,1)S(1)} %collective-permute-done.1.rows2), channel_id=1, source_target_pairs={{0,1},{1,0},{2,3},{3,2},{4,5},{5,4},{6,7},{7,6},{8,9},{9,8},{10,11... | collective-permute-start | bytes 884744 | tf_op jit(solution)/shard_map/ppermute | solution.py:449
  10.9 10.6 %collective-permute-start.9 = (bf16[128,1152]{1,0:T(8,128)(2,1)S(1)}, bf16[128,1152]{1,0:T(8,128)(2,1)S(1)}, u32[]{:S(2)}, u32[]{:S(2)}) collective-permute-start(bf16[128,1152]{1,0:T(8,128)(2,1)S(1)} %copy-done.1), channel_id=1, source_target_pairs={{0,2},{1,3},{2,0},{3,1},{4,6},{5,7},{6,4},{7,5},{8,10},{9,11},{10,... | collective-permute-start | bytes 884744 | tf_op jit(solution)/shard_map/ppermute | solution.py:449
  18.6 14.4 %collective-permute-start.3 = (bf16[256,1152]{1,0:T(8,128)(2,1)S(1)}, bf16[256,1152]{1,0:T(8,128)(2,1)S(1)}, u32[]{:S(2)}, u32[]{:S(2)}) collective-permute-start(bf16[256,1152]{1,0:T(8,128)(2,1)S(1)} %get-tuple-element.41), channel_id=1, source_target_pairs={{0,1},{1,0},{2,3},{3,2},{4,5},{5,4},{6,7},{7,6},{8,9},{9,8},{10,11... | collective-permute-start | bytes 1769480 | tf_op jit(solution)/shard_map/ppermute | solution.py:449
  18.9 4.8 %collective-permute-start.5 = (bf16[128,128]{1,0:T(8,128)(2,1)S(1)}, bf16[128,128]{1,0:T(8,128)(2,1)S(1)}, u32[]{:S(2)}, u32[]{:S(2)}) collective-permute-start(bf16[128,128]{1,0:T(8,128)(2,1)S(1)} %get-tuple-element.36), channel_id=1, source_target_pairs={{0,16},{4,20},{8,24},{12,28},{16,0},{20,4},{24,8},{28,12},{1,17},{... | collective-permute-start | bytes 98312 | tf_op jit(solution)/shard_map/ppermute | solution.py:449
  21.5 8.2 %collective-permute-start.8 = (bf16[128,1152]{1,0:T(8,128)(2,1)S(1)}, bf16[128,1152]{1,0:T(8,128)(2,1)S(1)}, u32[]{:S(2)}, u32[]{:S(2)}) collective-permute-start(bf16[128,1152]{1,0:T(8,128)(2,1)S(1)} %copy-done.1), channel_id=1, source_target_pairs={{0,1},{1,0},{2,3},{3,2},{4,5},{5,4},{6,7},{7,6},{8,9},{9,8},{10,11... | collective-permute-start | bytes 884744 | tf_op jit(solution)/shard_map/ppermute | solution.py:449
  21.5 8.1 %collective-permute-start.10 = (bf16[128,1152]{1,0:T(8,128)(2,1)S(1)}, bf16[128,1152]{1,0:T(8,128)(2,1)S(1)}, u32[]{:S(2)}, u32[]{:S(2)}) collective-permute-start(bf16[128,1152]{1,0:T(8,128)(2,1)S(1)} %collective-permute-done.9.grad2), channel_id=1, source_target_pairs={{0,1},{1,0},{2,3},{3,2},{4,5},{5,4},{6,7},{7,6},{8,9},{9,8},{10,11... | collective-permute-start | bytes 884744 | tf_op jit(solution)/shard_map/ppermute | solution.py:449
  23.7 4.3 %collective-permute-start.6 = (bf16[256,128]{1,0:T(8,128)(2,1)S(1)}, bf16[256,128]{1,0:T(8,128)(2,1)S(1)}, u32[]{:S(2)}, u32[]{:S(2)}) collective-permute-start(bf16[256,128]{1,0:T(8,128)(2,1)S(1)} %pad_maximum_fusion.2), channel_id=1, source_target_pairs={{0,4},{4,0},{8,12},{12,8},{16,20},{20,16},{24,28},{28,24},{1,5},{5... | collective-permute-start | bytes 196616 | tf_op jit(solution)/shard_map/ppermute | solution.py:449
  28.0 5.0 %collective-permute-start.7 = (bf16[512,128]{1,0:T(8,128)(2,1)S(1)}, bf16[512,128]{1,0:T(8,128)(2,1)S(1)}, u32[]{:S(2)}, u32[]{:S(2)}) collective-permute-start(bf16[512,128]{1,0:T(8,128)(2,1)S(1)} %pad_maximum_fusion.1), channel_id=1, source_target_pairs={{0,8},{4,12},{8,0},{12,4},{16,24},{20,28},{24,16},{28,20},{1,9},{5... | collective-permute-start | bytes 393224 | tf_op jit(solution)/shard_map/ppermute | solution.py:449
  33.1 6.8 %collective-permute-start.4 = (bf16[128,1152]{1,0:T(8,128)(2,1)S(1)}, bf16[128,1152]{1,0:T(8,128)(2,1)S(1)}, u32[]{:S(2)}, u32[]{:S(2)}) collective-permute-start(bf16[128,1152]{1,0:T(8,128)(2,1)S(1)} %add_convert_fusion.1), channel_id=1, source_target_pairs={{0,2},{1,3},{2,0},{3,1},{4,6},{5,7},{6,4},{7,5},{8,10},{9,11},{10,... | collective-permute-start | bytes 884744 | tf_op jit(solution)/shard_map/ppermute | solution.py:449
  34.6 5.3 %copy-start.4 = (bf16[1152,128]{1,0:T(8,128)(2,1)S(1)}, bf16[1152,128]{1,0:T(8,128)(2,1)}, u32[]{:S(2)}) copy-start(bf16[1152,128]{1,0:T(8,128)(2,1)} %embed_ref.1) | copy-start | bytes 884740
  46.1 33.7 %copy-start.7 = (s32[4]{0:T(128)S(1)}, s32[4]{0:T(128)}, u32[]{:S(2)}) copy-start(s32[4]{0:T(128)} %refs_3_.1) | copy-start | bytes 52
  46.1 2.1 %collective-permute-start.11 = (bf16[256,1152]{1,0:T(8,128)(2,1)S(1)}, bf16[256,1152]{1,0:T(8,128)(2,1)S(1)}, u32[]{:S(2)}, u32[]{:S(2)}) collective-permute-start(bf16[256,1152]{1,0:T(8,128)(2,1)S(1)} %get-tuple-element.55), channel_id=1, source_target_pairs={{0,1},{1,0},{2,3},{3,2},{4,5},{5,4},{6,7},{7,6},{8,9},{9,8},{10,11... | collective-permute-start | bytes 1769480 | tf_op jit(solution)/shard_map/ppermute | solution.py:449
  46.2 12.6 %collective-permute-start.13 = (bf16[576,288]{1,0:T(8,128)(2,1)S(1)}, bf16[576,288]{1,0:T(8,128)(2,1)S(1)}, u32[]{:S(2)}, u32[]{:S(2)}) collective-permute-start(bf16[576,288]{1,0:T(8,128)(2,1)S(1)} %get-tuple-element.57), channel_id=1, source_target_pairs={{0,4},{4,0},{8,12},{12,8},{16,20},{20,16},{24,28},{28,24},{1,5},{5... | collective-permute-start | bytes 995336 | tf_op jit(solution)/shard_map/ppermute | solution.py:449
  48.2 31.5 %collective-permute-start.12 = (bf16[128,1152]{1,0:T(8,128)(2,1)S(1)}, bf16[128,1152]{1,0:T(8,128)(2,1)S(1)}, u32[]{:S(2)}, u32[]{:S(2)}) collective-permute-start(bf16[128,1152]{1,0:T(8,128)(2,1)S(1)} %add_convert_fusion), channel_id=1, source_target_pairs={{0,2},{1,3},{2,0},{3,1},{4,6},{5,7},{6,4},{7,5},{8,10},{9,11},{10,... | collective-permute-start | bytes 884744 | tf_op jit(solution)/shard_map/ppermute | solution.py:449
  58.8 7.0 %collective-permute-start.14 = (bf16[288,288]{1,0:T(8,128)(2,1)S(1)}, bf16[288,288]{1,0:T(8,128)(2,1)S(1)}, u32[]{:S(2)}, u32[]{:S(2)}) collective-permute-start(bf16[288,288]{1,0:T(8,128)(2,1)S(1)} %add_convert_fusion.2), channel_id=1, source_target_pairs={{0,8},{4,12},{8,0},{12,4},{16,24},{20,28},{24,16},{28,20},{1,9},{5... | collective-permute-start | bytes 497672 | tf_op jit(solution)/shard_map/ppermute | solution.py:449
  65.9 7.2 %collective-permute-start.15 = (bf16[144,288]{1,0:T(8,128)(2,1)S(1)}, bf16[144,288]{1,0:T(8,128)(2,1)S(1)}, u32[]{:S(2)}, u32[]{:S(2)}) collective-permute-start(bf16[144,288]{1,0:T(8,128)(2,1)S(1)} %get-tuple-element.60), channel_id=1, source_target_pairs={{0,16},{4,20},{8,24},{12,28},{16,0},{20,4},{24,8},{28,12},{1,17},{... | collective-permute-start | bytes 248840 | tf_op jit(solution)/shard_map/ppermute | solution.py:449
  68.6 11.1 %all-to-all-start = ((f32[32,1,128]{2,1,0:T(1,128)}), f32[32,1,128]{2,1,0:T(1,128)S(1)}, u32[]{:S(2)}, u32[]{:S(2)}) async-start(f32[32,1,128]{2,1,0:T(1,128)} %bitcast.4), calls=%async_computation | async-start | bytes 32768 | tf_op jit(solution)/shard_map/all_to_all | solution.py:532
  (2 other events, 1.8 us)

commit v4 on v3

v4 whole, which is shorter than its diff:
```python
from functools import partial
import math

import jax
import jax.numpy as jnp
from jax import lax
from jax.experimental import pallas as pl
from jax.experimental.pallas import tpu as pltpu
from jax.sharding import PartitionSpec as P


HEAD_DIM = 72
LANES = 128
HEAD_LANES = 256
EMB = 128
QTOK = 32
MP = 4
DISTANCES = (4, 1, 2)
ARRIVAL = (0, 4, 1, 5, 2, 6, 3, 7)
SCALE = HEAD_DIM ** (-0.5)
LOG2E = math.log2(math.e)
F32 = jnp.float32
BF16 = jnp.bfloat16

HBM = pl.BlockSpec(memory_space=pltpu.HBM)
VMEM = pl.BlockSpec(memory_space=pltpu.VMEM)
SMEM = pl.BlockSpec(memory_space=pltpu.SMEM)


def dot(left, right, left_dim, right_dim):
    return lax.dot_general(
        left, right, (((left_dim,), (right_dim,)), ((), ())), preferred_element_type=F32
    )


def shape(dims, kind):
    return jax.ShapeDtypeStruct(dims, kind)


def cost(flops, size, exps=0):
    return pl.CostEstimate(flops=int(flops), bytes_accessed=int(size), transcendentals=int(exps))


def grant(mebibytes):
    return pltpu.CompilerParams(vmem_limit_bytes=mebibytes * 1024 * 1024)


def full(*dims):
    return pl.BlockSpec(dims, lambda *_: (0,) * len(dims))


def unit_rows(values):
    return values * lax.rsqrt(jnp.sum(values * values, axis=-1, keepdims=True) + 1e-06)


def place_of(index, model_index, rows_dev):
    return (model_index ^ (index // rows_dev)) * rows_dev + index % rows_dev


def gain_row(gain_ref):
    return jnp.concatenate([gain_ref[row : row + 1, :] for row in range(gain_ref.shape[0])], axis=1)


def norm_rows(block, gain):
    values = block.astype(F32)
    center = values - jnp.mean(values, axis=-1, keepdims=True)
    spread = jnp.mean(center * center, axis=-1, keepdims=True)
    return (center * lax.rsqrt(spread + 1e-06) * gain).astype(BF16)


def prepare_kernel(
    heads, rows_hbm, gain_hbm, mixing_hbm, output_hbm, rows1, mixing_pad, output_pad, packed_ref,
    rows0, gain_ref, mixing_ref, output_ref, normed, sems
):
    def spread(source, target, index, size, room):
        target[index * room : index * room + size, :] = source[index * size : (index + 1) * size, :]
        target[index * room + size : (index + 1) * room, :] = jnp.zeros(
            (room - size, target.shape[1]), BF16
        )

    sources = (rows_hbm, gain_hbm, mixing_hbm, output_hbm)
    targets = (rows0, gain_ref, mixing_ref, output_ref)
    fetches = [
        pltpu.make_async_copy(source, target, sems.at[index])
        for index, (source, target) in enumerate(zip(sources, targets))
    ]
    for fetch in fetches:
        fetch.start()
    fetches[0].wait()
    fetches[1].wait()
    size = rows0.shape[0]
    gain = gain_row(gain_ref)
    for index, block in enumerate((rows0, rows1)):
        normed[index * size : (index + 1) * size, :] = norm_rows(block[...], gain)
    fetches[2].wait()
    for index in range(heads):
        spread(mixing_ref, mixing_pad, index, 3 * HEAD_DIM, HEAD_LANES)
    fetches[3].wait()
    for index in range(heads):
        spread(output_ref, output_pad, index, HEAD_DIM, LANES)
    packed_ref[...] = dot(normed[...], mixing_pad[...], 1, 1).astype(BF16)


def in_hbm(values):
    return pltpu.with_memory_space_constraint(values, pltpu.HBM)


def prepare(mixing, output, rows0, rows1, gain, heads):
    width = mixing.shape[1]
    size = 2 * rows0.shape[0]
    return pl.pallas_call(
        partial(prepare_kernel, heads),
        out_shape=(
            shape((heads * HEAD_LANES, width), BF16),
            shape((heads * LANES, width), BF16),
            shape((size, heads * HEAD_LANES), BF16),
        ),
        in_specs=[HBM] * 4 + [VMEM],
        out_specs=(VMEM,) * 3,
        scratch_shapes=[
            pltpu.VMEM(rows0.shape, BF16),
            pltpu.VMEM(gain.shape, F32),
            pltpu.VMEM(mixing.shape, BF16),
            pltpu.VMEM(output.shape, BF16),
            pltpu.VMEM((size, width), BF16),
            pltpu.SemaphoreType.DMA((4,)),
        ],
        cost_estimate=cost(1e9, 8e6),
        name="prepare",
        compiler_params=grant(24),
    )(in_hbm(rows0), in_hbm(gain), in_hbm(mixing), in_hbm(output), rows1)


def head_parts(packed_ref, head):
    start = head * HEAD_LANES
    ends = [start + index * HEAD_DIM for index in range(4)]
    return [packed_ref[:, low:high] for low, high in zip(ends, ends[1:])]


def hand_out(product, keep0, keep2, send):
    size = keep0.shape[0]
    keep0[...] = product[:size].astype(BF16)
    send[:size, :] = product[size : 2 * size].astype(BF16)
    keep2[...] = product[2 * size : 3 * size].astype(BF16)
    send[size:, :] = product[3 * size :].astype(BF16)


def forward_kernel(
    heads,
    rows_dev,
    counts_ref,
    early_ref,
    rows2,
    rows3,
    gain_ref,
    mixing_ref,
    output_ref,
    packed_ref,
    prob_ref,
    attended_ref,
    keep0,
    keep2,
    send,
    normed,
):
    rows = rows_dev * MP
    gain = gain_row(gain_ref)
    for index, block in enumerate((rows2, rows3)):
        normed[index * rows_dev : (index + 1) * rows_dev, :] = norm_rows(block[...], gain)
    half = 2 * rows_dev
    packed_ref[:half, :] = early_ref[...]
    packed_ref[half:, :] = dot(normed[...], mixing_ref[...], 1, 1).astype(BF16)
    count = counts_ref[lax.axis_index("dp")]
    model_index = lax.axis_index("mp")
    columns = lax.broadcasted_iota(jnp.int32, (1, rows), 1)
    seen = place_of(columns, model_index, rows_dev) < count
    lines = lax.broadcasted_iota(jnp.int32, (rows, 1), 0)
    live = place_of(lines, model_index, rows_dev) < count
    for head in range(heads):
        query, key, value = head_parts(packed_ref, head)
        score = dot(query, key, 1, 1)
        score = jnp.where(seen, score, -1e30)
        largest = jnp.max(score, axis=-1, keepdims=True)
        raised = jnp.exp2((score - largest) * (SCALE * LOG2E))
        total = jnp.sum(raised, axis=-1, keepdims=True)
        prob = (raised * (1.0 / total)).astype(BF16)
        prob_ref[head] = prob
        found = dot(prob, value, 1, 0)
        start = head * LANES
        attended_ref[:, start : start + HEAD_DIM] = jnp.where(live, found, 0.0).astype(BF16)
        attended_ref[:, start + HEAD_DIM : start + LANES] = jnp.zeros(
            (rows, LANES - HEAD_DIM), BF16
        )
    hand_out(dot(attended_ref[...], output_ref[...], 1, 0), keep0, keep2, send)


def handed_shapes(rows_dev, width):
    kept = shape((rows_dev, width), BF16)
    return (kept, kept, shape((2 * rows_dev, width), BF16))


def forward(counts, early, blocks, gain, mixing_pad, output_pad, heads):
    rows_dev, width = blocks[0].shape
    rows = rows_dev * MP
    return pl.pallas_call(
        partial(forward_kernel, heads, rows_dev),
        out_shape=(
            shape((rows, heads * HEAD_LANES), BF16),
            shape((heads, rows, rows), BF16),
            shape((rows, heads * LANES), BF16),
        )
        + handed_shapes(rows_dev, width),
        in_specs=[SMEM] + [VMEM] * 6,
        out_specs=(VMEM,) * 6,
        scratch_shapes=[pltpu.VMEM((2 * rows_dev, width), BF16)],
        cost_estimate=cost(3e9, 12e6, heads * rows * rows),
        name="forward_attention",
        compiler_params=grant(28),
    )(counts, early, *blocks, gain, mixing_pad, output_pad)


def weight_kernel(
    heads, rows_dev, order, grad0, grad1, grad2, grad3, attended_ref, *refs
):
    (stacked, *outs), (result,) = refs[: len(refs) - 1], refs[len(refs) - 1 :]
    for index, block in enumerate((grad0, grad1, grad2, grad3)):
        stacked[index * rows_dev : (index + 1) * rows_dev, :] = block[...]
    product = dot(stacked[...], attended_ref[...], 0, 0)
    for index in range(heads):
        result[:, index * HEAD_DIM : (index + 1) * HEAD_DIM] = product[
            :, index * LANES : index * LANES + HEAD_DIM
        ]
    if order is None:
        outs[0][...] = result[...]
    else:
        mine = lax.axis_index("dp")
        share = result.shape[0] // sum(len(group) for group in order)
        for group, out in zip(order, outs):
            for spot, piece in enumerate(group):
                start = pl.multiple_of((mine ^ piece) * share, 16)
                out[spot * share : (spot + 1) * share, :] = result[
                    pl.ds(start, share), :
                ].astype(out.dtype)


def weight_parts(grads, attended, order):
    rows_dev, width = grads[0].shape
    heads = attended.shape[1] // LANES
    narrow = heads * HEAD_DIM
    if order is None:
        outs = (shape((width, narrow), F32),)
    else:
        share = width // sum(len(group) for group in order)
        outs = tuple(
            shape((len(group) * share, narrow), F32 if index == 0 else BF16)
            for index, group in enumerate(order)
        )
    outs = (shape((rows_dev * MP, width), BF16),) + outs
    return pl.pallas_call(
        partial(weight_kernel, heads, rows_dev, order),
        out_shape=outs,
        in_specs=[VMEM] * (MP + 1),
        out_specs=(VMEM,) * len(outs),
        scratch_shapes=[pltpu.VMEM((width, narrow), F32)],
        cost_estimate=cost(7e8, 4e6),
        name="weight_parts",
        compiler_params=grant(20),
    )(*grads, attended)


def backward_kernel(heads, counts_ref, stacked_ref, output_ref, packed_ref, prob_ref, out_ref):
    rows = stacked_ref.shape[0]
    count = counts_ref[lax.axis_index("dp")]
    lines = lax.broadcasted_iota(jnp.int32, (rows, 1), 0)
    live = place_of(lines, lax.axis_index("mp"), rows // MP) < count
    flows = dot(stacked_ref[...], output_ref[...], 1, 1)
    flows = jnp.where(live, flows, 0.0).astype(BF16)
    for head in range(heads):
        flow = flows[:, head * LANES : head * LANES + HEAD_DIM]
        query, key, value = head_parts(packed_ref, head)
        weights = prob_ref[head]
        prob = weights.astype(F32)
        grad_prob = dot(flow, value, 1, 1)
        delta = jnp.sum(grad_prob * prob, axis=-1, keepdims=True)
        grad_score = (prob * (grad_prob - delta)).astype(BF16)
        parts = (
            (dot(grad_score, key, 1, 0) * SCALE).astype(BF16),
            (dot(grad_score, query, 0, 0) * SCALE).astype(BF16),
            dot(weights, flow, 0, 0).astype(BF16),
            jnp.zeros((rows, HEAD_LANES - 3 * HEAD_DIM), BF16),
        )
        out_ref[:, head * HEAD_LANES : (head + 1) * HEAD_LANES] = jnp.concatenate(parts, axis=1)


def backward(counts, stacked, output_pad, packed, probs):
    heads, rows, _ = probs.shape
    return pl.pallas_call(
        partial(backward_kernel, heads),
        out_shape=shape((rows, heads * HEAD_LANES), BF16),
        in_specs=[SMEM] + [VMEM] * 4,
        out_specs=VMEM,
        cost_estimate=cost(4e9, 6e6),
        name="backward_attention",
        compiler_params=grant(28),
    )(counts, stacked, output_pad, packed, probs)


def branch_kernel(joined_ref, mixing_ref, keep0, keep2, send):
    hand_out(dot(joined_ref[...], mixing_ref[...], 1, 0), keep0, keep2, send)


def input_branch(joined, mixing_pad):
    return pl.pallas_call(
        branch_kernel,
        out_shape=handed_shapes(joined.shape[0] // MP, mixing_pad.shape[1]),
        in_specs=[VMEM] * 2,
        out_specs=(VMEM,) * 3,
        cost_estimate=cost(2e9, 8e6),
        name="input_branch",
        compiler_params=grant(24),
    )(joined, mixing_pad)


def score_kernel(
    rows_dev, few, counts_ref, patch_ref, part_ref, near_ref, far_ref, embed_ref, tokens_ref,
    hidden_ref, best_ref, page_emb
):
    mine = lax.axis_index("dp")

    def embed():
        near = near_ref[: part_ref.shape[0], :]
        mixed = part_ref[...].astype(F32) + near.astype(F32) + far_ref[...].astype(F32)
        hidden = (patch_ref[...].astype(F32) + mixed).astype(BF16)
        hidden_ref[...] = hidden
        embedded = dot(hidden, embed_ref[...], 1, 0)
        page_emb[...] = unit_rows(embedded).astype(BF16)

    if few:
        embed()
    else:
        pl.when(pl.program_id(0) == 0)(embed)
    tokens = unit_rows(tokens_ref[...].astype(F32)).astype(BF16)
    similar = dot(page_emb[...], tokens, 1, 1)
    lines = lax.broadcasted_iota(jnp.int32, (rows_dev, 1), 0) + lax.axis_index("mp") * rows_dev
    similar = jnp.where(lines < counts_ref[mine], similar, -2.0)
    best = jnp.max(similar, axis=0, keepdims=True)
    if few:
        size = best_ref.shape[1]
        for piece in range(best.shape[1] // size):
            row = best[:, piece * size : (piece + 1) * size]
            for copy in range(MP):
                best_ref[pl.ds((mine ^ ARRIVAL[piece]) * MP + copy, 1), :] = row
    else:
        best_ref[...] = best


def hidden_and_best(counts, patches, part, received, far, embed_weight, tokens, few, local):
    rows_dev, width = patches.shape
    size = tokens.shape[0]
    chunk = size if few else math.gcd(size, 1024)
    block = full(rows_dev, width)
    if few:
        best_shape = shape((size // local * MP, local), F32)
        layout = dict(in_specs=[SMEM] + [VMEM] * 6, out_specs=(VMEM, VMEM))
    else:
        best_shape = shape((1, size), F32)
        layout = dict(
            grid=(size // chunk,),
            in_specs=[SMEM]
            + [block] * 4
            + [full(width, EMB), pl.BlockSpec((chunk, EMB), lambda index: (index, 0))],
            out_specs=(block, pl.BlockSpec((1, chunk), lambda index: (0, index))),
        )
    return pl.pallas_call(
        partial(score_kernel, rows_dev, few),
        **layout,
        out_shape=(shape((rows_dev, width), BF16), best_shape),
        scratch_shapes=[pltpu.VMEM((rows_dev, EMB), BF16)],
        cost_estimate=cost(1e8, 2e6),
        name="hidden_and_best",
        compiler_params=grant(12),
    )(counts, patches, part, received, far, embed_weight, tokens)


def norm_back_kernel(patch_ref, gain_ref, grad_ref, part_ref, near_ref, far_ref, *refs):
    values = patch_ref[...].astype(F32)
    center = values - jnp.mean(values, axis=-1, keepdims=True)
    spread = jnp.mean(center * center, axis=-1, keepdims=True)
    inverse = lax.rsqrt(spread + 1e-06)
    near = near_ref[: part_ref.shape[0], :]
    flow = part_ref[...].astype(F32) + near.astype(F32) + far_ref[...].astype(F32)
    flow = flow * gain_row(gain_ref)
    along = jnp.mean(flow * center, axis=-1, keepdims=True)
    level = jnp.mean(flow, axis=-1, keepdims=True)
    result = inverse * (flow - level - center * (inverse * inverse * along))
    out = (grad_ref[...].astype(F32) + result).astype(BF16)
    if len(refs) == 1:
        refs[0][...] = out
        return
    mine_ref, other_ref, found_ref, positive_ref, out_ref, weight_ref, score_ref, loss_ref = refs
    out_ref[...] = out
    weight_ref[...] = mine_ref[...] + other_ref[...].astype(F32)
    pages = found_ref.shape[0] // MP
    best = jnp.max(found_ref[...].reshape(pages, MP, found_ref.shape[1]), axis=1)
    turned = best.T
    columns = lax.broadcasted_iota(jnp.int32, (1, pages), 1)
    for query in range(score_ref.shape[0]):
        row = jnp.sum(turned[query * QTOK : (query + 1) * QTOK], axis=0, keepdims=True)
        score_ref[query : query + 1, :] = row
        chosen = columns == positive_ref[query]
        positive = jnp.sum(jnp.where(chosen, row, 0.0), axis=1, keepdims=True)
        negative = jnp.max(jnp.where(chosen, -1e30, row), axis=1, keepdims=True)
        gap = negative - positive
        loss = jnp.maximum(gap, 0.0) + jnp.log1p(jnp.exp(-jnp.abs(gap)))
        loss_ref[query] = loss[0, 0]


def norm_back(patches, gain, grads, part, near, far, more=()):
    out_shape, out_specs, specs = [shape(patches.shape, BF16)], [VMEM], []
    if more:
        mine, _, found, positive = more
        scores = (positive.shape[0], found.shape[0] // MP)
        specs = [VMEM, VMEM, VMEM, SMEM]
        out_shape += [shape(mine.shape, F32), shape(scores, F32), shape(positive.shape, F32)]
        out_specs += [VMEM, VMEM, SMEM]
    return pl.pallas_call(
        norm_back_kernel,
        out_shape=tuple(out_shape),
        in_specs=[VMEM] * 6 + specs,
        out_specs=tuple(out_specs),
        cost_estimate=cost(3e6, 2e6),
        name="norm_back",
        compiler_params=grant(12),
    )(patches, gain, grads, part, near, far, *more)


def join_kernel(kept_ref, got1_ref, got2_ref, mine_ref, send_ref):
    half, share = kept_ref.shape[0], mine_ref.shape[0]
    total = kept_ref[...] + got1_ref[:half, :].astype(F32) + got2_ref[...].astype(F32)
    mine_ref[...] = total[:share]
    send_ref[...] = total[share:].astype(BF16)


def join_parts(kept, got1, got2):
    share = (kept.shape[0] // 2, kept.shape[1])
    return pl.pallas_call(
        join_kernel,
        out_shape=(shape(share, F32), shape(share, BF16)),
        in_specs=[VMEM] * 3,
        out_specs=(VMEM,) * 2,
        cost_estimate=cost(3e5, 1e6),
        name="join_parts",
        compiler_params=grant(6),
    )(kept, got1, got2)


def swap(values, axis, distance):
    size = lax.axis_size(axis)
    return lax.ppermute(values, axis, [(index, index ^ distance) for index in range(size)])


def scatter_sum(parts):
    part0, part2, send = parts
    received = swap(send, "mp", 1)
    relayed = received[part2.shape[0] :]
    going = (part2.astype(F32) + relayed.astype(F32)).astype(BF16)
    return part0, received, swap(going, "mp", 2), going


def after(values, *others):
    return lax.optimization_barrier((values, *others))[0]


def body(
    patches,
    norm_gain,
    query_key_value,
    output_weight,
    embed_weight,
    query_tokens,
    patch_counts,
    positive_page,
    hidden_grad,
):
    data_index = lax.axis_index("dp")
    data_size = lax.axis_size("dp")
    few = data_size == 8
    heads = output_weight.shape[1] // HEAD_DIM
    gain = norm_gain.reshape(-1, LANES)

    rows2 = swap(patches, "mp", 2)
    rows1 = swap(patches, "mp", 1)
    grads2 = swap(hidden_grad, "mp", 2)
    grads1 = swap(hidden_grad, "mp", 1)

    local = query_tokens.shape[0]
    own_tokens = query_tokens.reshape(local * QTOK, EMB)
    mixing_pad, output_pad, early = prepare(
        query_key_value.T, output_weight.T, patches, rows1, gain, heads
    )
    if few:
        tokens = own_tokens
        for distance in DISTANCES[:2]:
            other = swap(tokens, "dp", distance)
            tokens = jnp.concatenate([tokens, other], axis=0)
    else:
        tokens = lax.all_gather(own_tokens, "dp", axis=0, tiled=True)
    rows2 = after(rows2, early)
    rows3 = swap(rows2, "mp", 1)

    packed, probs, attended, *parts = forward(
        patch_counts, early, (rows2, rows3), gain, mixing_pad, output_pad, heads
    )
    grads3 = swap(after(grads2, rows3), "mp", 1)
    grads = (hidden_grad, grads1, grads2, grads3)
    part, received, far, _ = scatter_sum(parts)
    if few:
        order = ((0, 4), (2, 6), (1, 5, 3, 7))
        stacked, kept, second, first = weight_parts(grads, attended, order)
        got1 = swap(first, "dp", 1)
        other = swap(tokens, "dp", 2)
        near_tokens = tokens
        joined = backward(patch_counts, stacked, output_pad, packed, probs)
        tokens = jnp.concatenate([after(near_tokens, joined), after(other, joined)], axis=0)
    else:
        stacked, whole = weight_parts(grads, attended, None)
        weight_grad = lax.psum_scatter(whole, "dp", scatter_dimension=0, tiled=True)
        joined = backward(patch_counts, stacked, output_pad, packed, probs)
    hidden, best = hidden_and_best(
        patch_counts, patches, part, received, far, embed_weight, tokens, few, local * QTOK
    )
    if few:
        joined, best = lax.optimization_barrier((joined, best))
    grad_parts = input_branch(joined, mixing_pad)
    part, received, far, sent = scatter_sum(grad_parts)
    more = ()
    if few:
        going = (second.astype(F32) + got1[kept.shape[0] :].astype(F32)).astype(BF16)
        got2 = swap(going, "dp", 2)
        mine, send = join_parts(kept, got1, got2)
        other = swap(send, "dp", 4)
        found = lax.all_to_all(after(best, sent), ("dp", "mp"), 0, 0, tiled=True)
        more = (mine, other, found, positive_page)
    patch_grad, *rest = norm_back(patches, gain, hidden_grad, part, received, far, more)
    if few:
        return (hidden, patch_grad, *rest)
    best = jnp.maximum(best, swap(best, "mp", 1))
    best = jnp.maximum(best, swap(best, "mp", 2))
    part_scores = jnp.sum(best.reshape(-1, QTOK), axis=1)
    every = lax.all_gather(part_scores.reshape(-1, 1), "dp", axis=1, tiled=True)
    my_scores = lax.dynamic_slice_in_dim(every, data_index * local, local, 0)
    columns = jnp.arange(my_scores.shape[1], dtype=jnp.int32)
    chosen = columns[None, :] == positive_page[:, None]
    positive_score = jnp.sum(jnp.where(chosen, my_scores, 0.0), axis=1)
    negative_score = jnp.max(jnp.where(chosen, -1e30, my_scores), axis=1)
    loss = jax.nn.softplus(negative_score - positive_score)
    return (hidden, patch_grad, weight_grad, my_scores, loss)


def solution(mesh):
    return jax.shard_map(
        body,
        mesh=mesh,
        in_specs=(
            P(("dp", "mp"), None),
            P(),
            P(None, "mp"),
            P(None, "mp"),
            P(),
            P("dp", None, None),
            P(),
            P("dp"),
            P(("dp", "mp"), None),
        ),
        out_specs=(
            P(("dp", "mp"), None),
            P(("dp", "mp"), None),
            P("dp", "mp"),
            P("dp", None),
            P("dp"),
        ),
        check_vma=False,
    )
```

time: 82 us -> 76 us (0.927)
  local copies, waits for them, and re-layouts: 3.43 us -> 0.03 us
  starting transfers between devices: 24.4 us -> 23 us
  waiting for transfers between devices: 33.4 us -> 32.5 us
    unnamed x18 -> x14, local copies, waits for them, and re-layouts: 3.43 us -> 0.03 us
    pallas_call x1, Pallas kernels: 2.36 us -> 1.16 us  [weight_parts(): pl.pallas_call(partial(weight_kernel, heads, rows_dev, order), out_shape=...]
    all_to_all x1, starting transfers between devices: 3.99 us -> 2.87 us  [body(): found = lax.all_to_all(after(best, sent), ('dp', 'mp'), 0, 0, tiled=True)]
    pallas_call x6, Pallas kernels: 16.9 us -> 17.9 us  [the longest x1 5.06 us: backward(): pl.pallas_call(partial(backward_kernel, heads), out_shape=shape((rows, he...]
  transfers between devices with their start and end apart: 17 -> 17, of which waited for: 10 -> 9; matrix products, arithmetic and copies ran while one was open for 0% -> 0% of each run, Pallas kernels for 14% -> 19%
where the time goes in v4:
time: 76 us; the launch traced here: 75.8 us
  waiting for transfers between devices  32.5 us (43%)
  starting transfers between devices  23 us (30%)
  Pallas kernels  19.1 us (25%)
  between operations  0.79 us (1%)
    ppermute x16, waiting for transfers between devices, swap(): lax.ppermute(values, axis, [(index, index ^ distance) for index in range(...  26.6 us
    ppermute x16, starting transfers between devices, swap(): lax.ppermute(values, axis, [(index, index ^ distance) for index in range(...  20.2 us
    all_to_all x1, waiting for transfers between devices, body(): found = lax.all_to_all(after(best, sent), ('dp', 'mp'), 0, 0, tiled=True)  5.93 us
    pallas_call x1, Pallas kernels, backward(): pl.pallas_call(partial(backward_kernel, heads), out_shape=shape((rows, he...  5.06 us
    pallas_call x1, Pallas kernels, forward(): pl.pallas_call(partial(forward_kernel, heads, rows_dev), out_shape=(shape...  4.93 us
    all_to_all x1, starting transfers between devices, body(): found = lax.all_to_all(after(best, sent), ('dp', 'mp'), 0, 0, tiled=True)  2.87 us
    pallas_call x1, Pallas kernels, prepare(): pl.pallas_call(partial(prepare_kernel, heads), out_shape=(shape((heads *...  2.84 us
    pallas_call x1, Pallas kernels, norm_back(): pl.pallas_call(norm_back_kernel, out_shape=tuple(out_shape), in_specs=[VM...  1.83 us
  transfers between devices with their start and end apart: 17, of which 9 were waited for; matrix products, arithmetic and copies ran while one was open for 0% of the time, Pallas kernels for 19%

profile of v4, /device:TPU:0, one launch (start us, length us, event | category | flops | bytes accessed | tf_op | source)
XLA Modules:
  0.0 75.8 jit_solution(15007514306042244239)
XLA Ops:
  1.2 2.6 %collective-permute-start.1 = (bf16[128,1152]{1,0:T(8,128)(2,1)}, bf16[128,1152]{1,0:T(8,128)(2,1)S(1)}, u32[]{:S(2)}, u32[]{:S(2)}) collective-permute-start(bf16[128,1152]{1,0:T(8,128)(2,1)} %patch_ref.3), channel_id=1, source_target_pairs={{0,2},{1,3},{2,0},{3,1},{4,6},{5,7},{6,4},{7,5},{8,10},{9,11},{10,... | collective-permute-start | bytes 884744 | tf_op jit(solution)/shard_map/ppermute | solution.py:459
  3.8 2.8 %prepare.1 = (bf16[1024,1152]{1,0:T(8,128)(2,1)S(1)}, bf16[512,1152]{1,0:T(8,128)(2,1)S(1)}, bf16[256,1024]{1,0:T(8,128)(2,1)S(1)}) custom-call(bf16[128,1152]{1,0:T(8,128)(2,1)} %patch_ref.3, f32[9,128]{1,0:T(8,128)} %bitcast.9, bf16[864,1152]{1,0:T(8,128)(2,1)} %bitcast.15, bf16[288,1152]{1,0:T(8,128)(2,1)} %bitcast.16, ...), custom_call_target="tpu_custom_call" | custom-call | flops 1000000000 | bytes 8000000 | tf_op jit(solution)/shard_map/prepare/pallas_call | solution.py:111
  6.6 5.0 %collective-permute-done.1.rows2 = bf16[128,1152]{1,0:T(8,128)(2,1)S(1)} collective-permute-done((bf16[128,1152]{1,0:T(8,128)(2,1)}, bf16[128,1152]{1,0:T(8,128)(2,1)S(1)}, u32[]{:S(2)}, u32[]{:S(2)}) %collective-permute-start.1) | collective-permute-done | bytes 294944 | tf_op jit(solution)/shard_map/ppermute | solution.py:459
  11.6 1.7 %collective-permute-start.8 = (bf16[128,1152]{1,0:T(8,128)(2,1)S(1)}, bf16[128,1152]{1,0:T(8,128)(2,1)S(1)}, u32[]{:S(2)}, u32[]{:S(2)}) collective-permute-start(bf16[128,1152]{1,0:T(8,128)(2,1)S(1)} %copy-done.1), channel_id=1, source_target_pairs={{0,2},{1,3},{2,0},{3,1},{4,6},{5,7},{6,4},{7,5},{8,10},{9,11},{10,... | collective-permute-start | bytes 884744 | tf_op jit(solution)/shard_map/ppermute | solution.py:459
  13.4 4.9 %forward_attention.1 = (bf16[512,1024]{1,0:T(8,128)(2,1)S(1)}, bf16[4,512,512]{2,1,0:T(8,128)(2,1)S(1)}, bf16[512,512]{1,0:T(8,128)(2,1)S(1)}, bf16[128,1152]{1,...) custom-call(s32[8]{0:T(128)S(1)} %copy-done.4, ...), custom_call_target="tpu_custom_call" | custom-call | flops 3000000000 | bytes 12000000 | tf_op jit(solution)/shard_map/forward_attention/pallas_call | solution.py:205
  18.6 2.6 %collective-permute-start.5 = (bf16[128,128]{1,0:T(8,128)(2,1)S(1)}, bf16[128,128]{1,0:T(8,128)(2,1)S(1)}, u32[]{:S(2)}, u32[]{:S(2)}) collective-permute-start(bf16[128,128]{1,0:T(8,128)(2,1)S(1)} %bitcast.12), channel_id=1, source_target_pairs={{0,16},{4,20},{8,24},{12,28},{16,0},{20,4},{24,8},{28,12},{1,17},{... | collective-permute-start | bytes 98312 | tf_op jit(solution)/shard_map/ppermute | solution.py:459
  21.7 1.7 %collective-permute-done.5 = bf16[128,128]{1,0:T(8,128)(2,1)S(1)} collective-permute-done((bf16[128,128]{1,0:T(8,128)(2,1)S(1)}, bf16[128,128]{1,0:T(8,128)(2,1)S(1)}, u32[]{:S(2)}, u32[]{:S(2)}) %collective-permute-start.5) | collective-permute-done | bytes 32800 | tf_op jit(solution)/shard_map/ppermute | solution.py:459
  23.4 1.5 %collective-permute-start.6 = (bf16[256,128]{1,0:T(8,128)(2,1)S(1)}, bf16[256,128]{1,0:T(8,128)(2,1)S(1)}, u32[]{:S(2)}, u32[]{:S(2)}) collective-permute-start(bf16[256,128]{1,0:T(8,128)(2,1)S(1)} %pad_maximum_fusion.2), channel_id=1, source_target_pairs={{0,4},{4,0},{8,12},{12,8},{16,20},{20,16},{24,28},{28,24},{1,5},{5... | collective-permute-start | bytes 196616 | tf_op jit(solution)/shard_map/ppermute | solution.py:459
  24.9 2.7 %collective-permute-done.6 = bf16[256,128]{1,0:T(8,128)(2,1)S(1)} collective-permute-done((bf16[256,128]{1,0:T(8,128)(2,1)S(1)}, bf16[256,128]{1,0:T(8,128)(2,1)S(1)}, u32[]{:S(2)}, u32[]{:S(2)}) %collective-permute-start.6) | collective-permute-done | bytes 65568 | tf_op jit(solution)/shard_map/ppermute | solution.py:459
  27.7 1.6 %collective-permute-start.10 = (bf16[512,128]{1,0:T(8,128)(2,1)S(1)}, bf16[512,128]{1,0:T(8,128)(2,1)S(1)}, u32[]{:S(2)}, u32[]{:S(2)}) collective-permute-start(bf16[512,128]{1,0:T(8,128)(2,1)S(1)} %pad_maximum_fusion.1), channel_id=1, source_target_pairs={{0,8},{4,12},{8,0},{12,4},{16,24},{20,28},{24,16},{28,20},{1,9},{5... | collective-permute-start | bytes 393224 | tf_op jit(solution)/shard_map/ppermute | solution.py:459
  29.3 1.2 %weight_parts.1 = (bf16[512,1152]{1,0:T(8,128)(2,1)S(1)}, f32[288,288]{1,0:T(8,128)S(1)}, bf16[288,288]{1,0:T(8,128)(2,1)S(1)}, bf16[576,288]{1,0:T(8,128)(2,1)S(1)}) custom-call(bf16[128,1152]{1,0:T(8,128)(2,1)S(1)} %copy-done.1, bf16[128,1152]{1,0:T(8,128)(2,1)S(1)} %collective-permute-done.7.grad1, bf16[128,1152]{1,0:T(8,128)(2,1)S(1)} %collective-permute-done.8.grad2, ...), custom_call_target="tpu_custom_call" | custom-call | flops 700000000 | bytes 4000000 | tf_op jit(solution)/shard_map/weight_parts/pallas_call | solution.py:259
  30.6 1.5 %collective-permute-start.4 = (bf16[128,1152]{1,0:T(8,128)(2,1)S(1)}, bf16[128,1152]{1,0:T(8,128)(2,1)S(1)}, u32[]{:S(2)}, u32[]{:S(2)}) collective-permute-start(bf16[128,1152]{1,0:T(8,128)(2,1)S(1)} %add_convert_fusion.1), channel_id=1, source_target_pairs={{0,2},{1,3},{2,0},{3,1},{4,6},{5,7},{6,4},{7,5},{8,10},{9,11},{10,... | collective-permute-start | bytes 884744 | tf_op jit(solution)/shard_map/ppermute | solution.py:459
  32.1 5.1 %backward_attention.1.joined_ref = bf16[512,1024]{1,0:T(8,128)(2,1)S(1)} custom-call(s32[8]{0:T(128)S(1)} %copy-done.4, bf16[512,1152]{1,0:T(8,128)(2,1)S(1)} %get-tuple-element.45.stacked_ref, bf16[512,1152]{1,0:T(8,128)(2,1)S(1)} %get-tuple-element.39.output_ref, bf16[512,1024]{1,0:T(8,128)(2,1)S(1)} %get-tuple-element.46.packed_ref, ...), custom_call_target="tpu_custom_call" | custom-call | flops 4000000000 | bytes 6000000 | tf_op jit(solution)/shard_map/backward_attention/pallas_call | solution.py:297
  37.4 1.7 %hidden_and_best.1 = (bf16[128,1152]{1,0:T(8,128)(2,1)}, f32[32,128]{1,0:T(8,128)}) custom-call(s32[8]{0:T(128)S(1)} %copy-done.4, bf16[128,1152]{1,0:T(8,128)(2,1)S(1)} %copy-done, bf16[128,1152]{1,0:T(8,128)(2,1)S(1)} %get-tuple-element.40.part_ref, bf16[256,1152]{1,0:T(8,128)(2,1)S(1)} %collective-permute-done.3.near_ref, ...), custom_call_target="tpu_custom_call" | custom-call | flops 100000000 | bytes 2000000 | tf_op jit(solution)/shard_map/hidden_and_best/pallas_call | solution.py:374
  39.1 1.5 %input_branch.1 = (bf16[128,1152]{1,0:T(8,128)(2,1)S(1)}, bf16[128,1152]{1,0:T(8,128)(2,1)S(1)}, bf16[256,1152]{1,0:T(8,128)(2,1)S(1)}) custom-call(bf16[512,1024]{1,0:T(8,128)(2,1)S(1)} %backward_attention.1.joined_ref, bf16[1024,1152]{1,0:T(8,128)(2,1)S(1)} %get-tuple-element.38.mixing_ref), custom_call_target="tpu_custom_call" | custom-call | flops 2000000000 | bytes 8000000 | tf_op jit(solution)/shard_map/input_branch/pallas_call | solution.py:313
  40.7 1.6 %collective-permute-start.13 = (bf16[576,288]{1,0:T(8,128)(2,1)S(1)}, bf16[576,288]{1,0:T(8,128)(2,1)S(1)}, u32[]{:S(2)}, u32[]{:S(2)}) collective-permute-start(bf16[576,288]{1,0:T(8,128)(2,1)S(1)} %get-tuple-element.57), channel_id=1, source_target_pairs={{0,4},{4,0},{8,12},{12,8},{16,20},{20,16},{24,28},{28,24},{1,5},{5... | collective-permute-start | bytes 995336 | tf_op jit(solution)/shard_map/ppermute | solution.py:459
  42.8 1.5 %collective-permute-start.12 = (bf16[128,1152]{1,0:T(8,128)(2,1)S(1)}, bf16[128,1152]{1,0:T(8,128)(2,1)S(1)}, u32[]{:S(2)}, u32[]{:S(2)}) collective-permute-start(bf16[128,1152]{1,0:T(8,128)(2,1)S(1)} %add_convert_fusion), channel_id=1, source_target_pairs={{0,2},{1,3},{2,0},{3,1},{4,6},{5,7},{6,4},{7,5},{8,10},{9,11},{10,... | collective-permute-start | bytes 884744 | tf_op jit(solution)/shard_map/ppermute | solution.py:459
  44.3 9.0 %collective-permute-done.13.got1_ref = bf16[576,288]{1,0:T(8,128)(2,1)S(1)} collective-permute-done((bf16[576,288]{1,0:T(8,128)(2,1)S(1)}, bf16[576,288]{1,0:T(8,128)(2,1)S(1)}, u32[]{:S(2)}, u32[]{:S(2)}) %collective-permute-start.13) | collective-permute-done | bytes 331808 | tf_op jit(solution)/shard_map/ppermute | solution.py:459
  53.9 6.5 %collective-permute-done.14.got2_ref = bf16[288,288]{1,0:T(8,128)(2,1)S(1)} collective-permute-done((bf16[288,288]{1,0:T(8,128)(2,1)S(1)}, bf16[288,288]{1,0:T(8,128)(2,1)S(1)}, u32[]{:S(2)}, u32[]{:S(2)}) %collective-permute-start.14) | collective-permute-done | bytes 165920 | tf_op jit(solution)/shard_map/ppermute | solution.py:459
  60.4 3.6 %collective-permute-start.15 = (bf16[144,288]{1,0:T(8,128)(2,1)S(1)}, bf16[144,288]{1,0:T(8,128)(2,1)S(1)}, u32[]{:S(2)}, u32[]{:S(2)}) collective-permute-start(bf16[144,288]{1,0:T(8,128)(2,1)S(1)} %get-tuple-element.60), channel_id=1, source_target_pairs={{0,16},{4,20},{8,24},{12,28},{16,0},{20,4},{24,8},{28,12},{1,17},{... | collective-permute-start | bytes 248840 | tf_op jit(solution)/shard_map/ppermute | solution.py:459
  64.0 2.9 %all-to-all-start = ((f32[32,1,128]{2,1,0:T(1,128)}), f32[32,1,128]{2,1,0:T(1,128)S(1)}, u32[]{:S(2)}, u32[]{:S(2)}) async-start(f32[32,1,128]{2,1,0:T(1,128)} %bitcast.5), calls=%async_computation | async-start | bytes 32768 | tf_op jit(solution)/shard_map/all_to_all | solution.py:542
  66.9 1.2 %collective-permute-done.15.refs_1_ = bf16[144,288]{1,0:T(8,128)(2,1)S(1)} collective-permute-done((bf16[144,288]{1,0:T(8,128)(2,1)S(1)}, bf16[144,288]{1,0:T(8,128)(2,1)S(1)}, u32[]{:S(2)}, u32[]{:S(2)}) %collective-permute-start.15) | collective-permute-done | bytes 82976 | tf_op jit(solution)/shard_map/ppermute | solution.py:459
  68.0 5.9 %all-to-all-done = f32[32,1,128]{2,1,0:T(1,128)S(1)} async-done(((f32[32,1,128]{2,1,0:T(1,128)}), f32[32,1,128]{2,1,0:T(1,128)S(1)}, u32[]{:S(2)}, u32[]{:S(2)}) %all-to-all-start) | async-done | bytes 16416 | tf_op jit(solution)/shard_map/all_to_all | solution.py:542
  74.0 1.8 %norm_back.1 = (bf16[128,1152]{1,0:T(8,128)(2,1)}, f32[144,288]{1,0:T(8,128)}, f32[4,8]{1,0:T(4,128)}, f32[4]{0:T(128)}) custom-call(bf16[128,1152]{1,0:T(8,128)(2,1)S(1)} %copy-done, f32[9,128]{1,0:T(8,128)S(1)} %bitcast.11, bf16[128,1152]{1,0:T(8,128)(2,1)S(1)} %copy-done.1, bf16[128,1152]{1,0:T(8,128)(2,1)S(1)} %get-tuple-element.53.part_ref, ...), custom_call_target="tpu_custom_call" | custom-call | flops 3000000 | bytes 2000000 | tf_op jit(solution)/shard_map/norm_back/pallas_call | solution.py:426
  (38 shorter events, 2.9 us)
Async XLA Ops:
  0.6 12.7 %copy-start.3 = (f32[1152]{0:T(1024)S(1)}, f32[1152]{0:T(1024)}, u32[]{:S(2)}) copy-start(f32[1152]{0:T(1024)} %param.10) | copy-start | bytes 13828
  0.6 10.9 %copy-start.1 = (bf16[128,1152]{1,0:T(8,128)(2,1)S(1)}, bf16[128,1152]{1,0:T(8,128)(2,1)}, u32[]{:S(2)}) copy-start(bf16[128,1152]{1,0:T(8,128)(2,1)} %grad_ref.1) | copy-start | bytes 884740
  0.7 12.7 %copy-start.4 = (s32[8]{0:T(128)S(1)}, s32[8]{0:T(128)}, u32[]{:S(2)}) copy-start(s32[8]{0:T(128)} %counts_ref.5) | copy-start | bytes 100
  0.7 3.1 %collective-permute-start = (bf16[128,1152]{1,0:T(8,128)(2,1)}, bf16[128,1152]{1,0:T(8,128)(2,1)S(1)}, u32[]{:S(2)}, u32[]{:S(2)}) collective-permute-start(bf16[128,1152]{1,0:T(8,128)(2,1)} %patch_ref.3), channel_id=1, source_target_pairs={{0,1},{1,0},{2,3},{3,2},{4,5},{5,4},{6,7},{7,6},{8,9},{9,8},{10,11... | collective-permute-start | bytes 884744 | tf_op jit(solution)/shard_map/ppermute | solution.py:459
  1.2 10.4 %collective-permute-start.1 = (bf16[128,1152]{1,0:T(8,128)(2,1)}, bf16[128,1152]{1,0:T(8,128)(2,1)S(1)}, u32[]{:S(2)}, u32[]{:S(2)}) collective-permute-start(bf16[128,1152]{1,0:T(8,128)(2,1)} %patch_ref.3), channel_id=1, source_target_pairs={{0,2},{1,3},{2,0},{3,1},{4,6},{5,7},{6,4},{7,5},{8,10},{9,11},{10,... | collective-permute-start | bytes 884744 | tf_op jit(solution)/shard_map/ppermute | solution.py:459
  11.6 1.8 %collective-permute-start.2 = (bf16[128,1152]{1,0:T(8,128)(2,1)S(1)}, bf16[128,1152]{1,0:T(8,128)(2,1)S(1)}, u32[]{:S(2)}, u32[]{:S(2)}) collective-permute-start(bf16[128,1152]{1,0:T(8,128)(2,1)S(1)} %collective-permute-done.1.rows2), channel_id=1, source_target_pairs={{0,1},{1,0},{2,3},{3,2},{4,5},{5,4},{6,7},{7,6},{8,9},{9,8},{10,11... | collective-permute-start | bytes 884744 | tf_op jit(solution)/shard_map/ppermute | solution.py:459
  11.6 9.6 %collective-permute-start.8 = (bf16[128,1152]{1,0:T(8,128)(2,1)S(1)}, bf16[128,1152]{1,0:T(8,128)(2,1)S(1)}, u32[]{:S(2)}, u32[]{:S(2)}) collective-permute-start(bf16[128,1152]{1,0:T(8,128)(2,1)S(1)} %copy-done.1), channel_id=1, source_target_pairs={{0,2},{1,3},{2,0},{3,1},{4,6},{5,7},{6,4},{7,5},{8,10},{9,11},{10,... | collective-permute-start | bytes 884744 | tf_op jit(solution)/shard_map/ppermute | solution.py:459
  13.3 5.2 %copy-start.6 = (bf16[4,32,128]{2,1,0:T(8,128)(2,1)S(1)}, bf16[4,32,128]{2,1,0:T(8,128)(2,1)}, u32[]{:S(2)}) copy-start(bf16[4,32,128]{2,1,0:T(8,128)(2,1)} %param.14) | copy-start | bytes 98308
  18.3 12.2 %collective-permute-start.3 = (bf16[256,1152]{1,0:T(8,128)(2,1)S(1)}, bf16[256,1152]{1,0:T(8,128)(2,1)S(1)}, u32[]{:S(2)}, u32[]{:S(2)}) collective-permute-start(bf16[256,1152]{1,0:T(8,128)(2,1)S(1)} %get-tuple-element.41), channel_id=1, source_target_pairs={{0,1},{1,0},{2,3},{3,2},{4,5},{5,4},{6,7},{7,6},{8,9},{9,8},{10,11... | collective-permute-start | bytes 1769480 | tf_op jit(solution)/shard_map/ppermute | solution.py:459
  18.6 4.8 %collective-permute-start.5 = (bf16[128,128]{1,0:T(8,128)(2,1)S(1)}, bf16[128,128]{1,0:T(8,128)(2,1)S(1)}, u32[]{:S(2)}, u32[]{:S(2)}) collective-permute-start(bf16[128,128]{1,0:T(8,128)(2,1)S(1)} %bitcast.12), channel_id=1, source_target_pairs={{0,16},{4,20},{8,24},{12,28},{16,0},{20,4},{24,8},{28,12},{1,17},{... | collective-permute-start | bytes 98312 | tf_op jit(solution)/shard_map/ppermute | solution.py:459
  21.2 8.2 %collective-permute-start.7 = (bf16[128,1152]{1,0:T(8,128)(2,1)S(1)}, bf16[128,1152]{1,0:T(8,128)(2,1)S(1)}, u32[]{:S(2)}, u32[]{:S(2)}) collective-permute-start(bf16[128,1152]{1,0:T(8,128)(2,1)S(1)} %copy-done.1), channel_id=1, source_target_pairs={{0,1},{1,0},{2,3},{3,2},{4,5},{5,4},{6,7},{7,6},{8,9},{9,8},{10,11... | collective-permute-start | bytes 884744 | tf_op jit(solution)/shard_map/ppermute | solution.py:459
  21.2 8.1 %collective-permute-start.9 = (bf16[128,1152]{1,0:T(8,128)(2,1)S(1)}, bf16[128,1152]{1,0:T(8,128)(2,1)S(1)}, u32[]{:S(2)}, u32[]{:S(2)}) collective-permute-start(bf16[128,1152]{1,0:T(8,128)(2,1)S(1)} %collective-permute-done.8.grad2), channel_id=1, source_target_pairs={{0,1},{1,0},{2,3},{3,2},{4,5},{5,4},{6,7},{7,6},{8,9},{9,8},{10,11... | collective-permute-start | bytes 884744 | tf_op jit(solution)/shard_map/ppermute | solution.py:459
  23.4 4.3 %collective-permute-start.6 = (bf16[256,128]{1,0:T(8,128)(2,1)S(1)}, bf16[256,128]{1,0:T(8,128)(2,1)S(1)}, u32[]{:S(2)}, u32[]{:S(2)}) collective-permute-start(bf16[256,128]{1,0:T(8,128)(2,1)S(1)} %pad_maximum_fusion.2), channel_id=1, source_target_pairs={{0,4},{4,0},{8,12},{12,8},{16,20},{20,16},{24,28},{28,24},{1,5},{5... | collective-permute-start | bytes 196616 | tf_op jit(solution)/shard_map/ppermute | solution.py:459
  27.7 9.5 %collective-permute-start.10 = (bf16[512,128]{1,0:T(8,128)(2,1)S(1)}, bf16[512,128]{1,0:T(8,128)(2,1)S(1)}, u32[]{:S(2)}, u32[]{:S(2)}) collective-permute-start(bf16[512,128]{1,0:T(8,128)(2,1)S(1)} %pad_maximum_fusion.1), channel_id=1, source_target_pairs={{0,8},{4,12},{8,0},{12,4},{16,24},{20,28},{24,16},{28,20},{1,9},{5... | collective-permute-start | bytes 393224 | tf_op jit(solution)/shard_map/ppermute | solution.py:459
  30.6 6.8 %collective-permute-start.4 = (bf16[128,1152]{1,0:T(8,128)(2,1)S(1)}, bf16[128,1152]{1,0:T(8,128)(2,1)S(1)}, u32[]{:S(2)}, u32[]{:S(2)}) collective-permute-start(bf16[128,1152]{1,0:T(8,128)(2,1)S(1)} %add_convert_fusion.1), channel_id=1, source_target_pairs={{0,2},{1,3},{2,0},{3,1},{4,6},{5,7},{6,4},{7,5},{8,10},{9,11},{10,... | collective-permute-start | bytes 884744 | tf_op jit(solution)/shard_map/ppermute | solution.py:459
  32.1 5.3 %copy-start = (bf16[128,1152]{1,0:T(8,128)(2,1)S(1)}, bf16[128,1152]{1,0:T(8,128)(2,1)}, u32[]{:S(2)}) copy-start(bf16[128,1152]{1,0:T(8,128)(2,1)} %patch_ref.3) | copy-start | bytes 884740
  32.1 5.3 %copy-start.2 = (bf16[1152,128]{1,0:T(8,128)(2,1)S(1)}, bf16[1152,128]{1,0:T(8,128)(2,1)}, u32[]{:S(2)}) copy-start(bf16[1152,128]{1,0:T(8,128)(2,1)} %embed_ref.1) | copy-start | bytes 884740
  40.6 33.3 %copy-start.5 = (s32[4]{0:T(128)S(1)}, s32[4]{0:T(128)}, u32[]{:S(2)}) copy-start(s32[4]{0:T(128)} %refs_3_.1) | copy-start | bytes 52
  40.7 2.1 %collective-permute-start.11 = (bf16[256,1152]{1,0:T(8,128)(2,1)S(1)}, bf16[256,1152]{1,0:T(8,128)(2,1)S(1)}, u32[]{:S(2)}, u32[]{:S(2)}) collective-permute-start(bf16[256,1152]{1,0:T(8,128)(2,1)S(1)} %get-tuple-element.54), channel_id=1, source_target_pairs={{0,1},{1,0},{2,3},{3,2},{4,5},{5,4},{6,7},{7,6},{8,9},{9,8},{10,11... | collective-permute-start | bytes 1769480 | tf_op jit(solution)/shard_map/ppermute | solution.py:459
  40.7 12.6 %collective-permute-start.13 = (bf16[576,288]{1,0:T(8,128)(2,1)S(1)}, bf16[576,288]{1,0:T(8,128)(2,1)S(1)}, u32[]{:S(2)}, u32[]{:S(2)}) collective-permute-start(bf16[576,288]{1,0:T(8,128)(2,1)S(1)} %get-tuple-element.57), channel_id=1, source_target_pairs={{0,4},{4,0},{8,12},{12,8},{16,20},{20,16},{24,28},{28,24},{1,5},{5... | collective-permute-start | bytes 995336 | tf_op jit(solution)/shard_map/ppermute | solution.py:459
  42.8 31.2 %collective-permute-start.12 = (bf16[128,1152]{1,0:T(8,128)(2,1)S(1)}, bf16[128,1152]{1,0:T(8,128)(2,1)S(1)}, u32[]{:S(2)}, u32[]{:S(2)}) collective-permute-start(bf16[128,1152]{1,0:T(8,128)(2,1)S(1)} %add_convert_fusion), channel_id=1, source_target_pairs={{0,2},{1,3},{2,0},{3,1},{4,6},{5,7},{6,4},{7,5},{8,10},{9,11},{10,... | collective-permute-start | bytes 884744 | tf_op jit(solution)/shard_map/ppermute | solution.py:459
  53.4 7.0 %collective-permute-start.14 = (bf16[288,288]{1,0:T(8,128)(2,1)S(1)}, bf16[288,288]{1,0:T(8,128)(2,1)S(1)}, u32[]{:S(2)}, u32[]{:S(2)}) collective-permute-start(bf16[288,288]{1,0:T(8,128)(2,1)S(1)} %add_convert_fusion.2), channel_id=1, source_target_pairs={{0,8},{4,12},{8,0},{12,4},{16,24},{20,28},{24,16},{28,20},{1,9},{5... | collective-permute-start | bytes 497672 | tf_op jit(solution)/shard_map/ppermute | solution.py:459
  60.4 7.6 %collective-permute-start.15 = (bf16[144,288]{1,0:T(8,128)(2,1)S(1)}, bf16[144,288]{1,0:T(8,128)(2,1)S(1)}, u32[]{:S(2)}, u32[]{:S(2)}) collective-permute-start(bf16[144,288]{1,0:T(8,128)(2,1)S(1)} %get-tuple-element.60), channel_id=1, source_target_pairs={{0,16},{4,20},{8,24},{12,28},{16,0},{20,4},{24,8},{28,12},{1,17},{... | collective-permute-start | bytes 248840 | tf_op jit(solution)/shard_map/ppermute | solution.py:459
  64.0 10.0 %all-to-all-start = ((f32[32,1,128]{2,1,0:T(1,128)}), f32[32,1,128]{2,1,0:T(1,128)S(1)}, u32[]{:S(2)}, u32[]{:S(2)}) async-start(f32[32,1,128]{2,1,0:T(1,128)} %bitcast.5), calls=%async_computation | async-start | bytes 32768 | tf_op jit(solution)/shard_map/all_to_all | solution.py:542

commit v5 on v4

--- a/solution.py
+++ b/solution.py
@@ -285,8 +285,8 @@
         grad_score = (prob * (grad_prob - delta)).astype(BF16)
         parts = (
             (dot(grad_score, key, 1, 0) * SCALE).astype(BF16),
-            (dot(grad_score, query, 0, 0) * SCALE).astype(BF16),
-            dot(weights, flow, 0, 0).astype(BF16),
+            (dot(query, grad_score, 0, 0) * SCALE).T.astype(BF16),
+            dot(flow, weights, 0, 0).T.astype(BF16),
             jnp.zeros((rows, HEAD_LANES - 3 * HEAD_DIM), BF16),
         )
         out_ref[:, head * HEAD_LANES : (head + 1) * HEAD_LANES] = jnp.concatenate(parts, axis=1)
@@ -434,24 +434,26 @@
     )(patches, gain, grads, part, near, far, *more)
 
 
-def join_kernel(kept_ref, got1_ref, got2_ref, mine_ref, send_ref):
-    half, share = kept_ref.shape[0], mine_ref.shape[0]
-    total = kept_ref[...] + got1_ref[:half, :].astype(F32) + got2_ref[...].astype(F32)
+def join_kernel(kept_ref, got1_ref, got2_ref, got3_ref, mine_ref, send_ref):
+    share = mine_ref.shape[0]
+    total = kept_ref[...]
+    for ref in (got1_ref, got2_ref, got3_ref):
+        total = total + ref[...].astype(F32)
     mine_ref[...] = total[:share]
     send_ref[...] = total[share:].astype(BF16)
 
 
-def join_parts(kept, got1, got2):
+def join_parts(kept, *got):
     share = (kept.shape[0] // 2, kept.shape[1])
     return pl.pallas_call(
         join_kernel,
         out_shape=(shape(share, F32), shape(share, BF16)),
-        in_specs=[VMEM] * 3,
+        in_specs=[VMEM] * 4,
         out_specs=(VMEM,) * 2,
         cost_estimate=cost(3e5, 1e6),
         name="join_parts",
         compiler_params=grant(6),
-    )(kept, got1, got2)
+    )(kept, *got)
 
 
 def swap(values, axis, distance):
@@ -515,9 +517,9 @@
     grads = (hidden_grad, grads1, grads2, grads3)
     part, received, far, _ = scatter_sum(parts)
     if few:
-        order = ((0, 4), (2, 6), (1, 5, 3, 7))
-        stacked, kept, second, first = weight_parts(grads, attended, order)
-        got1 = swap(first, "dp", 1)
+        order = ((0, 4), (1, 5), (2, 6), (3, 7))
+        stacked, kept, *sent_parts = weight_parts(grads, attended, order)
+        got = [swap(values, "dp", index + 1) for index, values in enumerate(sent_parts)]
         other = swap(tokens, "dp", 2)
         near_tokens = tokens
         joined = backward(patch_counts, stacked, output_pad, packed, probs)
@@ -535,9 +537,7 @@
     part, received, far, sent = scatter_sum(grad_parts)
     more = ()
     if few:
-        going = (second.astype(F32) + got1[kept.shape[0] :].astype(F32)).astype(BF16)
-        got2 = swap(going, "dp", 2)
-        mine, send = join_parts(kept, got1, got2)
+        mine, send = join_parts(kept, *got)
         other = swap(send, "dp", 4)
         found = lax.all_to_all(after(best, sent), ("dp", "mp"), 0, 0, tiled=True)
         more = (mine, other, found, positive_page)

time: 76 us -> 72.9 us (0.959)
  waiting for transfers between devices: 32.5 us -> 29 us
  starting transfers between devices: 23 us -> 24.2 us
    ppermute x16 -> x17, waiting for transfers between devices: 26.6 us -> 23.4 us  [swap(): lax.ppermute(values, axis, [(index, index ^ distance) for index in range(...]
    ppermute x16 -> x17, starting transfers between devices: 20.2 us -> 21.7 us  [swap(): lax.ppermute(values, axis, [(index, index ^ distance) for index in range(...]
  transfers between devices with their start and end apart: 17 -> 18, of which waited for: 9 -> 10; matrix products, arithmetic and copies ran while one was open for 0% -> 0% of each run, Pallas kernels for 19% -> 18%
where the time goes in v5:
time: 72.9 us; the launch traced here: 72.7 us
  waiting for transfers between devices  29 us (40%)
  starting transfers between devices  24.2 us (33%)
  Pallas kernels  18.5 us (25%)
  between operations  0.79 us (1%)
    ppermute x17, waiting for transfers between devices, swap(): lax.ppermute(values, axis, [(index, index ^ distance) for index in range(...  23.4 us
    ppermute x17, starting transfers between devices, swap(): lax.ppermute(values, axis, [(index, index ^ distance) for index in range(...  21.7 us
    all_to_all x1, waiting for transfers between devices, body(): found = lax.all_to_all(after(best, sent), ('dp', 'mp'), 0, 0, tiled=True)  5.59 us
    pallas_call x1, Pallas kernels, forward(): pl.pallas_call(partial(forward_kernel, heads, rows_dev), out_shape=(shape...  4.93 us
    pallas_call x1, Pallas kernels, backward(): pl.pallas_call(partial(backward_kernel, heads), out_shape=shape((rows, he...  4.35 us
    pallas_call x1, Pallas kernels, prepare(): pl.pallas_call(partial(prepare_kernel, heads), out_shape=(shape((heads *...  2.84 us
    all_to_all x1, starting transfers between devices, body(): found = lax.all_to_all(after(best, sent), ('dp', 'mp'), 0, 0, tiled=True)  2.54 us
    pallas_call x1, Pallas kernels, norm_back(): pl.pallas_call(norm_back_kernel, out_shape=tuple(out_shape), in_specs=[VM...  1.83 us
  transfers between devices with their start and end apart: 18, of which 10 were waited for; matrix products, arithmetic and copies ran while one was open for 0% of the time, Pallas kernels for 18%

profile of v5, /device:TPU:0, one launch (start us, length us, event | category | flops | bytes accessed | tf_op | source)
XLA Modules:
  0.0 72.7 jit_solution(17104030090175817494)
XLA Ops:
  1.2 2.6 %collective-permute-start.1 = (bf16[128,1152]{1,0:T(8,128)(2,1)}, bf16[128,1152]{1,0:T(8,128)(2,1)S(1)}, u32[]{:S(2)}, u32[]{:S(2)}) collective-permute-start(bf16[128,1152]{1,0:T(8,128)(2,1)} %patch_ref.3), channel_id=1, source_target_pairs={{0,2},{1,3},{2,0},{3,1},{4,6},{5,7},{6,4},{7,5},{8,10},{9,11},{10,... | collective-permute-start | bytes 884744 | tf_op jit(solution)/shard_map/ppermute | solution.py:461
  3.8 2.8 %prepare.1 = (bf16[1024,1152]{1,0:T(8,128)(2,1)S(1)}, bf16[512,1152]{1,0:T(8,128)(2,1)S(1)}, bf16[256,1024]{1,0:T(8,128)(2,1)S(1)}) custom-call(bf16[128,1152]{1,0:T(8,128)(2,1)} %patch_ref.3, f32[9,128]{1,0:T(8,128)} %bitcast.9, bf16[864,1152]{1,0:T(8,128)(2,1)} %bitcast.15, bf16[288,1152]{1,0:T(8,128)(2,1)} %bitcast.16, ...), custom_call_target="tpu_custom_call" | custom-call | flops 1000000000 | bytes 8000000 | tf_op jit(solution)/shard_map/prepare/pallas_call | solution.py:111
  6.6 5.0 %collective-permute-done.1.rows2 = bf16[128,1152]{1,0:T(8,128)(2,1)S(1)} collective-permute-done((bf16[128,1152]{1,0:T(8,128)(2,1)}, bf16[128,1152]{1,0:T(8,128)(2,1)S(1)}, u32[]{:S(2)}, u32[]{:S(2)}) %collective-permute-start.1) | collective-permute-done | bytes 294944 | tf_op jit(solution)/shard_map/ppermute | solution.py:461
  11.6 1.7 %collective-permute-start.8 = (bf16[128,1152]{1,0:T(8,128)(2,1)S(1)}, bf16[128,1152]{1,0:T(8,128)(2,1)S(1)}, u32[]{:S(2)}, u32[]{:S(2)}) collective-permute-start(bf16[128,1152]{1,0:T(8,128)(2,1)S(1)} %copy-done.1), channel_id=1, source_target_pairs={{0,2},{1,3},{2,0},{3,1},{4,6},{5,7},{6,4},{7,5},{8,10},{9,11},{10,... | collective-permute-start | bytes 884744 | tf_op jit(solution)/shard_map/ppermute | solution.py:461
  13.4 4.9 %forward_attention.1 = (bf16[512,1024]{1,0:T(8,128)(2,1)S(1)}, bf16[4,512,512]{2,1,0:T(8,128)(2,1)S(1)}, bf16[512,512]{1,0:T(8,128)(2,1)S(1)}, bf16[128,1152]{1,...) custom-call(s32[8]{0:T(128)S(1)} %copy-done.4, ...), custom_call_target="tpu_custom_call" | custom-call | flops 3000000000 | bytes 12000000 | tf_op jit(solution)/shard_map/forward_attention/pallas_call | solution.py:205
  18.6 2.6 %collective-permute-start.5 = (bf16[128,128]{1,0:T(8,128)(2,1)S(1)}, bf16[128,128]{1,0:T(8,128)(2,1)S(1)}, u32[]{:S(2)}, u32[]{:S(2)}) collective-permute-start(bf16[128,128]{1,0:T(8,128)(2,1)S(1)} %bitcast.12), channel_id=1, source_target_pairs={{0,16},{4,20},{8,24},{12,28},{16,0},{20,4},{24,8},{28,12},{1,17},{... | collective-permute-start | bytes 98312 | tf_op jit(solution)/shard_map/ppermute | solution.py:461
  21.7 1.7 %collective-permute-done.5 = bf16[128,128]{1,0:T(8,128)(2,1)S(1)} collective-permute-done((bf16[128,128]{1,0:T(8,128)(2,1)S(1)}, bf16[128,128]{1,0:T(8,128)(2,1)S(1)}, u32[]{:S(2)}, u32[]{:S(2)}) %collective-permute-start.5) | collective-permute-done | bytes 32800 | tf_op jit(solution)/shard_map/ppermute | solution.py:461
  23.4 1.5 %collective-permute-start.6 = (bf16[256,128]{1,0:T(8,128)(2,1)S(1)}, bf16[256,128]{1,0:T(8,128)(2,1)S(1)}, u32[]{:S(2)}, u32[]{:S(2)}) collective-permute-start(bf16[256,128]{1,0:T(8,128)(2,1)S(1)} %pad_maximum_fusion.2), channel_id=1, source_target_pairs={{0,4},{4,0},{8,12},{12,8},{16,20},{20,16},{24,28},{28,24},{1,5},{5... | collective-permute-start | bytes 196616 | tf_op jit(solution)/shard_map/ppermute | solution.py:461
  24.9 2.7 %collective-permute-done.6 = bf16[256,128]{1,0:T(8,128)(2,1)S(1)} collective-permute-done((bf16[256,128]{1,0:T(8,128)(2,1)S(1)}, bf16[256,128]{1,0:T(8,128)(2,1)S(1)}, u32[]{:S(2)}, u32[]{:S(2)}) %collective-permute-start.6) | collective-permute-done | bytes 65568 | tf_op jit(solution)/shard_map/ppermute | solution.py:461
  27.7 1.6 %collective-permute-start.10 = (bf16[512,128]{1,0:T(8,128)(2,1)S(1)}, bf16[512,128]{1,0:T(8,128)(2,1)S(1)}, u32[]{:S(2)}, u32[]{:S(2)}) collective-permute-start(bf16[512,128]{1,0:T(8,128)(2,1)S(1)} %pad_maximum_fusion.1), channel_id=1, source_target_pairs={{0,8},{4,12},{8,0},{12,4},{16,24},{20,28},{24,16},{28,20},{1,9},{5... | collective-permute-start | bytes 393224 | tf_op jit(solution)/shard_map/ppermute | solution.py:461
  30.6 1.5 %collective-permute-start.4 = (bf16[128,1152]{1,0:T(8,128)(2,1)S(1)}, bf16[128,1152]{1,0:T(8,128)(2,1)S(1)}, u32[]{:S(2)}, u32[]{:S(2)}) collective-permute-start(bf16[128,1152]{1,0:T(8,128)(2,1)S(1)} %add_convert_fusion.1), channel_id=1, source_target_pairs={{0,2},{1,3},{2,0},{3,1},{4,6},{5,7},{6,4},{7,5},{8,10},{9,11},{10,... | collective-permute-start | bytes 884744 | tf_op jit(solution)/shard_map/ppermute | solution.py:461
  32.1 4.4 %backward_attention.1.joined_ref = bf16[512,1024]{1,0:T(8,128)(2,1)S(1)} custom-call(s32[8]{0:T(128)S(1)} %copy-done.4, bf16[512,1152]{1,0:T(8,128)(2,1)S(1)} %get-tuple-element.46.stacked_ref, bf16[512,1152]{1,0:T(8,128)(2,1)S(1)} %get-tuple-element.40.output_ref, bf16[512,1024]{1,0:T(8,128)(2,1)S(1)} %get-tuple-element.47.packed_ref, ...), custom_call_target="tpu_custom_call" | custom-call | flops 4000000000 | bytes 6000000 | tf_op jit(solution)/shard_map/backward_attention/pallas_call | solution.py:297
  37.4 1.7 %hidden_and_best.1 = (bf16[128,1152]{1,0:T(8,128)(2,1)}, f32[32,128]{1,0:T(8,128)}) custom-call(s32[8]{0:T(128)S(1)} %copy-done.4, bf16[128,1152]{1,0:T(8,128)(2,1)S(1)} %copy-done, bf16[128,1152]{1,0:T(8,128)(2,1)S(1)} %get-tuple-element.41.part_ref, bf16[256,1152]{1,0:T(8,128)(2,1)S(1)} %collective-permute-done.3.near_ref, ...), custom_call_target="tpu_custom_call" | custom-call | flops 100000000 | bytes 2000000 | tf_op jit(solution)/shard_map/hidden_and_best/pallas_call | solution.py:374
  39.1 1.5 %input_branch.1 = (bf16[128,1152]{1,0:T(8,128)(2,1)S(1)}, bf16[128,1152]{1,0:T(8,128)(2,1)S(1)}, bf16[256,1152]{1,0:T(8,128)(2,1)S(1)}) custom-call(bf16[512,1024]{1,0:T(8,128)(2,1)S(1)} %backward_attention.1.joined_ref, bf16[1024,1152]{1,0:T(8,128)(2,1)S(1)} %get-tuple-element.39.mixing_ref), custom_call_target="tpu_custom_call" | custom-call | flops 2000000000 | bytes 8000000 | tf_op jit(solution)/shard_map/input_branch/pallas_call | solution.py:313
  40.7 2.0 %collective-permute-done.11.near_ref = bf16[256,1152]{1,0:T(8,128)(2,1)S(1)} collective-permute-done((bf16[256,1152]{1,0:T(8,128)(2,1)S(1)}, bf16[256,1152]{1,0:T(8,128)(2,1)S(1)}, u32[]{:S(2)}, u32[]{:S(2)}) %collective-permute-start.11) | collective-permute-done | bytes 589856 | tf_op jit(solution)/shard_map/ppermute | solution.py:461
  42.8 1.5 %collective-permute-start.12 = (bf16[128,1152]{1,0:T(8,128)(2,1)S(1)}, bf16[128,1152]{1,0:T(8,128)(2,1)S(1)}, u32[]{:S(2)}, u32[]{:S(2)}) collective-permute-start(bf16[128,1152]{1,0:T(8,128)(2,1)S(1)} %add_convert_fusion), channel_id=1, source_target_pairs={{0,2},{1,3},{2,0},{3,1},{4,6},{5,7},{6,4},{7,5},{8,10},{9,11},{10,... | collective-permute-start | bytes 884744 | tf_op jit(solution)/shard_map/ppermute | solution.py:461
  44.3 1.5 %collective-permute-start.13 = (bf16[288,288]{1,0:T(8,128)(2,1)S(1)}, bf16[288,288]{1,0:T(8,128)(2,1)S(1)}, u32[]{:S(2)}, u32[]{:S(2)}) collective-permute-start(bf16[288,288]{1,0:T(8,128)(2,1)S(1)} %get-tuple-element.58), channel_id=1, source_target_pairs={{0,4},{4,0},{8,12},{12,8},{16,20},{20,16},{24,28},{28,24},{1,5},{5... | collective-permute-start | bytes 497672 | tf_op jit(solution)/shard_map/ppermute | solution.py:461
  47.8 3.9 %collective-permute-done.13.got1_ref = bf16[288,288]{1,0:T(8,128)(2,1)S(1)} collective-permute-done((bf16[288,288]{1,0:T(8,128)(2,1)S(1)}, bf16[288,288]{1,0:T(8,128)(2,1)S(1)}, u32[]{:S(2)}, u32[]{:S(2)}) %collective-permute-start.13) | collective-permute-done | bytes 165920 | tf_op jit(solution)/shard_map/ppermute | solution.py:461
  51.7 2.4 %collective-permute-done.14.got2_ref = bf16[288,288]{1,0:T(8,128)(2,1)S(1)} collective-permute-done((bf16[288,288]{1,0:T(8,128)(2,1)S(1)}, bf16[288,288]{1,0:T(8,128)(2,1)S(1)}, u32[]{:S(2)}, u32[]{:S(2)}) %collective-permute-start.14) | collective-permute-done | bytes 165920 | tf_op jit(solution)/shard_map/ppermute | solution.py:461
  54.1 3.3 %collective-permute-done.15.got3_ref = bf16[288,288]{1,0:T(8,128)(2,1)S(1)} collective-permute-done((bf16[288,288]{1,0:T(8,128)(2,1)S(1)}, bf16[288,288]{1,0:T(8,128)(2,1)S(1)}, u32[]{:S(2)}, u32[]{:S(2)}) %collective-permute-start.15) | collective-permute-done | bytes 165920 | tf_op jit(solution)/shard_map/ppermute | solution.py:461
  57.6 3.6 %collective-permute-start.16 = (bf16[144,288]{1,0:T(8,128)(2,1)S(1)}, bf16[144,288]{1,0:T(8,128)(2,1)S(1)}, u32[]{:S(2)}, u32[]{:S(2)}) collective-permute-start(bf16[144,288]{1,0:T(8,128)(2,1)S(1)} %get-tuple-element.62), channel_id=1, source_target_pairs={{0,16},{4,20},{8,24},{12,28},{16,0},{20,4},{24,8},{28,12},{1,17},{... | collective-permute-start | bytes 248840 | tf_op jit(solution)/shard_map/ppermute | solution.py:461
  61.2 2.5 %all-to-all-start = ((f32[32,1,128]{2,1,0:T(1,128)}), f32[32,1,128]{2,1,0:T(1,128)S(1)}, u32[]{:S(2)}, u32[]{:S(2)}) async-start(f32[32,1,128]{2,1,0:T(1,128)} %bitcast.5), calls=%async_computation | async-start | bytes 32768 | tf_op jit(solution)/shard_map/all_to_all | solution.py:542
  65.3 5.6 %all-to-all-done = f32[32,1,128]{2,1,0:T(1,128)S(1)} async-done(((f32[32,1,128]{2,1,0:T(1,128)}), f32[32,1,128]{2,1,0:T(1,128)S(1)}, u32[]{:S(2)}, u32[]{:S(2)}) %all-to-all-start) | async-done | bytes 16416 | tf_op jit(solution)/shard_map/all_to_all | solution.py:542
  70.8 1.8 %norm_back.1 = (bf16[128,1152]{1,0:T(8,128)(2,1)}, f32[144,288]{1,0:T(8,128)}, f32[4,8]{1,0:T(4,128)}, f32[4]{0:T(128)}) custom-call(bf16[128,1152]{1,0:T(8,128)(2,1)S(1)} %copy-done, f32[9,128]{1,0:T(8,128)S(1)} %bitcast.11, bf16[128,1152]{1,0:T(8,128)(2,1)S(1)} %copy-done.1, bf16[128,1152]{1,0:T(8,128)(2,1)S(1)} %get-tuple-element.54.part_ref, ...), custom_call_target="tpu_custom_call" | custom-call | flops 3000000 | bytes 2000000 | tf_op jit(solution)/shard_map/norm_back/pallas_call | solution.py:426
  (39 shorter events, 7.3 us)
Async XLA Ops:
  0.6 12.7 %copy-start.3 = (f32[1152]{0:T(1024)S(1)}, f32[1152]{0:T(1024)}, u32[]{:S(2)}) copy-start(f32[1152]{0:T(1024)} %param.10) | copy-start | bytes 13828
  0.6 10.9 %copy-start.1 = (bf16[128,1152]{1,0:T(8,128)(2,1)S(1)}, bf16[128,1152]{1,0:T(8,128)(2,1)}, u32[]{:S(2)}) copy-start(bf16[128,1152]{1,0:T(8,128)(2,1)} %grad_ref.1) | copy-start | bytes 884740
  0.7 12.7 %copy-start.4 = (s32[8]{0:T(128)S(1)}, s32[8]{0:T(128)}, u32[]{:S(2)}) copy-start(s32[8]{0:T(128)} %counts_ref.5) | copy-start | bytes 100
  0.7 3.1 %collective-permute-start = (bf16[128,1152]{1,0:T(8,128)(2,1)}, bf16[128,1152]{1,0:T(8,128)(2,1)S(1)}, u32[]{:S(2)}, u32[]{:S(2)}) collective-permute-start(bf16[128,1152]{1,0:T(8,128)(2,1)} %patch_ref.3), channel_id=1, source_target_pairs={{0,1},{1,0},{2,3},{3,2},{4,5},{5,4},{6,7},{7,6},{8,9},{9,8},{10,11... | collective-permute-start | bytes 884744 | tf_op jit(solution)/shard_map/ppermute | solution.py:461
  1.2 10.4 %collective-permute-start.1 = (bf16[128,1152]{1,0:T(8,128)(2,1)}, bf16[128,1152]{1,0:T(8,128)(2,1)S(1)}, u32[]{:S(2)}, u32[]{:S(2)}) collective-permute-start(bf16[128,1152]{1,0:T(8,128)(2,1)} %patch_ref.3), channel_id=1, source_target_pairs={{0,2},{1,3},{2,0},{3,1},{4,6},{5,7},{6,4},{7,5},{8,10},{9,11},{10,... | collective-permute-start | bytes 884744 | tf_op jit(solution)/shard_map/ppermute | solution.py:461
  11.6 1.8 %collective-permute-start.2 = (bf16[128,1152]{1,0:T(8,128)(2,1)S(1)}, bf16[128,1152]{1,0:T(8,128)(2,1)S(1)}, u32[]{:S(2)}, u32[]{:S(2)}) collective-permute-start(bf16[128,1152]{1,0:T(8,128)(2,1)S(1)} %collective-permute-done.1.rows2), channel_id=1, source_target_pairs={{0,1},{1,0},{2,3},{3,2},{4,5},{5,4},{6,7},{7,6},{8,9},{9,8},{10,11... | collective-permute-start | bytes 884744 | tf_op jit(solution)/shard_map/ppermute | solution.py:461
  11.6 9.6 %collective-permute-start.8 = (bf16[128,1152]{1,0:T(8,128)(2,1)S(1)}, bf16[128,1152]{1,0:T(8,128)(2,1)S(1)}, u32[]{:S(2)}, u32[]{:S(2)}) collective-permute-start(bf16[128,1152]{1,0:T(8,128)(2,1)S(1)} %copy-done.1), channel_id=1, source_target_pairs={{0,2},{1,3},{2,0},{3,1},{4,6},{5,7},{6,4},{7,5},{8,10},{9,11},{10,... | collective-permute-start | bytes 884744 | tf_op jit(solution)/shard_map/ppermute | solution.py:461
  18.3 12.2 %collective-permute-start.3 = (bf16[256,1152]{1,0:T(8,128)(2,1)S(1)}, bf16[256,1152]{1,0:T(8,128)(2,1)S(1)}, u32[]{:S(2)}, u32[]{:S(2)}) collective-permute-start(bf16[256,1152]{1,0:T(8,128)(2,1)S(1)} %get-tuple-element.42), channel_id=1, source_target_pairs={{0,1},{1,0},{2,3},{3,2},{4,5},{5,4},{6,7},{7,6},{8,9},{9,8},{10,11... | collective-permute-start | bytes 1769480 | tf_op jit(solution)/shard_map/ppermute | solution.py:461
  18.6 4.8 %collective-permute-start.5 = (bf16[128,128]{1,0:T(8,128)(2,1)S(1)}, bf16[128,128]{1,0:T(8,128)(2,1)S(1)}, u32[]{:S(2)}, u32[]{:S(2)}) collective-permute-start(bf16[128,128]{1,0:T(8,128)(2,1)S(1)} %bitcast.12), channel_id=1, source_target_pairs={{0,16},{4,20},{8,24},{12,28},{16,0},{20,4},{24,8},{28,12},{1,17},{... | collective-permute-start | bytes 98312 | tf_op jit(solution)/shard_map/ppermute | solution.py:461
  21.2 8.2 %collective-permute-start.7 = (bf16[128,1152]{1,0:T(8,128)(2,1)S(1)}, bf16[128,1152]{1,0:T(8,128)(2,1)S(1)}, u32[]{:S(2)}, u32[]{:S(2)}) collective-permute-start(bf16[128,1152]{1,0:T(8,128)(2,1)S(1)} %copy-done.1), channel_id=1, source_target_pairs={{0,1},{1,0},{2,3},{3,2},{4,5},{5,4},{6,7},{7,6},{8,9},{9,8},{10,11... | collective-permute-start | bytes 884744 | tf_op jit(solution)/shard_map/ppermute | solution.py:461
  21.2 8.1 %collective-permute-start.9 = (bf16[128,1152]{1,0:T(8,128)(2,1)S(1)}, bf16[128,1152]{1,0:T(8,128)(2,1)S(1)}, u32[]{:S(2)}, u32[]{:S(2)}) collective-permute-start(bf16[128,1152]{1,0:T(8,128)(2,1)S(1)} %collective-permute-done.8.grad2), channel_id=1, source_target_pairs={{0,1},{1,0},{2,3},{3,2},{4,5},{5,4},{6,7},{7,6},{8,9},{9,8},{10,11... | collective-permute-start | bytes 884744 | tf_op jit(solution)/shard_map/ppermute | solution.py:461
  23.4 4.3 %collective-permute-start.6 = (bf16[256,128]{1,0:T(8,128)(2,1)S(1)}, bf16[256,128]{1,0:T(8,128)(2,1)S(1)}, u32[]{:S(2)}, u32[]{:S(2)}) collective-permute-start(bf16[256,128]{1,0:T(8,128)(2,1)S(1)} %pad_maximum_fusion.2), channel_id=1, source_target_pairs={{0,4},{4,0},{8,12},{12,8},{16,20},{20,16},{24,28},{28,24},{1,5},{5... | collective-permute-start | bytes 196616 | tf_op jit(solution)/shard_map/ppermute | solution.py:461
  27.7 8.8 %collective-permute-start.10 = (bf16[512,128]{1,0:T(8,128)(2,1)S(1)}, bf16[512,128]{1,0:T(8,128)(2,1)S(1)}, u32[]{:S(2)}, u32[]{:S(2)}) collective-permute-start(bf16[512,128]{1,0:T(8,128)(2,1)S(1)} %pad_maximum_fusion.1), channel_id=1, source_target_pairs={{0,8},{4,12},{8,0},{12,4},{16,24},{20,28},{24,16},{28,20},{1,9},{5... | collective-permute-start | bytes 393224 | tf_op jit(solution)/shard_map/ppermute | solution.py:461
  30.6 6.8 %collective-permute-start.4 = (bf16[128,1152]{1,0:T(8,128)(2,1)S(1)}, bf16[128,1152]{1,0:T(8,128)(2,1)S(1)}, u32[]{:S(2)}, u32[]{:S(2)}) collective-permute-start(bf16[128,1152]{1,0:T(8,128)(2,1)S(1)} %add_convert_fusion.1), channel_id=1, source_target_pairs={{0,2},{1,3},{2,0},{3,1},{4,6},{5,7},{6,4},{7,5},{8,10},{9,11},{10,... | collective-permute-start | bytes 884744 | tf_op jit(solution)/shard_map/ppermute | solution.py:461
  32.1 5.3 %copy-start = (bf16[128,1152]{1,0:T(8,128)(2,1)S(1)}, bf16[128,1152]{1,0:T(8,128)(2,1)}, u32[]{:S(2)}) copy-start(bf16[128,1152]{1,0:T(8,128)(2,1)} %patch_ref.3) | copy-start | bytes 884740
  32.1 5.3 %copy-start.2 = (bf16[1152,128]{1,0:T(8,128)(2,1)S(1)}, bf16[1152,128]{1,0:T(8,128)(2,1)}, u32[]{:S(2)}) copy-start(bf16[1152,128]{1,0:T(8,128)(2,1)} %embed_ref.1) | copy-start | bytes 884740
  40.6 30.2 %copy-start.5 = (s32[4]{0:T(128)S(1)}, s32[4]{0:T(128)}, u32[]{:S(2)}) copy-start(s32[4]{0:T(128)} %refs_3_.1) | copy-start | bytes 52
  40.7 2.1 %collective-permute-start.11 = (bf16[256,1152]{1,0:T(8,128)(2,1)S(1)}, bf16[256,1152]{1,0:T(8,128)(2,1)S(1)}, u32[]{:S(2)}, u32[]{:S(2)}) collective-permute-start(bf16[256,1152]{1,0:T(8,128)(2,1)S(1)} %get-tuple-element.55), channel_id=1, source_target_pairs={{0,1},{1,0},{2,3},{3,2},{4,5},{5,4},{6,7},{7,6},{8,9},{9,8},{10,11... | collective-permute-start | bytes 1769480 | tf_op jit(solution)/shard_map/ppermute | solution.py:461
  42.8 28.0 %collective-permute-start.12 = (bf16[128,1152]{1,0:T(8,128)(2,1)S(1)}, bf16[128,1152]{1,0:T(8,128)(2,1)S(1)}, u32[]{:S(2)}, u32[]{:S(2)}) collective-permute-start(bf16[128,1152]{1,0:T(8,128)(2,1)S(1)} %add_convert_fusion), channel_id=1, source_target_pairs={{0,2},{1,3},{2,0},{3,1},{4,6},{5,7},{6,4},{7,5},{8,10},{9,11},{10,... | collective-permute-start | bytes 884744 | tf_op jit(solution)/shard_map/ppermute | solution.py:461
  44.3 7.4 %collective-permute-start.13 = (bf16[288,288]{1,0:T(8,128)(2,1)S(1)}, bf16[288,288]{1,0:T(8,128)(2,1)S(1)}, u32[]{:S(2)}, u32[]{:S(2)}) collective-permute-start(bf16[288,288]{1,0:T(8,128)(2,1)S(1)} %get-tuple-element.58), channel_id=1, source_target_pairs={{0,4},{4,0},{8,12},{12,8},{16,20},{20,16},{24,28},{28,24},{1,5},{5... | collective-permute-start | bytes 497672 | tf_op jit(solution)/shard_map/ppermute | solution.py:461
  45.8 8.3 %collective-permute-start.14 = (bf16[288,288]{1,0:T(8,128)(2,1)S(1)}, bf16[288,288]{1,0:T(8,128)(2,1)S(1)}, u32[]{:S(2)}, u32[]{:S(2)}) collective-permute-start(bf16[288,288]{1,0:T(8,128)(2,1)S(1)} %get-tuple-element.59), channel_id=1, source_target_pairs={{0,8},{4,12},{8,0},{12,4},{16,24},{20,28},{24,16},{28,20},{1,9},{5... | collective-permute-start | bytes 497672 | tf_op jit(solution)/shard_map/ppermute | solution.py:461
  46.3 11.1 %collective-permute-start.15 = (bf16[288,288]{1,0:T(8,128)(2,1)S(1)}, bf16[288,288]{1,0:T(8,128)(2,1)S(1)}, u32[]{:S(2)}, u32[]{:S(2)}) collective-permute-start(bf16[288,288]{1,0:T(8,128)(2,1)S(1)} %get-tuple-element.60), channel_id=1, source_target_pairs={{0,12},{4,8},{8,4},{12,0},{16,28},{20,24},{24,20},{28,16},{1,13},{... | collective-permute-start | bytes 497672 | tf_op jit(solution)/shard_map/ppermute | solution.py:461
  57.6 7.7 %collective-permute-start.16 = (bf16[144,288]{1,0:T(8,128)(2,1)S(1)}, bf16[144,288]{1,0:T(8,128)(2,1)S(1)}, u32[]{:S(2)}, u32[]{:S(2)}) collective-permute-start(bf16[144,288]{1,0:T(8,128)(2,1)S(1)} %get-tuple-element.62), channel_id=1, source_target_pairs={{0,16},{4,20},{8,24},{12,28},{16,0},{20,4},{24,8},{28,12},{1,17},{... | collective-permute-start | bytes 248840 | tf_op jit(solution)/shard_map/ppermute | solution.py:461
  61.2 9.7 %all-to-all-start = ((f32[32,1,128]{2,1,0:T(1,128)}), f32[32,1,128]{2,1,0:T(1,128)S(1)}, u32[]{:S(2)}, u32[]{:S(2)}) async-start(f32[32,1,128]{2,1,0:T(1,128)} %bitcast.5), calls=%async_computation | async-start | bytes 32768 | tf_op jit(solution)/shard_map/all_to_all | solution.py:542
  (1 other events, 5.2 us)

commit v6 on v5

--- a/solution.py
+++ b/solution.py
@@ -16,7 +16,6 @@
 QTOK = 32
 MP = 4
 DISTANCES = (4, 1, 2)
-ARRIVAL = (0, 4, 1, 5, 2, 6, 3, 7)
 SCALE = HEAD_DIM ** (-0.5)
 LOG2E = math.log2(math.e)
 F32 = jnp.float32
@@ -345,11 +344,11 @@
     similar = jnp.where(lines < counts_ref[mine], similar, -2.0)
     best = jnp.max(similar, axis=0, keepdims=True)
     if few:
-        size = best_ref.shape[1]
+        size = best_ref.shape[2]
         for piece in range(best.shape[1] // size):
-            row = best[:, piece * size : (piece + 1) * size]
-            for copy in range(MP):
-                best_ref[pl.ds((mine ^ ARRIVAL[piece]) * MP + copy, 1), :] = row
+            best_ref[piece // 2, piece % 2 : piece % 2 + 1, :] = best[
+                :, piece * size : (piece + 1) * size
+            ]
     else:
         best_ref[...] = best
 
@@ -360,7 +359,7 @@
     chunk = size if few else math.gcd(size, 1024)
     block = full(rows_dev, width)
     if few:
-        best_shape = shape((size // local * MP, local), F32)
+        best_shape = shape((size // local // 2, 2, local), F32)
         layout = dict(in_specs=[SMEM] + [VMEM] * 6, out_specs=(VMEM, VMEM))
     else:
         best_shape = shape((1, size), F32)
@@ -397,12 +396,18 @@
     if len(refs) == 1:
         refs[0][...] = out
         return
-    mine_ref, other_ref, found_ref, positive_ref, out_ref, weight_ref, score_ref, loss_ref = refs
+    mine_ref, other_ref, here_ref, one_ref, two_ref, three_ref, there_ref, positive_ref = refs[:8]
+    out_ref, weight_ref, score_ref, loss_ref, found_ref = refs[8:]
     out_ref[...] = out
     weight_ref[...] = mine_ref[...] + other_ref[...].astype(F32)
-    pages = found_ref.shape[0] // MP
-    best = jnp.max(found_ref[...].reshape(pages, MP, found_ref.shape[1]), axis=1)
-    turned = best.T
+    pages = found_ref.shape[0]
+    near = (here_ref, one_ref, two_ref, three_ref)
+    for index, ref in enumerate(near):
+        found_ref[index : index + 1, :] = ref[0, :1, :]
+    found_ref[len(near) :, :] = there_ref[...]
+    own = lax.axis_index("dp")
+    rows = [found_ref[pl.ds(page ^ own, 1), :] for page in range(pages)]
+    turned = jnp.concatenate(rows, axis=0).T
     columns = lax.broadcasted_iota(jnp.int32, (1, pages), 1)
     for query in range(score_ref.shape[0]):
         row = jnp.sum(turned[query * QTOK : (query + 1) * QTOK], axis=0, keepdims=True)
@@ -417,17 +422,21 @@
 
 def norm_back(patches, gain, grads, part, near, far, more=()):
     out_shape, out_specs, specs = [shape(patches.shape, BF16)], [VMEM], []
+    scratch = []
     if more:
-        mine, _, found, positive = more
-        scores = (positive.shape[0], found.shape[0] // MP)
-        specs = [VMEM, VMEM, VMEM, SMEM]
+        mine, positive, there = more[0], more[-1], more[-2]
+        pages = 2 * there.shape[0]
+        scores = (positive.shape[0], pages)
+        specs = [VMEM] * 7 + [SMEM]
         out_shape += [shape(mine.shape, F32), shape(scores, F32), shape(positive.shape, F32)]
         out_specs += [VMEM, VMEM, SMEM]
+        scratch = [pltpu.VMEM((pages, there.shape[1]), F32)]
     return pl.pallas_call(
         norm_back_kernel,
         out_shape=tuple(out_shape),
         in_specs=[VMEM] * 6 + specs,
         out_specs=tuple(out_specs),
+        scratch_shapes=scratch,
         cost_estimate=cost(3e6, 2e6),
         name="norm_back",
         compiler_params=grant(12),
@@ -533,14 +542,19 @@
     )
     if few:
         joined, best = lax.optimization_barrier((joined, best))
+        best = jnp.maximum(best, swap(best, "mp", 1))
+        best = jnp.maximum(best, swap(best, "mp", 2))
     grad_parts = input_branch(joined, mixing_pad)
-    part, received, far, sent = scatter_sum(grad_parts)
+    part, received, far, _ = scatter_sum(grad_parts)
     more = ()
     if few:
         mine, send = join_parts(kept, *got)
         other = swap(send, "dp", 4)
-        found = lax.all_to_all(after(best, sent), ("dp", "mp"), 0, 0, tiled=True)
-        more = (mine, other, found, positive_page)
+        best = after(best, send)
+        found = [best[:1]] + [swap(best[index : index + 1], "dp", index) for index in (1, 2, 3)]
+        going = jnp.concatenate([part[0, 1:] for part in found], axis=0)
+        there = swap(going, "dp", 4)
+        more = (mine, other, *found, there, positive_page)
     patch_grad, *rest = norm_back(patches, gain, hidden_grad, part, received, far, more)
     if few:
         return (hidden, patch_grad, *rest)

time: 72.9 us -> 65 us (0.89)
  waiting for transfers between devices: 29 us -> 19.6 us
  starting transfers between devices: 24.2 us -> 26.1 us
    all_to_all x1 -> x0, waiting for transfers between devices: 5.59 us -> none  [body(): found = lax.all_to_all(after(best, sent), ('dp', 'mp'), 0, 0, tiled=True)]
    ppermute x17 -> x23, starting transfers between devices: 21.7 us -> 26.1 us  [swap(): lax.ppermute(values, axis, [(index, index ^ distance) for index in range(...]
    ppermute x17 -> x23, waiting for transfers between devices: 23.4 us -> 19.6 us  [swap(): lax.ppermute(values, axis, [(index, index ^ distance) for index in range(...]
    all_to_all x1 -> x0, starting transfers between devices: 2.54 us -> none  [body(): found = lax.all_to_all(after(best, sent), ('dp', 'mp'), 0, 0, tiled=True)]
  transfers between devices with their start and end apart: 18 -> 23, of which waited for: 10 -> 10; matrix products, arithmetic and copies ran while one was open for 0% -> 0% of each run, Pallas kernels for 18% -> 25%
where the time goes in v6:
time: 65 us; the launch traced here: 64.9 us
  starting transfers between devices  26.1 us (40%)
  waiting for transfers between devices  19.6 us (30%)
  Pallas kernels  18.2 us (28%)
  between operations  0.78 us (1%)
    ppermute x23, starting transfers between devices, swap(): lax.ppermute(values, axis, [(index, index ^ distance) for index in range(...  26.1 us
    ppermute x23, waiting for transfers between devices, swap(): lax.ppermute(values, axis, [(index, index ^ distance) for index in range(...  19.6 us
    pallas_call x1, Pallas kernels, forward(): pl.pallas_call(partial(forward_kernel, heads, rows_dev), out_shape=(shape...  4.9 us
    pallas_call x1, Pallas kernels, backward(): pl.pallas_call(partial(backward_kernel, heads), out_shape=shape((rows, he...  4.35 us
    pallas_call x1, Pallas kernels, prepare(): pl.pallas_call(partial(prepare_kernel, heads), out_shape=(shape((heads *...  2.82 us
    pallas_call x1, Pallas kernels, norm_back(): pl.pallas_call(norm_back_kernel, out_shape=tuple(out_shape), in_specs=[VM...  1.83 us
    pallas_call x1, Pallas kernels, input_branch(): pl.pallas_call(branch_kernel, out_shape=handed_shapes(joined.shape[0] //...  1.53 us
    pallas_call x1, Pallas kernels, hidden_and_best(): pl.pallas_call(partial(score_kernel, rows_dev, few), **layout, out_shape=...  1.44 us
  transfers between devices with their start and end apart: 23, of which 10 were waited for; matrix products, arithmetic and copies ran while one was open for 0% of the time, Pallas kernels for 25%

profile of v6, /device:TPU:0, one launch (start us, length us, event | category | flops | bytes accessed | tf_op | source)
XLA Modules:
  0.0 64.9 jit_solution(8854384649814994334)
XLA Ops:
  1.2 2.6 %collective-permute-start.1 = (bf16[128,1152]{1,0:T(8,128)(2,1)}, bf16[128,1152]{1,0:T(8,128)(2,1)S(1)}, u32[]{:S(2)}, u32[]{:S(2)}) collective-permute-start(bf16[128,1152]{1,0:T(8,128)(2,1)} %patch_ref.3), channel_id=1, source_target_pairs={{0,2},{1,3},{2,0},{3,1},{4,6},{5,7},{6,4},{7,5},{8,10},{9,11},{10,... | collective-permute-start | bytes 884744 | tf_op jit(solution)/shard_map/ppermute | solution.py:470
  3.8 2.8 %prepare.1 = (bf16[1024,1152]{1,0:T(8,128)(2,1)S(1)}, bf16[512,1152]{1,0:T(8,128)(2,1)S(1)}, bf16[256,1024]{1,0:T(8,128)(2,1)S(1)}) custom-call(bf16[128,1152]{1,0:T(8,128)(2,1)} %patch_ref.3, f32[9,128]{1,0:T(8,128)} %bitcast.12, bf16[864,1152]{1,0:T(8,128)(2,1)} %bitcast.18, bf16[288,1152]{1,0:T(8,128)(2,1)} %bitcast.19, ...), custom_call_target="tpu_custom_call" | custom-call | flops 1000000000 | bytes 8000000 | tf_op jit(solution)/shard_map/prepare/pallas_call | solution.py:110
  6.6 5.0 %collective-permute-done.1.rows2 = bf16[128,1152]{1,0:T(8,128)(2,1)S(1)} collective-permute-done((bf16[128,1152]{1,0:T(8,128)(2,1)}, bf16[128,1152]{1,0:T(8,128)(2,1)S(1)}, u32[]{:S(2)}, u32[]{:S(2)}) %collective-permute-start.1) | collective-permute-done | bytes 294944 | tf_op jit(solution)/shard_map/ppermute | solution.py:470
  11.6 1.7 %collective-permute-start.8 = (bf16[128,1152]{1,0:T(8,128)(2,1)S(1)}, bf16[128,1152]{1,0:T(8,128)(2,1)S(1)}, u32[]{:S(2)}, u32[]{:S(2)}) collective-permute-start(bf16[128,1152]{1,0:T(8,128)(2,1)S(1)} %copy-done.2), channel_id=1, source_target_pairs={{0,2},{1,3},{2,0},{3,1},{4,6},{5,7},{6,4},{7,5},{8,10},{9,11},{10,... | collective-permute-start | bytes 884744 | tf_op jit(solution)/shard_map/ppermute | solution.py:470
  13.4 4.9 %forward_attention.1 = (bf16[512,1024]{1,0:T(8,128)(2,1)S(1)}, bf16[4,512,512]{2,1,0:T(8,128)(2,1)S(1)}, bf16[512,512]{1,0:T(8,128)(2,1)S(1)}, bf16[128,1152]{1,...) custom-call(s32[8]{0:T(128)S(1)} %copy-done.4, ...), custom_call_target="tpu_custom_call" | custom-call | flops 3000000000 | bytes 12000000 | tf_op jit(solution)/shard_map/forward_attention/pallas_call | solution.py:204
  18.6 2.6 %collective-permute-start.5 = (bf16[128,128]{1,0:T(8,128)(2,1)S(1)}, bf16[128,128]{1,0:T(8,128)(2,1)S(1)}, u32[]{:S(2)}, u32[]{:S(2)}) collective-permute-start(bf16[128,128]{1,0:T(8,128)(2,1)S(1)} %bitcast.15), channel_id=1, source_target_pairs={{0,16},{4,20},{8,24},{12,28},{16,0},{20,4},{24,8},{28,12},{1,17},{... | collective-permute-start | bytes 98312 | tf_op jit(solution)/shard_map/ppermute | solution.py:470
  21.7 1.7 %collective-permute-done.5 = bf16[128,128]{1,0:T(8,128)(2,1)S(1)} collective-permute-done((bf16[128,128]{1,0:T(8,128)(2,1)S(1)}, bf16[128,128]{1,0:T(8,128)(2,1)S(1)}, u32[]{:S(2)}, u32[]{:S(2)}) %collective-permute-start.5) | collective-permute-done | bytes 32800 | tf_op jit(solution)/shard_map/ppermute | solution.py:470
  23.4 1.5 %collective-permute-start.6 = (bf16[256,128]{1,0:T(8,128)(2,1)S(1)}, bf16[256,128]{1,0:T(8,128)(2,1)S(1)}, u32[]{:S(2)}, u32[]{:S(2)}) collective-permute-start(bf16[256,128]{1,0:T(8,128)(2,1)S(1)} %pad_maximum_fusion.2), channel_id=1, source_target_pairs={{0,4},{4,0},{8,12},{12,8},{16,20},{20,16},{24,28},{28,24},{1,5},{5... | collective-permute-start | bytes 196616 | tf_op jit(solution)/shard_map/ppermute | solution.py:470
  24.9 2.8 %collective-permute-done.6 = bf16[256,128]{1,0:T(8,128)(2,1)S(1)} collective-permute-done((bf16[256,128]{1,0:T(8,128)(2,1)S(1)}, bf16[256,128]{1,0:T(8,128)(2,1)S(1)}, u32[]{:S(2)}, u32[]{:S(2)}) %collective-permute-start.6) | collective-permute-done | bytes 65568 | tf_op jit(solution)/shard_map/ppermute | solution.py:470
  27.7 1.6 %collective-permute-start.10 = (bf16[512,128]{1,0:T(8,128)(2,1)S(1)}, bf16[512,128]{1,0:T(8,128)(2,1)S(1)}, u32[]{:S(2)}, u32[]{:S(2)}) collective-permute-start(bf16[512,128]{1,0:T(8,128)(2,1)S(1)} %pad_maximum_fusion.1), channel_id=1, source_target_pairs={{0,8},{4,12},{8,0},{12,4},{16,24},{20,28},{24,16},{28,20},{1,9},{5... | collective-permute-start | bytes 393224 | tf_op jit(solution)/shard_map/ppermute | solution.py:470
  29.3 1.2 %weight_parts.1 = (bf16[512,1152]{1,0:T(8,128)(2,1)S(1)}, f32[288,288]{1,0:T(8,128)S(1)}, bf16[288,288]{1,0:T(8,128)(2,1)S(1)}, bf16[288,288]{1,0:T(8,128)(2,1)S(1)}, bf16[288,288]{1,0:T(8,128)(2,1)S(1)}) custom-call(bf16[128,1152]{1,0:T(8,128)(2,1)S(1)} %copy-done.2, bf16[128,1152]{1,0:T(8,128)(2,1)S(1)} %collective-permute-done.7.grad1, ...), custom_call_target="tpu_custom_call" | custom-call | flops 700000000 | bytes 4000000 | tf_op jit(solution)/shard_map/weight_parts/pallas_call | solution.py:258
  30.5 1.6 %collective-permute-start.13 = (bf16[288,288]{1,0:T(8,128)(2,1)S(1)}, bf16[288,288]{1,0:T(8,128)(2,1)S(1)}, u32[]{:S(2)}, u32[]{:S(2)}) collective-permute-start(bf16[288,288]{1,0:T(8,128)(2,1)S(1)} %get-tuple-element.58), channel_id=1, source_target_pairs={{0,4},{4,0},{8,12},{12,8},{16,20},{20,16},{24,28},{28,24},{1,5},{5... | collective-permute-start | bytes 497672 | tf_op jit(solution)/shard_map/ppermute | solution.py:470
  32.5 1.5 %collective-permute-start.15 = (bf16[288,288]{1,0:T(8,128)(2,1)S(1)}, bf16[288,288]{1,0:T(8,128)(2,1)S(1)}, u32[]{:S(2)}, u32[]{:S(2)}) collective-permute-start(bf16[288,288]{1,0:T(8,128)(2,1)S(1)} %get-tuple-element.60), channel_id=1, source_target_pairs={{0,12},{4,8},{8,4},{12,0},{16,28},{20,24},{24,20},{28,16},{1,13},{... | collective-permute-start | bytes 497672 | tf_op jit(solution)/shard_map/ppermute | solution.py:470
  34.1 1.5 %collective-permute-start.4 = (bf16[128,1152]{1,0:T(8,128)(2,1)S(1)}, bf16[128,1152]{1,0:T(8,128)(2,1)S(1)}, u32[]{:S(2)}, u32[]{:S(2)}) collective-permute-start(bf16[128,1152]{1,0:T(8,128)(2,1)S(1)} %add_convert_fusion.1), channel_id=1, source_target_pairs={{0,2},{1,3},{2,0},{3,1},{4,6},{5,7},{6,4},{7,5},{8,10},{9,11},{10,... | collective-permute-start | bytes 884744 | tf_op jit(solution)/shard_map/ppermute | solution.py:470
  35.6 4.4 %backward_attention.1.joined_ref = bf16[512,1024]{1,0:T(8,128)(2,1)S(1)} custom-call(s32[8]{0:T(128)S(1)} %copy-done.4, bf16[512,1152]{1,0:T(8,128)(2,1)S(1)} %get-tuple-element.46.stacked_ref, bf16[512,1152]{1,0:T(8,128)(2,1)S(1)} %get-tuple-element.40.output_ref, bf16[512,1024]{1,0:T(8,128)(2,1)S(1)} %get-tuple-element.47.packed_ref, ...), custom_call_target="tpu_custom_call" | custom-call | flops 4000000000 | bytes 6000000 | tf_op jit(solution)/shard_map/backward_attention/pallas_call | solution.py:296
  40.9 1.4 %hidden_and_best.1 = (bf16[128,1152]{1,0:T(8,128)(2,1)}, f32[4,2,128]{2,1,0:T(2,128)S(1)}) custom-call(s32[8]{0:T(128)S(1)} %copy-done.4, bf16[128,1152]{1,0:T(8,128)(2,1)S(1)} %copy-done, bf16[128,1152]{1,0:T(8,128)(2,1)S(1)} %get-tuple-element.41.part_ref, bf16[256,1152]{1,0:T(8,128)(2,1)S(1)} %collective-permute-done.3.near_ref, ...), custom_call_target="tpu_custom_call" | custom-call | flops 100000000 | bytes 2000000 | tf_op jit(solution)/shard_map/hidden_and_best/pallas_call | solution.py:373
  43.1 2.8 %collective-permute-start.16 = (bf16[144,288]{1,0:T(8,128)(2,1)S(1)}, bf16[144,288]{1,0:T(8,128)(2,1)S(1)}, u32[]{:S(2)}, u32[]{:S(2)}) collective-permute-start(bf16[144,288]{1,0:T(8,128)(2,1)S(1)} %get-tuple-element.62), channel_id=1, source_target_pairs={{0,16},{4,20},{8,24},{12,28},{16,0},{20,4},{24,8},{28,12},{1,17},{... | collective-permute-start | bytes 248840 | tf_op jit(solution)/shard_map/ppermute | solution.py:470
  45.9 1.5 %collective-permute-start.18 = (f32[4,2,128]{2,1,0:T(2,128)S(1)}, f32[4,2,128]{2,1,0:T(2,128)S(1)}, u32[]{:S(2)}, u32[]{:S(2)}) collective-permute-start(f32[4,2,128]{2,1,0:T(2,128)S(1)} %max.6), channel_id=1, source_target_pairs={{0,2},{1,3},{2,0},{3,1},{4,6},{5,7},{6,4},{7,5},{8,10},{9,11},{10,... | collective-permute-start | bytes 12296 | tf_op jit(solution)/shard_map/ppermute | solution.py:470
  47.4 1.5 %input_branch.1 = (bf16[128,1152]{1,0:T(8,128)(2,1)S(1)}, bf16[128,1152]{1,0:T(8,128)(2,1)S(1)}, bf16[256,1152]{1,0:T(8,128)(2,1)S(1)}) custom-call(bf16[512,1024]{1,0:T(8,128)(2,1)S(1)} %backward_attention.1.joined_ref, bf16[1024,1152]{1,0:T(8,128)(2,1)S(1)} %get-tuple-element.39.mixing_ref), custom_call_target="tpu_custom_call" | custom-call | flops 2000000000 | bytes 8000000 | tf_op jit(solution)/shard_map/input_branch/pallas_call | solution.py:312
  49.6 1.9 %collective-permute-start.21 = (f32[1,2,128]{2,1,0:T(2,128)S(1)}, f32[1,2,128]{2,1,0:T(2,128)S(1)}, u32[]{:S(2)}, u32[]{:S(2)}) collective-permute-start(f32[1,2,128]{2,1,0:T(2,128)S(1)} %get-tuple-element.69), channel_id=1, source_target_pairs={{0,12},{4,8},{8,4},{12,0},{16,28},{20,24},{24,20},{28,16},{1,13},{... | collective-permute-start | bytes 3080 | tf_op jit(solution)/shard_map/ppermute | solution.py:470
  55.2 1.6 %collective-permute-start.12 = (bf16[128,1152]{1,0:T(8,128)(2,1)S(1)}, bf16[128,1152]{1,0:T(8,128)(2,1)S(1)}, u32[]{:S(2)}, u32[]{:S(2)}) collective-permute-start(bf16[128,1152]{1,0:T(8,128)(2,1)S(1)} %add_convert_fusion), channel_id=1, source_target_pairs={{0,2},{1,3},{2,0},{3,1},{4,6},{5,7},{6,4},{7,5},{8,10},{9,11},{10,... | collective-permute-start | bytes 884744 | tf_op jit(solution)/shard_map/ppermute | solution.py:470
  56.9 4.4 %collective-permute-done.22.refs_6_ = f32[4,128]{1,0:T(4,128)S(1)} collective-permute-done((f32[4,128]{1,0:T(4,128)S(1)}, f32[4,128]{1,0:T(4,128)S(1)}, u32[]{:S(2)}, u32[]{:S(2)}) %collective-permute-start.22) | collective-permute-done | bytes 2080 | tf_op jit(solution)/shard_map/ppermute | solution.py:470
  61.3 1.7 %collective-permute-done.12.far_ref = bf16[128,1152]{1,0:T(8,128)(2,1)S(1)} collective-permute-done((bf16[128,1152]{1,0:T(8,128)(2,1)S(1)}, bf16[128,1152]{1,0:T(8,128)(2,1)S(1)}, u32[]{:S(2)}, u32[]{:S(2)}) %collective-permute-start.12) | collective-permute-done | bytes 294944 | tf_op jit(solution)/shard_map/ppermute | solution.py:470
  63.0 1.8 %norm_back.1 = (bf16[128,1152]{1,0:T(8,128)(2,1)}, f32[144,288]{1,0:T(8,128)}, f32[4,8]{1,0:T(4,128)}, f32[4]{0:T(128)}) custom-call(bf16[128,1152]{1,0:T(8,128)(2,1)S(1)} %copy-done, f32[9,128]{1,0:T(8,128)S(1)} %bitcast.14, bf16[128,1152]{1,0:T(8,128)(2,1)S(1)} %copy-done.2, bf16[128,1152]{1,0:T(8,128)(2,1)S(1)} %get-tuple-element.54.part_ref, ...), custom_call_target="tpu_custom_call" | custom-call | flops 3000000 | bytes 2000000 | tf_op jit(solution)/shard_map/norm_back/pallas_call | solution.py:434
  (57 shorter events, 8.0 us)
Async XLA Ops:
  0.7 3.1 %collective-permute-start = (bf16[128,1152]{1,0:T(8,128)(2,1)}, bf16[128,1152]{1,0:T(8,128)(2,1)S(1)}, u32[]{:S(2)}, u32[]{:S(2)}) collective-permute-start(bf16[128,1152]{1,0:T(8,128)(2,1)} %patch_ref.3), channel_id=1, source_target_pairs={{0,1},{1,0},{2,3},{3,2},{4,5},{5,4},{6,7},{7,6},{8,9},{9,8},{10,11... | collective-permute-start | bytes 884744 | tf_op jit(solution)/shard_map/ppermute | solution.py:470
  1.2 10.4 %collective-permute-start.1 = (bf16[128,1152]{1,0:T(8,128)(2,1)}, bf16[128,1152]{1,0:T(8,128)(2,1)S(1)}, u32[]{:S(2)}, u32[]{:S(2)}) collective-permute-start(bf16[128,1152]{1,0:T(8,128)(2,1)} %patch_ref.3), channel_id=1, source_target_pairs={{0,2},{1,3},{2,0},{3,1},{4,6},{5,7},{6,4},{7,5},{8,10},{9,11},{10,... | collective-permute-start | bytes 884744 | tf_op jit(solution)/shard_map/ppermute | solution.py:470
  11.6 1.8 %collective-permute-start.2 = (bf16[128,1152]{1,0:T(8,128)(2,1)S(1)}, bf16[128,1152]{1,0:T(8,128)(2,1)S(1)}, u32[]{:S(2)}, u32[]{:S(2)}) collective-permute-start(bf16[128,1152]{1,0:T(8,128)(2,1)S(1)} %collective-permute-done.1.rows2), channel_id=1, source_target_pairs={{0,1},{1,0},{2,3},{3,2},{4,5},{5,4},{6,7},{7,6},{8,9},{9,8},{10,11... | collective-permute-start | bytes 884744 | tf_op jit(solution)/shard_map/ppermute | solution.py:470
  11.6 9.6 %collective-permute-start.8 = (bf16[128,1152]{1,0:T(8,128)(2,1)S(1)}, bf16[128,1152]{1,0:T(8,128)(2,1)S(1)}, u32[]{:S(2)}, u32[]{:S(2)}) collective-permute-start(bf16[128,1152]{1,0:T(8,128)(2,1)S(1)} %copy-done.2), channel_id=1, source_target_pairs={{0,2},{1,3},{2,0},{3,1},{4,6},{5,7},{6,4},{7,5},{8,10},{9,11},{10,... | collective-permute-start | bytes 884744 | tf_op jit(solution)/shard_map/ppermute | solution.py:470
  18.3 15.8 %collective-permute-start.3 = (bf16[256,1152]{1,0:T(8,128)(2,1)S(1)}, bf16[256,1152]{1,0:T(8,128)(2,1)S(1)}, u32[]{:S(2)}, u32[]{:S(2)}) collective-permute-start(bf16[256,1152]{1,0:T(8,128)(2,1)S(1)} %get-tuple-element.42), channel_id=1, source_target_pairs={{0,1},{1,0},{2,3},{3,2},{4,5},{5,4},{6,7},{7,6},{8,9},{9,8},{10,11... | collective-permute-start | bytes 1769480 | tf_op jit(solution)/shard_map/ppermute | solution.py:470
  18.6 4.8 %collective-permute-start.5 = (bf16[128,128]{1,0:T(8,128)(2,1)S(1)}, bf16[128,128]{1,0:T(8,128)(2,1)S(1)}, u32[]{:S(2)}, u32[]{:S(2)}) collective-permute-start(bf16[128,128]{1,0:T(8,128)(2,1)S(1)} %bitcast.15), channel_id=1, source_target_pairs={{0,16},{4,20},{8,24},{12,28},{16,0},{20,4},{24,8},{28,12},{1,17},{... | collective-permute-start | bytes 98312 | tf_op jit(solution)/shard_map/ppermute | solution.py:470
  21.2 8.2 %collective-permute-start.7 = (bf16[128,1152]{1,0:T(8,128)(2,1)S(1)}, bf16[128,1152]{1,0:T(8,128)(2,1)S(1)}, u32[]{:S(2)}, u32[]{:S(2)}) collective-permute-start(bf16[128,1152]{1,0:T(8,128)(2,1)S(1)} %copy-done.2), channel_id=1, source_target_pairs={{0,1},{1,0},{2,3},{3,2},{4,5},{5,4},{6,7},{7,6},{8,9},{9,8},{10,11... | collective-permute-start | bytes 884744 | tf_op jit(solution)/shard_map/ppermute | solution.py:470
  21.2 8.1 %collective-permute-start.9 = (bf16[128,1152]{1,0:T(8,128)(2,1)S(1)}, bf16[128,1152]{1,0:T(8,128)(2,1)S(1)}, u32[]{:S(2)}, u32[]{:S(2)}) collective-permute-start(bf16[128,1152]{1,0:T(8,128)(2,1)S(1)} %collective-permute-done.8.grad2), channel_id=1, source_target_pairs={{0,1},{1,0},{2,3},{3,2},{4,5},{5,4},{6,7},{7,6},{8,9},{9,8},{10,11... | collective-permute-start | bytes 884744 | tf_op jit(solution)/shard_map/ppermute | solution.py:470
  23.4 4.3 %collective-permute-start.6 = (bf16[256,128]{1,0:T(8,128)(2,1)S(1)}, bf16[256,128]{1,0:T(8,128)(2,1)S(1)}, u32[]{:S(2)}, u32[]{:S(2)}) collective-permute-start(bf16[256,128]{1,0:T(8,128)(2,1)S(1)} %pad_maximum_fusion.2), channel_id=1, source_target_pairs={{0,4},{4,0},{8,12},{12,8},{16,20},{20,16},{24,28},{28,24},{1,5},{5... | collective-permute-start | bytes 196616 | tf_op jit(solution)/shard_map/ppermute | solution.py:470
  27.7 12.4 %collective-permute-start.10 = (bf16[512,128]{1,0:T(8,128)(2,1)S(1)}, bf16[512,128]{1,0:T(8,128)(2,1)S(1)}, u32[]{:S(2)}, u32[]{:S(2)}) collective-permute-start(bf16[512,128]{1,0:T(8,128)(2,1)S(1)} %pad_maximum_fusion.1), channel_id=1, source_target_pairs={{0,8},{4,12},{8,0},{12,4},{16,24},{20,28},{24,16},{28,20},{1,9},{5... | collective-permute-start | bytes 393224 | tf_op jit(solution)/shard_map/ppermute | solution.py:470
  30.5 11.9 %collective-permute-start.13 = (bf16[288,288]{1,0:T(8,128)(2,1)S(1)}, bf16[288,288]{1,0:T(8,128)(2,1)S(1)}, u32[]{:S(2)}, u32[]{:S(2)}) collective-permute-start(bf16[288,288]{1,0:T(8,128)(2,1)S(1)} %get-tuple-element.58), channel_id=1, source_target_pairs={{0,4},{4,0},{8,12},{12,8},{16,20},{20,16},{24,28},{28,24},{1,5},{5... | collective-permute-start | bytes 497672 | tf_op jit(solution)/shard_map/ppermute | solution.py:470
  32.1 10.3 %collective-permute-start.14 = (bf16[288,288]{1,0:T(8,128)(2,1)S(1)}, bf16[288,288]{1,0:T(8,128)(2,1)S(1)}, u32[]{:S(2)}, u32[]{:S(2)}) collective-permute-start(bf16[288,288]{1,0:T(8,128)(2,1)S(1)} %get-tuple-element.59), channel_id=1, source_target_pairs={{0,8},{4,12},{8,0},{12,4},{16,24},{20,28},{24,16},{28,20},{1,9},{5... | collective-permute-start | bytes 497672 | tf_op jit(solution)/shard_map/ppermute | solution.py:470
  32.5 10.5 %collective-permute-start.15 = (bf16[288,288]{1,0:T(8,128)(2,1)S(1)}, bf16[288,288]{1,0:T(8,128)(2,1)S(1)}, u32[]{:S(2)}, u32[]{:S(2)}) collective-permute-start(bf16[288,288]{1,0:T(8,128)(2,1)S(1)} %get-tuple-element.60), channel_id=1, source_target_pairs={{0,12},{4,8},{8,4},{12,0},{16,28},{20,24},{24,20},{28,16},{1,13},{... | collective-permute-start | bytes 497672 | tf_op jit(solution)/shard_map/ppermute | solution.py:470
  34.1 6.8 %collective-permute-start.4 = (bf16[128,1152]{1,0:T(8,128)(2,1)S(1)}, bf16[128,1152]{1,0:T(8,128)(2,1)S(1)}, u32[]{:S(2)}, u32[]{:S(2)}) collective-permute-start(bf16[128,1152]{1,0:T(8,128)(2,1)S(1)} %add_convert_fusion.1), channel_id=1, source_target_pairs={{0,2},{1,3},{2,0},{3,1},{4,6},{5,7},{6,4},{7,5},{8,10},{9,11},{10,... | collective-permute-start | bytes 884744 | tf_op jit(solution)/shard_map/ppermute | solution.py:470
  42.4 3.6 %collective-permute-start.17 = (f32[4,2,128]{2,1,0:T(2,128)S(1)}, f32[4,2,128]{2,1,0:T(2,128)S(1)}, u32[]{:S(2)}, u32[]{:S(2)}) collective-permute-start(f32[4,2,128]{2,1,0:T(2,128)S(1)} %get-tuple-element.63), channel_id=1, source_target_pairs={{0,1},{1,0},{2,3},{3,2},{4,5},{5,4},{6,7},{7,6},{8,9},{9,8},{10,11... | collective-permute-start | bytes 12296 | tf_op jit(solution)/shard_map/ppermute | solution.py:470
  43.1 13.8 %collective-permute-start.16 = (bf16[144,288]{1,0:T(8,128)(2,1)S(1)}, bf16[144,288]{1,0:T(8,128)(2,1)S(1)}, u32[]{:S(2)}, u32[]{:S(2)}) collective-permute-start(bf16[144,288]{1,0:T(8,128)(2,1)S(1)} %get-tuple-element.62), channel_id=1, source_target_pairs={{0,16},{4,20},{8,24},{12,28},{16,0},{20,4},{24,8},{28,12},{1,17},{... | collective-permute-start | bytes 248840 | tf_op jit(solution)/shard_map/ppermute | solution.py:470
  45.9 17.1 %copy-start.5 = (s32[4]{0:T(128)S(1)}, s32[4]{0:T(128)}, u32[]{:S(2)}) copy-start(s32[4]{0:T(128)} %refs_7_.1) | copy-start | bytes 52
  45.9 3.7 %collective-permute-start.18 = (f32[4,2,128]{2,1,0:T(2,128)S(1)}, f32[4,2,128]{2,1,0:T(2,128)S(1)}, u32[]{:S(2)}, u32[]{:S(2)}) collective-permute-start(f32[4,2,128]{2,1,0:T(2,128)S(1)} %max.6), channel_id=1, source_target_pairs={{0,2},{1,3},{2,0},{3,1},{4,6},{5,7},{6,4},{7,5},{8,10},{9,11},{10,... | collective-permute-start | bytes 12296 | tf_op jit(solution)/shard_map/ppermute | solution.py:470
  49.0 6.1 %collective-permute-start.11 = (bf16[256,1152]{1,0:T(8,128)(2,1)S(1)}, bf16[256,1152]{1,0:T(8,128)(2,1)S(1)}, u32[]{:S(2)}, u32[]{:S(2)}) collective-permute-start(bf16[256,1152]{1,0:T(8,128)(2,1)S(1)} %get-tuple-element.55), channel_id=1, source_target_pairs={{0,1},{1,0},{2,3},{3,2},{4,5},{5,4},{6,7},{7,6},{8,9},{9,8},{10,11... | collective-permute-start | bytes 1769480 | tf_op jit(solution)/shard_map/ppermute | solution.py:470
  49.6 4.5 %collective-permute-start.21 = (f32[1,2,128]{2,1,0:T(2,128)S(1)}, f32[1,2,128]{2,1,0:T(2,128)S(1)}, u32[]{:S(2)}, u32[]{:S(2)}) collective-permute-start(f32[1,2,128]{2,1,0:T(2,128)S(1)} %get-tuple-element.69), channel_id=1, source_target_pairs={{0,12},{4,8},{8,4},{12,0},{16,28},{20,24},{24,20},{28,16},{1,13},{... | collective-permute-start | bytes 3080 | tf_op jit(solution)/shard_map/ppermute | solution.py:470
  51.5 3.6 %collective-permute-start.20 = (f32[1,2,128]{2,1,0:T(2,128)S(1)}, f32[1,2,128]{2,1,0:T(2,128)S(1)}, u32[]{:S(2)}, u32[]{:S(2)}) collective-permute-start(f32[1,2,128]{2,1,0:T(2,128)S(1)} %get-tuple-element.70), channel_id=1, source_target_pairs={{0,8},{4,12},{8,0},{12,4},{16,24},{20,28},{24,16},{28,20},{1,9},{5... | collective-permute-start | bytes 3080 | tf_op jit(solution)/shard_map/ppermute | solution.py:470
  52.2 4.5 %collective-permute-start.19 = (f32[1,2,128]{2,1,0:T(2,128)S(1)}, f32[1,2,128]{2,1,0:T(2,128)S(1)}, u32[]{:S(2)}, u32[]{:S(2)}) collective-permute-start(f32[1,2,128]{2,1,0:T(2,128)S(1)} %get-tuple-element.71), channel_id=1, source_target_pairs={{0,4},{4,0},{8,12},{12,8},{16,20},{20,16},{24,28},{28,24},{1,5},{5... | collective-permute-start | bytes 3080 | tf_op jit(solution)/shard_map/ppermute | solution.py:470
  55.2 7.9 %collective-permute-start.12 = (bf16[128,1152]{1,0:T(8,128)(2,1)S(1)}, bf16[128,1152]{1,0:T(8,128)(2,1)S(1)}, u32[]{:S(2)}, u32[]{:S(2)}) collective-permute-start(bf16[128,1152]{1,0:T(8,128)(2,1)S(1)} %add_convert_fusion), channel_id=1, source_target_pairs={{0,2},{1,3},{2,0},{3,1},{4,6},{5,7},{6,4},{7,5},{8,10},{9,11},{10,... | collective-permute-start | bytes 884744 | tf_op jit(solution)/shard_map/ppermute | solution.py:470
  56.8 4.5 %collective-permute-start.22 = (f32[4,128]{1,0:T(4,128)S(1)}, f32[4,128]{1,0:T(4,128)S(1)}, u32[]{:S(2)}, u32[]{:S(2)}) collective-permute-start(f32[4,128]{1,0:T(4,128)S(1)} %pad_maximum_fusion.3), channel_id=1, source_target_pairs={{0,16},{4,20},{8,24},{12,28},{16,0},{20,4},{24,8},{28,12},{1,17},{... | collective-permute-start | bytes 6152 | tf_op jit(solution)/shard_map/ppermute | solution.py:470
  (6 other events, 52.1 us)
